TPU v7x, 128 devices: a whole 4x4x4 slice. The times are simulated.
128 devices in a mesh: ctx: 64 (over z, y, x_hi, core), chan: 2 (over x_lo).
Axes of the slice: x: 4 (x_hi: 2, x_lo: 2; x = x_hi * 2 + x_lo), y: 4, z: 4, core: 2. Of those that a mesh axis runs over, the one named last changes fastest.
Arguments:
- hidden: bfloat16 [16384, 2048], P('ctx'), may hold values from -6 to 6
- in_weight: bfloat16 [2048, 4096], P(None, 'chan'), may hold values from -0.125 to 0.125
- state_proj: bfloat16 [2, 16384, 128], P(None, 'ctx'), may hold values from -2.09375 to 2.09375
- log_decay: float32 [2, 16384, 64], P(None, 'ctx', 'chan'), may hold values from -1.6 to 0, as said below
- step_size: float32 [2, 16384, 64], P(None, 'ctx', 'chan'), may hold values from 0 to 1, as said below
- skip_gain: float32 [64], P('chan'), may hold values from 0.1 to 1.9
- cotangent: bfloat16 [16384, 4096], P('ctx', 'chan'), may hold values from -6 to 6
Outputs:
- layer_out: bfloat16 [16384, 4096], P('ctx', 'chan')
- input_grad: bfloat16 [16384, 2048], P('ctx', 'chan')
Inputs may be any that keep to these rules, and one draw needn't show every extreme that they name: log_decay is never positive. step_size is positive.
All inputs are finite; a program needn't handle non-finite values.
Results may differ from a plain program's by a relative error of at most 0.014.
Values may be sent and summed in bfloat16 or wider, within the bound.
No kernel may reach another device: no remote copies, remote signals or barrier semaphores. Data moves between devices by JAX's collectives and lax.ppermute only.
A program may use at most 640 MiB of HBM per device.

v0:
```python
import jax
import jax.numpy as jnp
from jax import lax
from jax.sharding import PartitionSpec as P

HEAD_DIM = 64
GROUP = 128


def partner(block, axis, apart):
    count = lax.axis_size(axis)
    route = []
    for low in range(count):
        high = low | 1 << apart
        if high != low and high < count:
            route += [(low, high), (high, low)]
    return lax.ppermute(block, axis, route)


def carried_in(x, axis, combine, identity, reverse):
    devices, position = (lax.axis_size(axis), lax.axis_index(axis))
    everything = jax.tree.map(
        lambda part, kind: lax.all_gather(part.astype(kind), axis),
        x,
        jax.tree.map(lambda a: jnp.bfloat16 if a.dtype == jnp.float32 else a.dtype, x),
    )
    start = jax.tree.map(
        lambda part, zero: jnp.broadcast_to(jnp.asarray(zero, part.dtype), part.shape), x, identity
    )

    def step(k, before):
        at = devices - 1 - k if reverse else k
        reached = at > position if reverse else at < position
        new = combine(
            before, jax.tree.map(lambda part, own: part[at].astype(own.dtype), everything, x)
        )
        return jax.tree.map(lambda a, b: jnp.where(reached, a, b), new, before)

    return lax.fori_loop(0, devices, step, start)


def reverse_rows(array):
    return jnp.flip(array, 0)


def local_blocks(query_rows, key_rows, value_rows, weights, decay_values, exclusive):
    length = query_rows.shape[0]
    blocks = length // GROUP
    head_count = value_rows.shape[1]
    head_width = value_rows.shape[2]
    state_width = query_rows.shape[1]

    def advance(carry_pair, members):
        states, offset = carry_pair
        query_blk, key_blk, value_blk, weight_blk, decay_blk = members
        cumul = jnp.cumsum(decay_blk, axis=0)
        if exclusive:
            level = cumul - decay_blk
        else:
            level = cumul
        affinity = jnp.dot(query_blk, key_blk.T, preferred_element_type=jnp.float32)
        row_index = lax.broadcasted_iota(jnp.int32, (GROUP, GROUP), 0)
        col_index = lax.broadcasted_iota(jnp.int32, (GROUP, GROUP), 1)
        level_heads = level.T
        mixing = (
            affinity[None]
            * jnp.exp(
                jnp.where(
                    (row_index >= col_index)[None],
                    level_heads[:, :, None] - level_heads[:, None, :],
                    -jnp.inf,
                )
            )
            * weight_blk.T[:, None, :]
        ).astype(jnp.bfloat16)
        within = jnp.einsum("hts,shp->thp", mixing, value_blk, preferred_element_type=jnp.float32)
        closing = cumul[-1]
        fading = jnp.exp(closing[None, :] - level) * weight_blk
        weighted = (fading[:, :, None] * key_blk.astype(jnp.float32)[:, None, :]).astype(
            jnp.bfloat16
        )
        new_states = jnp.exp(closing)[:, None, None] * states + jnp.einsum(
            "shn,shp->hpn", weighted, value_blk, preferred_element_type=jnp.float32
        )
        return ((new_states, offset + closing), (within, level, states, offset))

    members = tuple(
        (
            member.reshape((blocks, GROUP) + member.shape[1:])
            for member in (query_rows, key_rows, value_rows, weights, decay_values)
        )
    )
    initial = (
        jnp.zeros((head_count, head_width, state_width), jnp.float32),
        jnp.zeros((head_count,), jnp.float32),
    )
    (states, log_total), (within, levels, before, offsets) = lax.scan(advance, initial, members)
    return (within, levels, log_total, states, before, offsets)


def finish(parts, query_rows, carry_in):
    within, levels, before, offsets = (parts[0], parts[1], parts[4], parts[5])
    blocks = within.shape[0]
    full = before + jnp.exp(offsets)[:, :, None, None] * carry_in[1][None]
    query_blocks = query_rows.reshape((blocks, GROUP) + query_rows.shape[1:])
    incoming = jnp.einsum(
        "btn,bhpn->bthp",
        query_blocks,
        full.astype(jnp.bfloat16),
        preferred_element_type=jnp.float32,
    )
    total = within + jnp.exp(levels)[:, :, :, None] * incoming
    return total.reshape((blocks * GROUP,) + total.shape[2:])


def link_one(earlier, latter):
    return (earlier[0] + latter[0], jnp.exp(latter[0])[:, None, None] * earlier[1] + latter[1])


def link_both(earlier, latter):
    return (link_one(earlier[0], latter[0]), link_one(earlier[1], latter[1]))


def shards(hidden, in_weight, state_proj, log_decay, step_size, skip_gain, cotangent):
    rows_here = hidden.shape[0]
    head_count = skip_gain.shape[0]
    local_inner = in_weight.shape[1]
    half_state = state_proj.shape[2] // 2
    keys_f = state_proj[0, :, :half_state]
    query_f = state_proj[0, :, half_state:]
    keys_r = state_proj[1, :, :half_state]
    query_r = state_proj[1, :, half_state:]
    flipped = hidden[:, ::-1]
    other_weight, other_decay, other_step, other_skip = (
        partner(in_weight, "chan", 0),
        partner(log_decay[1].astype(jnp.bfloat16), "chan", 0).astype(jnp.float32),
        partner(step_size[1].astype(jnp.bfloat16), "chan", 0).astype(jnp.float32),
        partner(skip_gain.astype(jnp.bfloat16), "chan", 0).astype(skip_gain.dtype),
    )
    rc_weight = other_weight.reshape(-1, head_count, HEAD_DIM)[:, ::-1, :].reshape(-1, local_inner)
    rc_decay = other_decay[:, ::-1]
    rc_step = other_step[:, ::-1]
    rc_skip = other_skip[::-1]
    rc_cotangent = cotangent.reshape(rows_here, head_count, HEAD_DIM)[:, :, ::-1]
    fwd_inner = jnp.dot(hidden, in_weight, preferred_element_type=jnp.float32).astype(jnp.bfloat16)
    rc_inner = jnp.dot(flipped, rc_weight, preferred_element_type=jnp.float32).astype(jnp.bfloat16)
    fwd_values = fwd_inner.reshape(rows_here, head_count, HEAD_DIM)
    rc_values = rc_inner.reshape(rows_here, head_count, HEAD_DIM)
    cot_values = cotangent.reshape(rows_here, head_count, HEAD_DIM)
    unit = jnp.ones_like(step_size[0])
    query_r_back = reverse_rows(query_r)
    keys_f_back = reverse_rows(keys_f)
    part_ff = local_blocks(query_f, keys_f, fwd_values, step_size[0], log_decay[0], False)
    part_rb = local_blocks(keys_r, query_r, rc_cotangent, unit, rc_decay, True)
    part_rf = local_blocks(
        query_r_back,
        reverse_rows(keys_r),
        reverse_rows(rc_values),
        reverse_rows(rc_step),
        reverse_rows(rc_decay),
        False,
    )
    part_fb = local_blocks(
        keys_f_back,
        reverse_rows(query_f),
        reverse_rows(cot_values),
        unit,
        reverse_rows(log_decay[0]),
        True,
    )
    zero_pair = (
        jnp.zeros((head_count,), jnp.float32),
        jnp.zeros((head_count, HEAD_DIM, half_state), jnp.float32),
    )
    carry_ff, carry_rb = carried_in(
        ((part_ff[2], part_ff[3]), (part_rb[2], part_rb[3])),
        "ctx",
        link_both,
        (zero_pair, zero_pair),
        False,
    )
    carry_rf, carry_fb = carried_in(
        ((part_rf[2], part_rf[3]), (part_fb[2], part_fb[3])),
        "ctx",
        link_both,
        (zero_pair, zero_pair),
        True,
    )
    scan_ff = finish(part_ff, query_f, carry_ff)
    scan_rb = finish(part_rb, keys_r, carry_rb)
    scan_rf = reverse_rows(finish(part_rf, query_r_back, carry_rf))
    scan_fb = reverse_rows(finish(part_fb, keys_f_back, carry_fb))
    gains = skip_gain[None, :, None]
    rc_gains = rc_skip[None, :, None]
    fwd_out = scan_ff + gains * fwd_values.astype(jnp.float32)
    rc_out = (scan_rf + rc_gains * rc_values.astype(jnp.float32)).astype(jnp.bfloat16)
    rc_part = rc_out[:, :, ::-1].reshape(rows_here, local_inner)
    layer_out = (fwd_out.reshape(rows_here, local_inner) + rc_part.astype(jnp.float32)).astype(
        jnp.bfloat16
    )
    grad_f = (step_size[0][:, :, None] * scan_fb + gains * cot_values.astype(jnp.float32)).astype(
        jnp.bfloat16
    )
    grad_r = (rc_step[:, :, None] * scan_rb + rc_gains * rc_cotangent.astype(jnp.float32)).astype(
        jnp.bfloat16
    )
    direct = jnp.dot(
        grad_f.reshape(rows_here, local_inner), in_weight.T, preferred_element_type=jnp.float32
    )
    mirrored = jnp.dot(
        grad_r.reshape(rows_here, local_inner), rc_weight.T, preferred_element_type=jnp.float32
    )
    grad_terms = direct + mirrored[:, ::-1]
    input_grad = lax.psum_scatter(
        grad_terms.astype(jnp.bfloat16), "chan", scatter_dimension=1, tiled=True
    )
    return (layer_out, input_grad)


def solution(mesh):
    in_specs = (
        P("ctx", None),
        P(None, "chan"),
        P(None, "ctx", None),
        P(None, "ctx", "chan"),
        P(None, "ctx", "chan"),
        P("chan"),
        P("ctx", "chan"),
    )
    out_specs = (P("ctx", "chan"), P("ctx", "chan"))
    return jax.shard_map(shards, mesh=mesh, in_specs=in_specs, out_specs=out_specs, check_vma=False)
```

profile of v0, /device:TPU:1, one launch (start us, length us, event | category | flops | bytes accessed | tf_op | source)
XLA Modules:
  0.0 1158.6 jit_solution(4280243458082191520)
XLA Ops:
  9.0 6.1 convolution_convert_fusion.1
  27.3 8.3 while.118
  47.3 11.0 while.119
  64.3 8.1 while.122
  73.4 11.8 %copy.132 = bf16[2048,2048]{0,1:T(8,128)(2,1)} copy(bf16[2048,2048]{1,0:T(8,128)(2,1)} %param.20) | data formatting | bytes 16777216 | tf_op args[1]
  89.9 11.3 rev.64
  111.2 238.1 %collective-permute-done.3 = bf16[32]{0:T(256)(128)(2,1)} collective-permute-done((bf16[32]{0:T(256)(128)(2,1)}, bf16[32]{0:T(256)(128)(2,1)}, u32[]{:S(2)}, u32[]{:S(2)}) %collective-permute-start.3) | collective-permute-done | bytes 96 | tf_op jit(solution)/shard_map/ppermute | solution.py:17
  357.4 8.5 rev.65
  365.8 7.1 convolution_convert_fusion
  375.2 3.6 rev.66
  385.6 15.7 %while.121 = (s32[]{:T(128)}, f32[32,64,64]{2,1,0:T(8,128)S(1)}, f32[32]{0:T(128)S(1)}, f32[2,128,32,64]{1,3,2,0:T(8,128)}, f32[2,128,32]{2,1,0:T(8,128)}, /*ind...) while((s32[]{:T(128)}, f32[32,64,64]{2,1,0:T(8,128)S(1)}, ...), condition=%wide.region_10.11_spmd.clone, body=%wide.region_8.10_spmd.clone.sunk | while | flops 106983488 | bytes 10263585 | solution.py:97
  401.7 325.5 %all-reduce.4 = (bf16[2048]{0:T(1024)(128)(2,1)S(1)}, bf16[2048]{0:T(1024)(128)(2,1)S(1)}, bf16[2048]{0:T(1024)(128)(2,1)S(1)}, bf16[2048]{0:T(1024)(128)(2,1)S(1)}) all-reduce(bf16[2048]{0:T(1024)(128)(2,1)S(1)} %dynamic-update-slice.2, bf16[2048]{0:T(1024)(128)(2,1)S(1)} %copy-done.39, ...), channel_id=6, replica_groups=mesh['ctx'=64,'chan'=2] {'ctx'}, use_global_device_ids=true, to_apply=%add.2 | all-reduce | flops 8192 | bytes 32768
  729.7 235.0 %while.120 = (s32[]{:T(128)}, f32[32,64,64]{2,1,0:T(8,128)}, f32[32,64,64]{2,1,0:T(8,128)}, s32[]{:T(128)}, bf16[64,32]{1,0:T(8,128)(2,1)S(1)}, /*index=5*/bf16[...) while((s32[]{:T(128)}, f32[32,64,64]{2,1,0:T(8,128)}, ...), condition=%wide.region_7.8_spmd.clone, body=%wide.region_6.7_spmd.clone.sunk | while | flops 1310788 | bytes 2622213 | solution.py:39
  732.8 3.6 fusion.208
  740.1 3.8 fusion.208
  743.9 3.6 fusion.208
  747.6 3.6 fusion.208
  751.2 3.6 fusion.208
  765.8 3.6 fusion.208
  769.5 3.6 fusion.208
  773.1 3.6 fusion.208
  776.8 3.6 fusion.208
  780.4 3.6 fusion.208
  784.1 3.7 fusion.208
  798.7 3.7 fusion.208
  802.4 4.5 fusion.208
  821.5 3.6 fusion.208
  825.2 3.6 fusion.208
  828.8 3.6 fusion.208
  832.5 3.6 fusion.208
  836.1 3.7 fusion.208
  843.5 3.6 fusion.208
  847.1 3.6 fusion.208
  850.8 3.7 fusion.208
  854.5 3.6 fusion.208
  858.2 3.6 fusion.208
  861.8 3.6 fusion.208
  865.4 4.5 fusion.208
  873.7 3.6 fusion.208
  967.9 7.2 convolution_bitcast_fusion.4
  975.1 17.6 %rev.79 = f32[256,2048]{1,0:T(8,128)} reverse(f32[256,2048]{1,0:T(8,128)} %convolution_bitcast_fusion.4), dimensions={1} | reverse | bytes 4194304 | tf_op jit(solution)/shard_map/rev | solution.py:213
  992.7 106.9 %while.123 = (s32[]{:T(128)}, f32[32,64,64]{2,1,0:T(8,128)S(1)}, f32[32,64,64]{2,1,0:T(8,128)S(1)}, s32[]{:T(128)}, bf16[64,32]{1,0:T(8,128)(2,1)S(1)}, /*index=...) while((s32[]{:T(128)}, f32[32,64,64]{2,1,0:T(8,128)S(1)}, ...), condition=%wide.region_15.16_spmd.clone, body=%wide.region_14.15_spmd.clone.sunk | while | flops 1310792 | bytes 2622275 | solution.py:39
  1104.0 4.3 rev.77
  1110.2 5.9 fusion.140
  1117.5 4.0 fusion.124
  1121.5 5.6 copy.167
  1127.1 3.7 reshape.382
  1135.0 4.3 rev.74
  (752 shorter events, 378.4 us)
Async XLA Ops:
  7.2 722.5 %all-gather.13.cloned.1.call-start = ((), (), s32[]{:S(2)}) async-start(), calls=%async_computation.2 | async-start | bytes 34078720 | tf_op jit(solution)/shard_map/all_gather | solution.py:23
  19.2 3.3 copy-start.33
  19.2 4.1 copy-start.34
  35.6 3.7 copy-start.18
  35.6 3.7 copy-start.42
  36.5 693.1 %all-gather.15.cloned.1.call-start = ((), (), s32[]{:S(2)}) async-start(), calls=%async_computation.3 | async-start | bytes 34078720 | tf_op jit(solution)/shard_map/all_gather | solution.py:23
  36.6 5.4 collective-permute-start
  39.3 19.9 %copy-start.1 = (bf16[256,2048]{0,1:T(8,128)(2,1)}, bf16[256,2048]{0,1:T(8,128)(2,1)S(1)}, u32[]{:S(2)}) copy-start(bf16[256,2048]{0,1:T(8,128)(2,1)S(1)} %copy.122) | copy-start | bytes 3145732
  48.5 3.2 copy-start.15
  53.9 3.2 copy-start.15
  59.2 933.6 %all-gather.19.cloned.1.call-start = ((), (), s32[]{:S(2)}) async-start(), calls=%async_computation.5 | async-start | bytes 34078720 | tf_op jit(solution)/shard_map/all_gather | solution.py:23
  72.4 12.8 %copy-start.11 = (bf16[2,128,64]{2,1,0:T(8,128)(2,1)}, bf16[2,128,64]{2,1,0:T(8,128)(2,1)S(1)}, u32[]{:S(2)}) copy-start(bf16[2,128,64]{2,1,0:T(8,128)(2,1)S(1)} %get-tuple-element.1794) | copy-start | bytes 98308
  72.4 12.8 %copy-start.20 = (f32[2,128,32]{2,1,0:T(8,128)}, f32[2,128,32]{2,1,0:T(8,128)S(1)}, u32[]{:S(2)}) copy-start(f32[2,128,32]{2,1,0:T(8,128)S(1)} %get-tuple-element.618) | copy-start | bytes 98308
  72.4 12.8 %copy-start.56 = (f32[2,32]{1,0:T(2,128)}, f32[2,32]{1,0:T(2,128)S(1)}, u32[]{:S(2)}) copy-start(f32[2,32]{1,0:T(2,128)S(1)} %get-tuple-element.620) | copy-start | bytes 772
  73.4 14.9 %copy-start.51 = (f32[32]{0:T(128)S(1)}, f32[32]{0:T(128)}, u32[]{:S(2)}) copy-start(f32[32]{0:T(128)} %param.24) | copy-start | bytes 388
  73.4 16.5 %copy-start.17 = (bf16[256,2048]{1,0:T(8,128)(2,1)S(1)}, bf16[256,2048]{1,0:T(8,128)(2,1)}, u32[]{:S(2)}) copy-start(bf16[256,2048]{1,0:T(8,128)(2,1)} %param.19) | copy-start | bytes 3145732
  73.4 919.3 %all-gather.17.cloned.1.call-start = ((), (), s32[]{:S(2)}) async-start(), calls=%async_computation.4 | async-start | bytes 34078720 | tf_op jit(solution)/shard_map/all_gather | solution.py:23
  85.2 16.0 %copy-start.23 = (bf16[256,64]{1,0:T(8,128)(2,1)S(1)}, bf16[256,64]{1,0:T(8,128)(2,1)}, u32[]{:S(2)}) copy-start(bf16[256,64]{1,0:T(8,128)(2,1)} %get-tuple-element.1101) | copy-start | bytes 98308
  85.2 16.6 %copy-start.22 = (bf16[256,64]{1,0:T(8,128)(2,1)S(1)}, bf16[256,64]{1,0:T(8,128)(2,1)}, u32[]{:S(2)}) copy-start(bf16[256,64]{1,0:T(8,128)(2,1)} %get-tuple-element.1102) | copy-start | bytes 98308
  85.2 17.4 %copy-start.43 = (f32[32]{0:T(128)S(1)}, f32[32]{0:T(128)}, u32[]{:S(2)}) copy-start(f32[32]{0:T(128)} %copy-done.42) | copy-start | bytes 388
  85.3 17.4 %copy-start.45 = (f32[32]{0:T(128)S(1)}, f32[32]{0:T(128)}, u32[]{:S(2)}) copy-start(f32[32]{0:T(128)} %copy-done.44) | copy-start | bytes 388
  85.3 265.3 %copy-start.32 = (bf16[256,32]{0,1:T(8,128)(2,1)S(1)}, bf16[256,32]{0,1:T(8,128)(2,1)}, u32[]{:S(2)}) copy-start(bf16[256,32]{0,1:T(8,128)(2,1)} %copy-done.31) | copy-start | bytes 49156
  85.3 272.1 %collective-permute-start.1 = (bf16[2048,2048]{0,1:T(8,128)(2,1)}, bf16[2048,2048]{0,1:T(8,128)(2,1)}, u32[]{:S(2)}, u32[]{:S(2)}) collective-permute-start(bf16[2048,2048]{0,1:T(8,128)(2,1)} %copy.132), channel_id=1, source_target_pairs={{0,1},{1,0},{2,3},{3,2},{4,5},{5,4},{6,7},{7,6},{8,9},{9,8},{10,11... | collective-permute-start | bytes 25165832 | tf_op jit(solution)/shard_map/ppermute | solution.py:17
  86.5 19.1 %copy-start.19 = (f32[2,128,32]{2,1,0:T(8,128)S(1)}, f32[2,128,32]{2,1,0:T(8,128)}, u32[]{:S(2)}) copy-start(f32[2,128,32]{2,1,0:T(8,128)} %copy-done.18) | copy-start | bytes 98308
  87.8 263.6 %collective-permute-start.2 = (bf16[256,32]{0,1:T(8,128)(2,1)}, bf16[256,32]{0,1:T(8,128)(2,1)}, u32[]{:S(2)}, u32[]{:S(2)}) collective-permute-start(bf16[256,32]{0,1:T(8,128)(2,1)} %fusion.137), channel_id=1, source_target_pairs={{0,1},{1,0},{2,3},{3,2},{4,5},{5,4},{6,7},{7,6},{8,9},{9,8},{10,11... | collective-permute-start | bytes 49160 | tf_op jit(solution)/shard_map/ppermute | solution.py:17
  88.8 260.5 %collective-permute-start.3 = (bf16[32]{0:T(256)(128)(2,1)}, bf16[32]{0:T(256)(128)(2,1)}, u32[]{:S(2)}, u32[]{:S(2)}) collective-permute-start(bf16[32]{0:T(256)(128)(2,1)} %convert_element_type.265), channel_id=1, source_target_pairs={{0,1},{1,0},{2,3},{3,2},{4,5},{5,4},{6,7},{7,6},{8,9},{9,8},{10,11... | collective-permute-start | bytes 200 | tf_op jit(solution)/shard_map/ppermute | solution.py:17
  110.9 238.3 %copy-start.36 = (bf16[2048]{0:T(1024)(128)(2,1)}, bf16[2048]{0:T(1024)(128)(2,1)S(1)}, u32[]{:S(2)}) copy-start(bf16[2048]{0:T(1024)(128)(2,1)S(1)} %dynamic-update-slice) | copy-start | bytes 12292
  111.2 238.1 %copy-start.38 = (bf16[2048]{0:T(1024)(128)(2,1)}, bf16[2048]{0:T(1024)(128)(2,1)S(1)}, u32[]{:S(2)}) copy-start(bf16[2048]{0:T(1024)(128)(2,1)S(1)} %dynamic-update-slice.3) | copy-start | bytes 12292
  381.3 4.3 copy-start.41
  385.6 16.0 %copy-start.37 = (bf16[2048]{0:T(1024)(128)(2,1)S(1)}, bf16[2048]{0:T(1024)(128)(2,1)}, u32[]{:S(2)}) copy-start(bf16[2048]{0:T(1024)(128)(2,1)} %copy-done.36) | copy-start | bytes 12292
  385.6 16.0 %copy-start.39 = (bf16[2048]{0:T(1024)(128)(2,1)S(1)}, bf16[2048]{0:T(1024)(128)(2,1)}, u32[]{:S(2)}) copy-start(bf16[2048]{0:T(1024)(128)(2,1)} %copy-done.38) | copy-start | bytes 12292
  401.4 327.9 %copy-start.59 = (f32[2,32]{1,0:T(2,128)S(1)}, f32[2,32]{1,0:T(2,128)}, u32[]{:S(2)}) copy-start(f32[2,32]{1,0:T(2,128)} %get-tuple-element.611) | copy-start | bytes 772
  729.4 422.7 %reduce-scatter.2.cloned.1.call-start = ((), (), s32[]{:S(2)}) async-start(), calls=%async_computation.1 | async-start | bytes 1572864 | tf_op jit(solution)/shard_map/reduce_scatter | solution.py:214
  729.7 235.0 %copy-start.10 = (bf16[2,128,64]{2,1,0:T(8,128)(2,1)S(1)}, bf16[2,128,64]{2,1,0:T(8,128)(2,1)}, u32[]{:S(2)}) copy-start(bf16[2,128,64]{2,1,0:T(8,128)(2,1)} %get-tuple-element.1793) | copy-start | bytes 98308
  729.7 235.0 %copy-start.29 = (f32[2,128,32]{1,2,0:T(8,128)S(1)}, f32[2,128,32]{1,2,0:T(8,128)}, u32[]{:S(2)}) copy-start(f32[2,128,32]{1,2,0:T(8,128)} %copy.149) | copy-start | bytes 98308
  729.7 235.0 %copy-start.50 = (f32[2,32]{1,0:T(2,128)S(1)}, f32[2,32]{1,0:T(2,128)}, u32[]{:S(2)}) copy-start(f32[2,32]{1,0:T(2,128)} %exp.161) | copy-start | bytes 772
  964.7 3.2 copy-start.4
  964.7 3.2 copy-start.21
  964.8 3.2 copy-start.40
  992.7 106.9 %copy-start.12 = (bf16[2,128,64]{2,1,0:T(8,128)(2,1)S(1)}, bf16[2,128,64]{2,1,0:T(8,128)(2,1)}, u32[]{:S(2)}) copy-start(bf16[2,128,64]{2,1,0:T(8,128)(2,1)} %copy-done.11) | copy-start | bytes 98308
  992.7 106.9 %copy-start.28 = (f32[2,128,32]{1,2,0:T(8,128)S(1)}, f32[2,128,32]{1,2,0:T(8,128)}, u32[]{:S(2)}) copy-start(f32[2,128,32]{1,2,0:T(8,128)} %copy.146) | copy-start | bytes 98308
  992.7 106.9 %copy-start.49 = (f32[2,32]{1,0:T(2,128)S(1)}, f32[2,32]{1,0:T(2,128)}, u32[]{:S(2)}) copy-start(f32[2,32]{1,0:T(2,128)} %exp.159) | copy-start | bytes 772
  1103.9 4.3 copy-start.2
  1103.9 4.3 copy-start.26
  1103.9 4.3 copy-start.52
  1110.2 5.9 copy-start.7
  1127.1 3.7 copy-start.13
  1135.0 4.3 copy-start.6
  (30 other events, 48.5 us)
Sparse Core Ops, SparseCore 0:
  36.7 222.9 all-gather.12
  262.8 175.2 all-gather.14
  441.2 157.7 all-gather.18
  729.5 159.5 all-gather.16
  1117.6 24.9 reduce-scatter.1
where the time goes:
time: 1170 us; the launch traced here: 1160 us
  other arithmetic  365 us (31%)
  blocking collectives  325 us (28%)
  waiting for transfers between devices  238 us (20%)
  local copies, waits for them, and re-layouts  141 us (12%)
  matrix products  63.8 us (5%)
  between operations  15.2 us (1%)
    select_n x128, other arithmetic, step(): return jax.tree.map(lambda a, b: jnp.where(reached, a, b), new, before)  334 us
    unnamed x1, blocking collectives  325 us
    ppermute x4, waiting for transfers between devices, partner(): return lax.ppermute(block, axis, route)  238 us
    unnamed x121, local copies, waits for them, and re-layouts  25.2 us
  transfers between devices with their start and end apart: 9, of which 1 were waited for; matrix products, arithmetic and copies ran while one was open for 36% of the time, Pallas kernels for 0%

commit v1 on v0

v1 whole, which is shorter than its diff:
```python
import jax
import jax.numpy as jnp
from jax import lax
from jax.experimental import pallas as pl
from jax.experimental.pallas import tpu as pltpu
from jax.sharding import PartitionSpec as P

F32 = jnp.float32
BF16 = jnp.bfloat16
ROWS = 256
WIDTH = 2048
LANES = 256
STEPS = WIDTH // LANES
HEAD = 64
STATE = 64
SUB = 64
TILE = 128
SLICES = WIDTH // TILE
BODY = 4 * STATE
FULL = BODY + 16
FF, RF, FB, RB = 0, 1, 2, 3
FORWARD = (True, False, False, True)
NT = (((1,), (1,)), ((), ()))


def mm(a, b):
    return jnp.dot(a, b, preferred_element_type=F32)


def mm_nt(a, b):
    return lax.dot_general(a, b, NT, preferred_element_type=F32)


def iota(shape, dim):
    return lax.broadcasted_iota(jnp.int32, shape, dim)


def split3(x):
    high = x.astype(BF16)
    rest = x - high.astype(F32)
    middle = rest.astype(BF16)
    low = (rest - middle.astype(F32)).astype(BF16)
    return high, middle, low


def exact_mm(ones, x):
    high, middle, low = split3(x)
    return mm(ones, high) + mm(ones, middle) + mm(ones, low)


def pair(x):
    high = x.astype(BF16)
    low = (x - high.astype(F32)).astype(BF16)
    return jnp.concatenate([high, low], axis=1)


def exchange_matrix(n):
    return (iota((n, n), 0) + iota((n, n), 1) == n - 1).astype(BF16)


def spread(rows, base, block, mirrored):
    row = iota((rows, LANES), 0) & 127
    head = block * (LANES // HEAD) + iota((rows, LANES), 1) // HEAD
    if mirrored:
        head = WIDTH // HEAD - 1 - head
    return (row == base + head).astype(BF16)


def picks(n, offset):
    row = iota((n, TILE), 0) & (STATE - 1)
    return (iota((n, TILE), 1) == offset + row).astype(BF16)


def place():
    index = lax.axis_index("ctx")
    return index & 1, (index >> 1) & 1, (index >> 2) & 3, index >> 4


def project_kernel(hidden, weight, proj, pack, cot, u_f, u_r, states, both, scale, keys):
    step = pl.program_id(0)

    @pl.when(step == 0)
    def _():
        flip = exchange_matrix(LANES)
        for b in range(STEPS):
            block = hidden[:, b * LANES : (b + 1) * LANES]
            back = STEPS - 1 - b
            both[0:ROWS, b * LANES : (b + 1) * LANES] = block
            both[ROWS : 2 * ROWS, back * LANES : (back + 1) * LANES] = mm(block, flip).astype(BF16)
        table = pack[0:ROWS, :]
        lane = iota((ROWS, TILE), 1)
        decay = jnp.where(lane < 64, table, 0.0)
        lower = (iota((ROWS, ROWS), 0) >= iota((ROWS, ROWS), 1)).astype(BF16)
        total = exact_mm(lower, decay)
        last = total[ROWS - 1 : ROWS, :]
        weight_of = pltpu.roll(table, 64, 1)
        values = jnp.where(
            lane < 32,
            jnp.exp(last - total) * weight_of,
            jnp.where(
                lane < 64, jnp.exp(total - decay) * weight_of, pltpu.roll(jnp.exp(total), 64, 1)
            ),
        )
        scale[...] = pair(values)
        keys[0] = mm_nt(picks(STATE, 0), proj[0]).astype(BF16)
        keys[1] = mm_nt(picks(STATE, 0), proj[1]).astype(BF16)
        keys[2] = mm_nt(picks(STATE, STATE), proj[0]).astype(BF16)

    u = mm(both[...], weight[...]).astype(BF16)
    u_f[...] = u[0:ROWS]
    u_r[...] = u[ROWS : 2 * ROWS]
    values = (u[0:ROWS].astype(F32), u[ROWS : 2 * ROWS].astype(F32), cot[...].astype(F32))
    for scan in range(3):
        wide = mm(scale[...], spread(2 * TILE, 32 * scan, step, False))
        state = mm(keys[scan], (values[scan] * wide).astype(BF16)).astype(BF16)
        for j in range(LANES // TILE):
            states[j, scan * STATE : (scan + 1) * STATE, :] = state[:, j * TILE : (j + 1) * TILE]


def project(hidden, weight, proj, pack, cot):
    columns = pl.BlockSpec((ROWS, LANES), lambda i: (0, i))
    return pl.pallas_call(
        project_kernel,
        grid=(STEPS,),
        in_specs=[
            pl.BlockSpec((ROWS, WIDTH), lambda i: (0, 0)),
            pl.BlockSpec((WIDTH, LANES), lambda i: (0, i)),
            pl.BlockSpec((2, ROWS, TILE), lambda i: (0, 0, 0)),
            pl.BlockSpec((ROWS + 8, TILE), lambda i: (0, 0)),
            columns,
        ],
        out_specs=[
            columns,
            columns,
            pl.BlockSpec((LANES // TILE, 3 * STATE, TILE), lambda i: (i, 0, 0)),
        ],
        out_shape=[
            jax.ShapeDtypeStruct((ROWS, WIDTH), BF16),
            jax.ShapeDtypeStruct((ROWS, WIDTH), BF16),
            jax.ShapeDtypeStruct((SLICES, 3 * STATE, TILE), BF16),
        ],
        scratch_shapes=[
            pltpu.VMEM((2 * ROWS, WIDTH), BF16),
            pltpu.VMEM((ROWS, 2 * TILE), BF16),
            pltpu.VMEM((3, STATE, ROWS), BF16),
        ],
        cost_estimate=pl.CostEstimate(
            flops=4 * ROWS * WIDTH * WIDTH, bytes_accessed=14 << 20, transcendentals=0
        ),
        name="project",
    )(hidden, weight, proj, pack, cot)


def mirror_kernel(cot, proj, pack, other_pack, states, keep, send):
    core, _, _, _ = place()
    decay = jnp.where(iota((ROWS, TILE), 1) < 64, other_pack[0:ROWS, :], 0.0)
    own = jnp.where(iota((ROWS, TILE), 1) < 64, pack[0:ROWS, :], 0.0)
    lower = (iota((ROWS, ROWS), 0) >= iota((ROWS, ROWS), 1)).astype(BF16)
    total = exact_mm(lower, decay)
    last = total[ROWS - 1 : ROWS, :]
    scale = pair(jnp.exp(last - total + decay))
    keys = mm_nt(picks(STATE, STATE), proj[1]).astype(BF16)
    own_last = exact_mm(jnp.ones((16, ROWS), BF16), own)
    other_last = jnp.broadcast_to(last, (16, TILE))
    row, lane = iota((16, TILE), 0), iota((16, TILE), 1)
    scan, part = row // 3, row % 3

    def parts(x, wanted):
        high, middle, low = split3(jnp.exp(x))
        chosen = jnp.where(
            part == 0, high.astype(F32), jnp.where(part == 1, middle.astype(F32), low.astype(F32))
        )
        return jnp.where(wanted, chosen, 0.0).astype(BF16)

    direction = lane // 32
    own_rows = parts(own_last, (scan < 3) & (direction == (scan == RF).astype(jnp.int32)))
    other_rows = parts(other_last, (scan == RB) & (direction == 1))
    head_row = iota((TILE, LANES), 0) & 31
    for b in range(STEPS):
        head = b * (LANES // HEAD) + iota((TILE, LANES), 1) // HEAD
        straight = (head_row == head).astype(BF16)
        turned = (head_row == WIDTH // HEAD - 1 - head).astype(BF16)
        decays = (mm(own_rows, straight) + mm(other_rows, turned)).astype(BF16)
        wide = mm(scale, spread(2 * TILE, 32, b, True))
        block = cot[:, b * LANES : (b + 1) * LANES].astype(F32)
        state = mm(keys, (block * wide).astype(BF16)).astype(BF16)
        for j in range(LANES // TILE):
            s = b * (LANES // TILE) + j
            half, at = s // (SLICES // 2), s % (SLICES // 2)
            columns = slice(j * TILE, (j + 1) * TILE)

            def write(out):
                out[at, 0 : 3 * STATE, :] = states[s]
                out[at, 3 * STATE : BODY, :] = state[:, columns]
                out[at, BODY:FULL, :] = decays[:, columns]

            @pl.when(core == half)
            def _():
                write(keep)

            @pl.when(core != half)
            def _():
                write(send)


def whole(kernel, outs, args, scratch=(), name=None, flops=0):
    bytes_accessed = sum(a.size * a.dtype.itemsize for a in args)
    bytes_accessed += sum(2 * o.size for o in outs)
    return pl.pallas_call(
        kernel,
        out_shape=outs,
        in_specs=[pl.BlockSpec(memory_space=pltpu.VMEM)] * len(args),
        out_specs=[pl.BlockSpec(memory_space=pltpu.VMEM)] * len(outs),
        scratch_shapes=list(scratch),
        cost_estimate=pl.CostEstimate(
            flops=flops, bytes_accessed=bytes_accessed, transcendentals=0
        ),
        name=name,
    )(*args)


def shape(*dims):
    return jax.ShapeDtypeStruct(dims, BF16)


def read_decays(tile):
    tile = tile.astype(F32)
    return [
        tile[3 * i : 3 * i + 1] + tile[3 * i + 1 : 3 * i + 2] + tile[3 * i + 2 : 3 * i + 3]
        for i in range(tile.shape[0] // 4)
    ]


def decay_rows(decays):
    row = iota((16, TILE), 0)
    out = jnp.zeros((16, TILE), F32)
    for i, d in enumerate(decays):
        for j, p in enumerate(split3(d)):
            out = jnp.where(row == 3 * i + j, p.astype(F32), out)
    return out.astype(BF16)


def rows_of(scan):
    return slice(scan * STATE, (scan + 1) * STATE)


def pair_total(own, got, at, first, out, to):
    mine, theirs = read_decays(own[at, BODY:FULL, :]), read_decays(got[at, BODY:FULL, :])
    for scan in range(4):
        early = first if FORWARD[scan] else 1.0 - first
        alpha = early * theirs[scan] + (1.0 - early)
        beta = early + (1.0 - early) * mine[scan]
        out[to, rows_of(scan), :] = (
            alpha * own[at, rows_of(scan), :].astype(F32)
            + beta * got[at, rows_of(scan), :].astype(F32)
        ).astype(BF16)
    out[to, BODY:FULL, :] = decay_rows([a * b for a, b in zip(mine, theirs)])


def pair_carry(own, got, at, first, carry, mine, theirs, scan):
    early = first if FORWARD[scan] else 1.0 - first
    here = (1.0 - early) * (theirs[scan] * carry + got[at, rows_of(scan), :].astype(F32))
    here = here + early * carry
    there = early * (mine[scan] * carry + own[at, rows_of(scan), :].astype(F32))
    there = there + (1.0 - early) * carry
    return here.astype(BF16), there.astype(BF16)


def core_up_kernel(own, got, keep, send):
    core, x, _, _ = place()
    first = 1.0 - core.astype(F32)

    @pl.loop(0, 4)
    def _(j):
        pair_total(own, got, x * 4 + j, first, keep, j)
        pair_total(own, got, (1 - x) * 4 + j, first, send, j)


def x_up_kernel(own, got, *outs):
    _, x, y, _ = place()
    first = 1.0 - x.astype(F32)
    for k in range(4):
        pair_total(own, got, (y + k) & 3, first, outs[k], 0)


def y_total_kernel(a0, a1, a2, a3, z1, z2, z3, stack, total):
    _, _, y, z = place()
    for k, a in enumerate((a0, a1, a2, a3)):
        stack[(y - k) & 3] = a[0]
    decays = [read_decays(stack[p, BODY:FULL, :]) for p in range(4)]
    for scan in range(4):
        order = (0, 1, 2, 3) if FORWARD[scan] else (3, 2, 1, 0)
        t = stack[order[0], rows_of(scan), :].astype(F32)
        for p in order[1:]:
            t = decays[p][scan] * t + stack[p, rows_of(scan), :].astype(F32)
        total[rows_of(scan), :] = t.astype(BF16)
    product = [decays[0][s] * decays[1][s] * decays[2][s] * decays[3][s] for s in range(4)]
    later = decay_rows([product[FF], product[RB]])
    earlier = decay_rows([product[RF], product[FB]])
    for k, out in enumerate((z1, z2, z3)):

        @pl.when(z + k + 1 < 4)
        def _():
            out[0:STATE, :] = total[rows_of(FF), :]
            out[STATE : 2 * STATE, :] = total[rows_of(RB), :]
            out[2 * STATE :, :] = later

        @pl.when(z + k + 1 >= 4)
        def _():
            out[0:STATE, :] = total[rows_of(RF), :]
            out[STATE : 2 * STATE, :] = total[rows_of(FB), :]
            out[2 * STATE :, :] = earlier


def z_carry_kernel(a0, a1, a2, a3, q1, q2, q3, d0, d1, d2, d3, stack, out):
    _, _, y, z = place()
    for k, a in enumerate((a0, a1, a2, a3)):
        stack[(y - k) & 3] = a[0]
    decays = [read_decays(stack[p, BODY:FULL, :]) for p in range(4)]
    got = (q1, q2, q3)
    plane = [read_decays(q[2 * STATE :, :]) for q in got]
    before = [(z >= k).astype(F32) for k in (1, 2, 3)]
    for scan in range(4):
        half = 0 if scan in (FF, RF) else 1
        part = [q[half * STATE : (half + 1) * STATE, :].astype(F32) for q in got]
        d = [p[half] for p in plane]
        if FORWARD[scan]:
            m = before
            order, positions = (0, 1, 2), (0, 1, 2, 3)
        else:
            m = [1.0 - b for b in before]
            order, positions = (2, 1, 0), (3, 2, 1, 0)
        i, j, k = order
        c = m[i] * (part[i] + d[i] * (m[j] * (part[j] + d[j] * (m[k] * part[k]))))
        for p in positions:
            out[p, rows_of(scan), :] = c.astype(BF16)
            if p != positions[-1]:
                c = decays[p][scan] * c + stack[p, rows_of(scan), :].astype(F32)
    for k, d in enumerate((d0, d1, d2, d3)):
        d[...] = out[(y - k) & 3]


def x_down_kernel(c0, c1, c2, c3, own, got, keep, send):
    _, x, y, _ = place()
    first = 1.0 - x.astype(F32)
    for k, c in enumerate((c0, c1, c2, c3)):
        at = (y + k) & 3
        mine, theirs = read_decays(own[at, BODY:FULL, :]), read_decays(got[at, BODY:FULL, :])
        for scan in range(4):
            here, there = pair_carry(
                own, got, at, first, c[rows_of(scan), :].astype(F32), mine, theirs, scan
            )
            keep[at, rows_of(scan), :] = here
            send[at, rows_of(scan), :] = there


def core_down_kernel(c_own, c_got, own, got, f_keep, f_send, b_same, b_cross, r_same, r_cross):
    core, x, _, _ = place()
    first = 1.0 - core.astype(F32)

    @pl.loop(0, 4)
    def _(j):
        for carry, side in ((c_own, x), (c_got, 1 - x)):
            at = side * 4 + j
            mine, theirs = read_decays(own[at, BODY:FULL, :]), read_decays(got[at, BODY:FULL, :])
            for scan, here_out, there_out, row in (
                (FF, f_keep, f_send, 0),
                (FB, f_keep, f_send, STATE),
                (RB, b_same, b_cross, 0),
                (RF, r_same, r_cross, 0),
            ):
                here, there = pair_carry(
                    own,
                    got,
                    at,
                    first,
                    carry[j, rows_of(scan), :].astype(F32),
                    mine,
                    theirs,
                    scan,
                )
                here_out[at, row : row + STATE, :] = here
                there_out[at, row : row + STATE, :] = there


def ctx_permute(x, target):
    return lax.ppermute(x, "ctx", [(i, target(i)) for i in range(64)])


def core_swap(x):
    return ctx_permute(x, lambda i: i ^ 1)


def x_swap(x):
    return ctx_permute(x, lambda i: i ^ 2)


def y_shift(x, k):
    return ctx_permute(x, lambda i: (i & ~12) | ((i + 4 * k) & 12))


def z_shift(x, k):
    return ctx_permute(x, lambda i: (i + 16 * k) & 63)


def chan_swap(x):
    return lax.ppermute(x, "chan", [(0, 1), (1, 0)])


def cross_swap(x):
    return lax.ppermute(x, ("ctx", "chan"), [(i, i ^ 3) for i in range(128)])


def carries(keep1, send1):
    slices = SLICES // 2
    got1 = core_swap(send1)
    keep2, send2 = whole(
        core_up_kernel, [shape(4, FULL, TILE)] * 2, (keep1, got1), name="core_up"
    )
    got2 = x_swap(send2)
    tops = whole(x_up_kernel, [shape(1, FULL, TILE)] * 4, (keep2, got2), name="x_up")
    row = [tops[0]] + [y_shift(tops[k], k) for k in (1, 2, 3)]
    stack = pltpu.VMEM((4, FULL, TILE), BF16)
    planes = whole(
        y_total_kernel,
        [shape(2 * STATE + 16, TILE)] * 3,
        row,
        [stack, pltpu.VMEM((BODY, TILE), BF16)],
        name="y_total",
    )
    other = [z_shift(planes[k - 1], k) for k in (1, 2, 3)]
    down = whole(
        z_carry_kernel,
        [shape(BODY, TILE)] * 4,
        row + other,
        [stack, pltpu.VMEM((4, BODY, TILE), BF16)],
        name="z_carry",
    )
    down = [down[0]] + [y_shift(down[k], -k) for k in (1, 2, 3)]
    keep3, send3 = whole(
        x_down_kernel, [shape(4, BODY, TILE)] * 2, [*down, keep2, got2], name="x_down"
    )
    got3 = x_swap(send3)
    f_keep, f_send, b_same, b_cross, r_same, r_cross = whole(
        core_down_kernel,
        [shape(slices, 2 * STATE, TILE)] * 2 + [shape(slices, STATE, TILE)] * 4,
        (keep3, got3, keep1, got1),
        name="core_down",
    )
    return (
        (f_keep, core_swap(f_send)),
        (chan_swap(b_same), cross_swap(b_cross)),
        (chan_swap(r_same), cross_swap(r_cross)),
    )


def prepare(tables, proj_of, forward, exclusive, with_weight, in_scale, out_scale, rows_scale):
    lane = iota((ROWS, TILE), 1)
    first, second = tables
    table = jnp.where(lane & 32 == 0, first[0:ROWS, :], second[0:ROWS, :])
    decay = jnp.where(lane < 64, table, 0.0)
    weight = pltpu.roll(table, 64, 1)
    row, column = iota((ROWS, ROWS), 0), iota((ROWS, ROWS), 1)
    same = row // SUB == column // SUB
    total = exact_mm((same & (row >= column)).astype(BF16), decay)
    full = exact_mm(same.astype(BF16), decay)

    def level(i):
        c = total if forward[i] else full - total + decay
        return c - decay if exclusive[i] else c

    rise = jnp.where(lane < 32, level(0), level(1)) - 0.5 * full
    in_scale[...] = pair(jnp.exp(-rise) * weight if with_weight else jnp.exp(-rise))
    out_scale[...] = pair(jnp.exp(rise) if with_weight else jnp.exp(rise) * weight)
    small = iota((16, TILE), 0)
    tail = jnp.where(
        iota((8, TILE), 1) & 32 == 0, first[ROWS : ROWS + 8, :], second[ROWS : ROWS + 8, :]
    )
    half = jnp.exp(0.5 * full)
    values = jnp.broadcast_to(tail[0:1], (16, TILE))
    for b in range(ROWS // SUB):
        values = jnp.where(small == b, half[b * SUB : b * SUB + 1], values)
    rows_scale[...] = pair(values)


def prepare_matrices(proj, query_at, forward, inside, query, keys):
    key_at = STATE - query_at
    row, column = iota((ROWS, ROWS), 0), iota((ROWS, ROWS), 1)
    same = row // SUB == column // SUB
    order = (row >= column) if forward else (row <= column)
    tiled_query = mm_nt(proj, picks(ROWS, query_at))
    tiled_keys = mm_nt(picks(ROWS, key_at), proj)
    q = jnp.where(iota((ROWS, TILE), 1) // STATE == query_at // STATE, proj.astype(F32), 0.0)
    swapped = pltpu.roll(proj.astype(F32), STATE, 1).astype(BF16)
    affinity = mm_nt(q.astype(BF16), swapped)
    inside[...] = jnp.where(same & order, affinity, 0.0).astype(BF16)
    query[...] = jnp.where(same, tiled_query, 0.0).astype(BF16)
    keys[...] = jnp.where(same, tiled_keys, 0.0).astype(BF16)


def scan_block(values, carry, forward, lanes, in_scale, out_scale, rows_scale, mats):
    inside, query, keys = mats
    wide = mm(in_scale[...], lanes)
    small = mm(rows_scale[...], lanes)
    out = mm(out_scale[...], lanes)
    scaled = (values * wide).astype(BF16)
    fresh = mm(keys[...], scaled)
    blocks = ROWS // SUB
    entering = [None] * blocks
    state = carry
    for b in range(blocks) if forward else range(blocks - 1, -1, -1):
        half = small[b : b + 1]
        met = half * state
        entering[b] = met.astype(BF16)
        state = half * (met + fresh[b * SUB : (b + 1) * SUB])
    scan = mm(inside[...], scaled) + mm(query[...], jnp.concatenate(entering, axis=0))
    return scan * out + small[8:9] * values


def carry_block(keep, got, core, block, row):
    mine = (core == block // (STEPS // 2)).astype(F32)
    parts = [
        mine * keep[j, row : row + STATE, :].astype(F32)
        + (1.0 - mine) * got[j, row : row + STATE, :].astype(F32)
        for j in range(LANES // TILE)
    ]
    return jnp.concatenate(parts, axis=1)


def grads_kernel(
    cot, other_cot, proj, pack, f_keep, f_got, b_keep, b_got, du_f, du_r, *scratch
):
    step = pl.program_id(0)
    core, _, _, _ = place()
    in_scale, out_scale, rows_scale = scratch[0:3]
    straight, turned = scratch[3:6], scratch[6:9]

    @pl.when(step == 0)
    def _():
        tables = (pack, pack)
        prepare(
            tables, proj, (False, True), (True, True), False, in_scale, out_scale, rows_scale
        )
        prepare_matrices(proj[0], 0, False, *straight)
        prepare_matrices(proj[1], 0, True, *turned)

    back = STEPS - 1 - step
    du_f[...] = scan_block(
        cot[...].astype(F32),
        carry_block(f_keep, f_got, core, step, STATE),
        False,
        spread(2 * TILE, 0, step, False),
        in_scale,
        out_scale,
        rows_scale,
        straight,
    ).astype(BF16)
    mirrored = scan_block(
        other_cot[...].astype(F32),
        carry_block(b_keep, b_got, core, back, 0),
        True,
        spread(2 * TILE, 32, back, True),
        in_scale,
        out_scale,
        rows_scale,
        turned,
    ).astype(BF16)
    du_r[...] = mm(mirrored, exchange_matrix(LANES)).astype(BF16)


def layer_kernel(
    u_f, other_u, proj, pack, other_pack, f_keep, f_got, r_keep, r_got, out, *scratch
):
    step = pl.program_id(0)
    core, _, _, _ = place()
    in_scale, out_scale, rows_scale = scratch[0:3]
    straight, turned = scratch[3:6], scratch[6:9]

    @pl.when(step == 0)
    def _():
        tables = (pack, other_pack)
        prepare(
            tables, proj, (True, False), (False, False), True, in_scale, out_scale, rows_scale
        )
        prepare_matrices(proj[0], STATE, True, *straight)
        prepare_matrices(proj[1], STATE, False, *turned)

    back = STEPS - 1 - step
    y_f = scan_block(
        u_f[...].astype(F32),
        carry_block(f_keep, f_got, core, step, 0),
        True,
        spread(2 * TILE, 0, step, False),
        in_scale,
        out_scale,
        rows_scale,
        straight,
    )
    y_r = scan_block(
        other_u[...].astype(F32),
        carry_block(r_keep, r_got, core, back, 0),
        False,
        spread(2 * TILE, 32, back, False),
        in_scale,
        out_scale,
        rows_scale,
        turned,
    ).astype(BF16)
    out[...] = (y_f + mm(y_r, exchange_matrix(LANES))).astype(BF16)


def scan_scratch():
    square = pltpu.VMEM((ROWS, ROWS), BF16)
    wide = pltpu.VMEM((ROWS, 2 * TILE), BF16)
    return [wide, wide, pltpu.VMEM((16, 2 * TILE), BF16)] + [square] * 6


def carry_specs(rows, mirrored):
    half = STEPS // 2
    if mirrored:
        return [pl.BlockSpec((LANES // TILE, rows, TILE), lambda i: ((STEPS - 1 - i) % half, 0, 0))] * 2
    return [pl.BlockSpec((LANES // TILE, rows, TILE), lambda i: (i % half, 0, 0))] * 2


COLUMNS = pl.BlockSpec((ROWS, LANES), lambda i: (0, i))
MIRRORED = pl.BlockSpec((ROWS, LANES), lambda i: (0, STEPS - 1 - i))
PROJ = pl.BlockSpec((2, ROWS, TILE), lambda i: (0, 0, 0))
PACK = pl.BlockSpec((ROWS + 8, TILE), lambda i: (0, 0))
SCAN_COST = pl.CostEstimate(flops=10 << 30, bytes_accessed=6 << 20, transcendentals=0)


def grads(cot, other_cot, proj, pack, f_carry, b_carry):
    return pl.pallas_call(
        grads_kernel,
        grid=(STEPS,),
        in_specs=[COLUMNS, MIRRORED, PROJ, PACK]
        + carry_specs(2 * STATE, False)
        + carry_specs(STATE, True),
        out_specs=[COLUMNS, COLUMNS],
        out_shape=[shape(ROWS, WIDTH), shape(ROWS, WIDTH)],
        scratch_shapes=scan_scratch(),
        cost_estimate=SCAN_COST,
        name="grads",
    )(cot, other_cot, proj, pack, *f_carry, *b_carry)


def layer(u_f, other_u, proj, pack, other_pack, f_carry, r_carry):
    return pl.pallas_call(
        layer_kernel,
        grid=(STEPS,),
        in_specs=[COLUMNS, MIRRORED, PROJ, PACK, PACK]
        + carry_specs(2 * STATE, False)
        + carry_specs(STATE, True),
        out_specs=COLUMNS,
        out_shape=shape(ROWS, WIDTH),
        scratch_shapes=scan_scratch(),
        cost_estimate=SCAN_COST,
        name="layer",
    )(u_f, other_u, proj, pack, other_pack, *f_carry, *r_carry)


def back_kernel(half, du_f, du_r, direct, mirrored, *rest):
    total = mm_nt(du_f[...], direct[...])
    turn = mm_nt(du_r[...], mirrored[...])
    high = turn.astype(BF16)
    low = (turn - high.astype(F32)).astype(BF16)
    flip = exchange_matrix(LANES)
    total = total + mm(high, flip) + mm(low, flip)
    if len(rest) == 2:
        total = total + rest[0][...].astype(F32)
    rest[-1][...] = total.astype(rest[-1].dtype)


def back(half, du_f, du_r, weight, dtype):
    steps = STEPS // 2
    spec = pltpu.PrefetchScalarGridSpec(
        num_scalar_prefetch=1,
        grid=(steps,),
        in_specs=[
            pl.BlockSpec((ROWS, WIDTH), lambda i, h: (0, 0)),
            pl.BlockSpec((ROWS, WIDTH), lambda i, h: (0, 0)),
            pl.BlockSpec((LANES, WIDTH), lambda i, h: (h[0] * steps + i, 0)),
            pl.BlockSpec((LANES, WIDTH), lambda i, h: (STEPS - 1 - h[0] * steps - i, 0)),
        ],
        out_specs=pl.BlockSpec((ROWS, LANES), lambda i, h: (0, i)),
    )
    return pl.pallas_call(
        back_kernel,
        grid_spec=spec,
        out_shape=jax.ShapeDtypeStruct((ROWS, WIDTH // 2), dtype),
        cost_estimate=pl.CostEstimate(
            flops=2 * ROWS * WIDTH * WIDTH, bytes_accessed=11 << 20, transcendentals=0
        ),
        name="back",
    )(half, du_f, du_r, weight, weight)


def shards(hidden, in_weight, state_proj, log_decay, step_size, skip_gain, cotangent):
    table = jnp.concatenate([log_decay[0], log_decay[1], step_size[0], step_size[1]], axis=1)
    gains = jnp.broadcast_to(jnp.tile(skip_gain, 4)[None], (8, TILE))
    pack = jnp.concatenate([table, gains], axis=0)
    other_pack = chan_swap(pack)
    other_cot = chan_swap(cotangent)
    u_f, u_r, states = project(hidden, in_weight, state_proj, pack, cotangent)
    keep, send = whole(
        mirror_kernel,
        [shape(SLICES // 2, FULL, TILE)] * 2,
        (cotangent, state_proj, pack, other_pack, states),
        name="mirror",
    )
    other_u = chan_swap(u_r)
    f_carry, b_carry, r_carry = carries(keep, send)
    du_f, du_r = grads(cotangent, other_cot, state_proj, pack, f_carry, b_carry)
    here = lax.axis_index("chan").astype(jnp.int32)[None]
    given = chan_swap(back(1 - here, du_f, du_r, in_weight, BF16))
    kept = back(here, du_f, du_r, in_weight, F32)
    layer_out = layer(u_f, other_u, state_proj, pack, other_pack, f_carry, r_carry)
    input_grad = (kept + given.astype(F32)).astype(BF16)
    return (layer_out, input_grad)


def solution(mesh):
    in_specs = (
        P("ctx", None),
        P(None, "chan"),
        P(None, "ctx", None),
        P(None, "ctx", "chan"),
        P(None, "ctx", "chan"),
        P("chan"),
        P("ctx", "chan"),
    )
    out_specs = (P("ctx", "chan"), P("ctx", "chan"))
    return jax.shard_map(shards, mesh=mesh, in_specs=in_specs, out_specs=out_specs, check_vma=False)
```

time: 1170 us -> 172 us (0.15)
  other arithmetic: 365 us -> 2.33 us
  blocking collectives: 325 us -> 0 us
  waiting for transfers between devices: 238 us -> 53 us
  local copies, waits for them, and re-layouts: 141 us -> 8.86 us
  Pallas kernels: 0 us -> 75.8 us
  matrix products: 63.8 us -> 0 us
  starting transfers between devices: 5.18 us -> 30.7 us
  between operations: 15.2 us -> 0.73 us
    select_n x128 -> x0, other arithmetic: 334 us -> none  [step(): return jax.tree.map(lambda a, b: jnp.where(reached, a, b), new, before)]
    unnamed x1 -> x0, blocking collectives: 325 us -> none
    ppermute x4 -> x21, waiting for transfers between devices: 238 us -> 53 us  [the longest x13 42.8 us: ctx_permute(): return lax.ppermute(x, 'ctx', [(i, target(i)) for i in range(64)])]
    pallas_call x0 -> x12, Pallas kernels: none -> 75.8 us  [the longest x7 18.7 us: whole(): pl.pallas_call(kernel, out_shape=outs, in_specs=[pl.BlockSpec(memory_spac...]
    dot_general x32 -> x0, matrix products: 63.8 us -> none  [the longest x8 17.5 us: advance(): jnp.einsum('hts,shp->thp', mixing, value_blk, preferred_element_type=jnp....]
    rev x23 -> x0, local copies, waits for them, and re-layouts: 59.3 us -> none  [the longest x1 17.6 us: shards(): grad_terms = direct + mirrored[:, ::-1]]
    ppermute x4 -> x21, starting transfers between devices: 4.76 us -> 30.7 us  [the longest x13 23.5 us: ctx_permute(): return lax.ppermute(x, 'ctx', [(i, target(i)) for i in range(64)])]
    unnamed x121 -> x46, local copies, waits for them, and re-layouts: 25.2 us -> 6.54 us
  transfers between devices with their start and end apart: 9 -> 21, of which waited for: 1 -> 14; matrix products, arithmetic and copies ran while one was open for 36% -> 0% of each run, Pallas kernels for 0% -> 41%
where the time goes in v1:
time: 172 us; the launch traced here: 171 us
  Pallas kernels  75.8 us (44%)
  waiting for transfers between devices  53 us (31%)
  starting transfers between devices  30.7 us (18%)
  local copies, waits for them, and re-layouts  8.86 us (5%)
  other arithmetic  2.33 us (1%)
    ppermute x13, waiting for transfers between devices, ctx_permute(): return lax.ppermute(x, 'ctx', [(i, target(i)) for i in range(64)])  42.8 us
    ppermute x13, starting transfers between devices, ctx_permute(): return lax.ppermute(x, 'ctx', [(i, target(i)) for i in range(64)])  23.5 us
    pallas_call x7, Pallas kernels, whole(): pl.pallas_call(kernel, out_shape=outs, in_specs=[pl.BlockSpec(memory_spac...  18.7 us
    pallas_call x2, Pallas kernels, back(): pl.pallas_call(back_kernel, grid_spec=spec, out_shape=jax.ShapeDtypeStruc...  17.7 us
    pallas_call x1, Pallas kernels, project(): pl.pallas_call(project_kernel, grid=(STEPS,), in_specs=[pl.BlockSpec((ROW...  14.9 us
    pallas_call x1, Pallas kernels, layer(): pl.pallas_call(layer_kernel, grid=(STEPS,), in_specs=[COLUMNS, MIRRORED,...  12.3 us
    pallas_call x1, Pallas kernels, grads(): pl.pallas_call(grads_kernel, grid=(STEPS,), in_specs=[COLUMNS, MIRRORED,...  12.2 us
    unnamed x46, local copies, waits for them, and re-layouts  6.54 us
  transfers between devices with their start and end apart: 21, of which 14 were waited for; matrix products, arithmetic and copies ran while one was open for 0% of the time, Pallas kernels for 41%

profile of v1, /device:TPU:1, one launch (start us, length us, event | category | flops | bytes accessed | tf_op | source)
XLA Modules:
  0.0 171.4 jit_solution(2197343328019738844)
XLA Ops:
  0.6 0.7 tile.2
  1.4 0.8 fusion.1
  2.4 0.8 fusion
  3.5 2.1 %collective-permute-start.1 = (f32[264,128]{1,0:T(8,128)S(1)}, f32[264,128]{1,0:T(8,128)S(1)}, u32[]{:S(2)}, u32[]{:S(2)}) collective-permute-start(f32[264,128]{1,0:T(8,128)S(1)} %pad_maximum_fusion.pack), channel_id=1, source_target_pairs={{0,1},{1,0},{2,3},{3,2},{4,5},{5,4},{6,7},{7,6},{8,9},{9,8},{10,11... | collective-permute-start | bytes 405512 | tf_op jit(solution)/shard_map/ppermute | solution.py:407
  5.7 14.9 %project.1 = (bf16[256,2048]{1,0:T(8,128)(2,1)}, bf16[256,2048]{1,0:T(8,128)(2,1)}, bf16[16,192,128]{2,1,0:T(8,128)(2,1)}) custom-call(bf16[256,2048]{1,0:T(8,128)(2,1)} %hidden.1, bf16[2048,2048]{1,0:T(8,128)(2,1)} %mirrored.3, bf16[2,256,128]{2,1,0:T(8,128)(2,1)} %proj.7, f32[264,128]{1,0:T(8,128)} %copy-done.3, bf16[256,2048]{1,0:T(8,128)(2,1)} %cot.5), custom_call_target="tpu_custom_call" | custom-call | flops 4294967296 | bytes 14680064 | tf_op jit(solution)/shard_map/project/pallas_call | solution.py:122
  20.5 0.6 copy-done.8
  21.2 5.8 %mirror.1 = (bf16[8,272,128]{2,1,0:T(8,128)(2,1)}, bf16[8,272,128]{2,1,0:T(8,128)(2,1)}) custom-call(bf16[256,2048]{1,0:T(8,128)(2,1)} %cot.5, bf16[2,256,128]{2,1,0:T(8,128)(2,1)} %proj.7, f32[264,128]{1,0:T(8,128)} %copy-done.3, f32[264,128]{1,0:T(8,128)} %copy-done.8, bf16[16,192,128]{2,1,0:T(8,128)(2,1)} %get-tuple-element.32.states), custom_call_target="tpu_custom_call" | custom-call | bytes 3350528 | tf_op jit(solution)/shard_map/mirror/pallas_call | solution.py:209
  27.0 1.0 collective-permute-start.2
  28.2 1.5 collective-permute-done.2.got
  29.8 0.8 copy-done
  30.6 2.3 %core_up.1 = (bf16[4,272,128]{2,1,0:T(8,128)(2,1)}, bf16[4,272,128]{2,1,0:T(8,128)(2,1)}) custom-call(bf16[8,272,128]{2,1,0:T(8,128)(2,1)} %get-tuple-element.33.own, bf16[8,272,128]{2,1,0:T(8,128)(2,1)} %copy-done), custom_call_target="tpu_custom_call" | custom-call | bytes 1671168 | tf_op jit(solution)/shard_map/core_up/pallas_call | solution.py:209
  32.9 2.4 %collective-permute-start.3 = (bf16[4,272,128]{2,1,0:T(8,128)(2,1)}, bf16[4,272,128]{2,1,0:T(8,128)(2,1)S(1)}, u32[]{:S(2)}, u32[]{:S(2)}) collective-permute-start(bf16[4,272,128]{2,1,0:T(8,128)(2,1)} %get-tuple-element.36), channel_id=1, source_target_pairs={{0,4},{2,6},{4,0},{6,2},{8,12},{10,14},{12,8},{14,10},{16,20},{18,... | collective-permute-start | bytes 835592 | tf_op jit(solution)/shard_map/ppermute | solution.py:387
  35.3 24.9 %collective-permute-done.3.got = bf16[4,272,128]{2,1,0:T(8,128)(2,1)S(1)} collective-permute-done((bf16[4,272,128]{2,1,0:T(8,128)(2,1)}, bf16[4,272,128]{2,1,0:T(8,128)(2,1)S(1)}, u32[]{:S(2)}, u32[]{:S(2)}) %collective-permute-start.3) | collective-permute-done | bytes 278560 | tf_op jit(solution)/shard_map/ppermute | solution.py:387
  60.2 0.7 copy-done.1
  60.9 1.8 %x_up.1 = (bf16[1,272,128]{2,1,0:T(8,128)(2,1)}, bf16[1,272,128]{2,1,0:T(8,128)(2,1)}, bf16[1,272,128]{2,1,0:T(8,128)(2,1)}, bf16[1,272,128]{2,1,0:T(8,128)(2,1)}) custom-call(bf16[4,272,128]{2,1,0:T(8,128)(2,1)} %get-tuple-element.35.own, bf16[4,272,128]{2,1,0:T(8,128)(2,1)} %copy-done.1), custom_call_target="tpu_custom_call" | custom-call | bytes 835584 | tf_op jit(solution)/shard_map/x_up/pallas_call | solution.py:209
  62.7 1.3 collective-permute-start.4
  64.0 2.6 %collective-permute-start.5 = (bf16[1,272,128]{2,1,0:T(8,128)(2,1)}, bf16[1,272,128]{2,1,0:T(8,128)(2,1)S(1)}, u32[]{:S(2)}, u32[]{:S(2)}) collective-permute-start(bf16[1,272,128]{2,1,0:T(8,128)(2,1)} %get-tuple-element.39), channel_id=1, source_target_pairs={{0,16},{2,18},{4,20},{6,22},{8,24},{10,26},{12,28},{14,30},{16,0},... | collective-permute-start | bytes 208904 | tf_op jit(solution)/shard_map/ppermute | solution.py:387
  66.6 1.1 collective-permute-start.6
  67.7 1.7 %collective-permute-done.5.a2 = bf16[1,272,128]{2,1,0:T(8,128)(2,1)S(1)} collective-permute-done((bf16[1,272,128]{2,1,0:T(8,128)(2,1)}, bf16[1,272,128]{2,1,0:T(8,128)(2,1)S(1)}, u32[]{:S(2)}, u32[]{:S(2)}) %collective-permute-start.5) | collective-permute-done | bytes 69664 | tf_op jit(solution)/shard_map/ppermute | solution.py:387
  69.4 1.1 collective-permute-done.6.a3
  71.1 1.7 %y_total.1 = (bf16[144,128]{1,0:T(8,128)(2,1)}, bf16[144,128]{1,0:T(8,128)(2,1)}, bf16[144,128]{1,0:T(8,128)(2,1)}) custom-call(bf16[1,272,128]{2,1,0:T(8,128)(2,1)} %get-tuple-element.37.a0, bf16[1,272,128]{2,1,0:T(8,128)(2,1)} %copy-done.4, bf16[1,272,128]{2,1,0:T(8,128)(2,1)} %copy-done.5, bf16[1,272,128]{2,1,0:T(8,128)(2,1)} %copy-done.6), custom_call_target="tpu_custom_call" | custom-call | bytes 389120 | tf_op jit(solution)/shard_map/y_total/pallas_call | solution.py:209
  72.9 1.6 collective-permute-start.7
  74.5 3.3 %collective-permute-start.8 = (bf16[144,128]{1,0:T(8,128)(2,1)}, bf16[144,128]{1,0:T(8,128)(2,1)S(1)}, u32[]{:S(2)}, u32[]{:S(2)}) collective-permute-start(bf16[144,128]{1,0:T(8,128)(2,1)} %get-tuple-element.42), channel_id=1, source_target_pairs={{0,64},{2,66},{4,68},{6,70},{8,72},{10,74},{12,76},{14,78},{16,80}... | collective-permute-start | bytes 110600 | tf_op jit(solution)/shard_map/ppermute | solution.py:387
  77.8 0.7 collective-permute-start.9
  78.5 1.2 collective-permute-done.8.q2
  79.8 1.1 collective-permute-done.9.q3
  81.4 1.9 %z_carry.1 = (bf16[256,128]{1,0:T(8,128)(2,1)}, bf16[256,128]{1,0:T(8,128)(2,1)}, bf16[256,128]{1,0:T(8,128)(2,1)}, bf16[256,128]{1,0:T(8,128)(2,1)}) custom-call(bf16[1,272,128]{2,1,0:T(8,128)(2,1)} %get-tuple-element.37.a0, bf16[1,272,128]{2,1,0:T(8,128)(2,1)} %copy-done.4, bf16[1,272,128]{2,1,0:T(8,128)(2,1)} %copy-done.5, ...), custom_call_target="tpu_custom_call" | custom-call | bytes 651264 | tf_op jit(solution)/shard_map/z_carry/pallas_call | solution.py:209
  83.3 2.2 %collective-permute-start.10 = (bf16[256,128]{1,0:T(8,128)(2,1)}, bf16[256,128]{1,0:T(8,128)(2,1)S(1)}, u32[]{:S(2)}, u32[]{:S(2)}) collective-permute-start(bf16[256,128]{1,0:T(8,128)(2,1)} %get-tuple-element.45), channel_id=1, source_target_pairs={{0,24},{2,26},{4,28},{6,30},{8,0},{10,2},{12,4},{14,6},{16,8},{18,... | collective-permute-start | bytes 196616 | tf_op jit(solution)/shard_map/ppermute | solution.py:387
  86.1 1.6 collective-permute-done.10.c1
  87.7 2.7 %collective-permute-done.11.c2 = bf16[256,128]{1,0:T(8,128)(2,1)S(1)} collective-permute-done((bf16[256,128]{1,0:T(8,128)(2,1)}, bf16[256,128]{1,0:T(8,128)(2,1)S(1)}, u32[]{:S(2)}, u32[]{:S(2)}) %collective-permute-start.11) | collective-permute-done | bytes 65568 | tf_op jit(solution)/shard_map/ppermute | solution.py:387
  91.3 2.2 %x_down.1 = (bf16[4,256,128]{2,1,0:T(8,128)(2,1)}, bf16[4,256,128]{2,1,0:T(8,128)(2,1)}) custom-call(bf16[256,128]{1,0:T(8,128)(2,1)} %get-tuple-element.44.c0, bf16[256,128]{1,0:T(8,128)(2,1)} %copy-done.9, bf16[256,128]{1,0:T(8,128)(2,1)} %copy-done.10, bf16[256,128]{1,0:T(8,128)(2,1)} %copy-done.11, bf16[4,272,128]{2,1,0:T(8,128)(2,1)} %get-tuple-element.35.own, ...), custom_call_target="tpu_custom_call" | custom-call | bytes 1343488 | tf_op jit(solution)/shard_map/x_down/pallas_call | solution.py:209
  93.8 6.7 %collective-permute-done.13.c_got = bf16[4,256,128]{2,1,0:T(8,128)(2,1)S(1)} collective-permute-done((bf16[4,256,128]{2,1,0:T(8,128)(2,1)}, bf16[4,256,128]{2,1,0:T(8,128)(2,1)S(1)}, u32[]{:S(2)}, u32[]{:S(2)}) %collective-permute-start.13) | collective-permute-done | bytes 262176 | tf_op jit(solution)/shard_map/ppermute | solution.py:387
  100.5 0.7 copy-done.7
  101.2 2.9 %core_down.1 = (bf16[8,128,128]{2,1,0:T(8,128)(2,1)}, bf16[8,128,128]{2,1,0:T(8,128)(2,1)}, bf16[8,64,128]{2,1,0:T(8,128)(2,1)}, bf16[8,64,128]{2,1,0:T(8,128)(2...) custom-call(bf16[4,256,128]{2,1,0:T(8,128)(2,1)} %get-tuple-element.48.c_own, ...), custom_call_target="tpu_custom_call" | custom-call | bytes 2686976 | tf_op jit(solution)/shard_map/core_down/pallas_call | solution.py:209
  104.1 6.5 %collective-permute-start.14 = (bf16[8,128,128]{2,1,0:T(8,128)(2,1)}, bf16[8,128,128]{2,1,0:T(8,128)(2,1)S(1)}, u32[]{:S(2)}, u32[]{:S(2)}) collective-permute-start(bf16[8,128,128]{2,1,0:T(8,128)(2,1)} %get-tuple-element.51), channel_id=1, source_target_pairs={{0,2},{2,0},{4,6},{6,4},{8,10},{10,8},{12,14},{14,12},{16,18},{18,... | collective-permute-start | bytes 786440 | tf_op jit(solution)/shard_map/ppermute | solution.py:387
  110.8 1.4 collective-permute-start.19
  112.5 1.2 collective-permute-start.15
  113.7 2.2 %collective-permute-done.18.b_keep = bf16[8,64,128]{2,1,0:T(8,128)(2,1)S(1)} collective-permute-done((bf16[8,64,128]{2,1,0:T(8,128)(2,1)}, bf16[8,64,128]{2,1,0:T(8,128)(2,1)S(1)}, u32[]{:S(2)}, u32[]{:S(2)}) %collective-permute-start.18) | collective-permute-done | bytes 131104 | tf_op jit(solution)/shard_map/ppermute | solution.py:407
  115.9 1.4 collective-permute-start.16
  117.2 1.9 %collective-permute-done.19.b_got = bf16[8,64,128]{2,1,0:T(8,128)(2,1)S(1)} collective-permute-done((bf16[8,64,128]{2,1,0:T(8,128)(2,1)}, bf16[8,64,128]{2,1,0:T(8,128)(2,1)S(1)}, u32[]{:S(2)}, u32[]{:S(2)}) %collective-permute-start.19) | collective-permute-done | bytes 131104 | tf_op jit(solution)/shard_map/ppermute | solution.py:411
  119.9 12.2 %grads.1 = (bf16[256,2048]{1,0:T(8,128)(2,1)}, bf16[256,2048]{1,0:T(8,128)(2,1)}) custom-call(bf16[256,2048]{1,0:T(8,128)(2,1)} %cot.5, bf16[256,2048]{1,0:T(8,128)(2,1)} %copy-done.15, bf16[2,256,128]{2,1,0:T(8,128)(2,1)} %proj.7, f32[264,128]{1,0:T(8,128)} %copy-done.3, bf16[8,128,128]{2,1,0:T(8,128)(2,1)} %get-tuple-element.50.f_keep, ...), custom_call_target="tpu_custom_call" | custom-call | flops 10737418240 | bytes 6291456 | tf_op jit(solution)/shard_map/grads/pallas_call | solution.py:633
  132.2 8.8 %back.3 = bf16[256,1024]{1,0:T(8,128)(2,1)} custom-call(s32[1]{0:T(128)S(6)} %sub.3.half, bf16[256,2048]{1,0:T(8,128)(2,1)} %get-tuple-element.56.du_f, bf16[256,2048]{1,0:T(8,128)(2,1)} %get-tuple-element.57.du_r, bf16[2048,2048]{1,0:T(8,128)(2,1)} %mirrored.3, bf16[2048,2048]{1,0:T(8,128)(2,1)} %mirrored.3), custom_call_target="tpu_custom_call" | custom-call | flops 2147483648 | bytes 11534336 | tf_op jit(solution)/shard_map/back/pallas_call | solution.py:687
  141.2 2.7 %collective-permute-done.15.r_keep = bf16[8,64,128]{2,1,0:T(8,128)(2,1)S(1)} collective-permute-done((bf16[8,64,128]{2,1,0:T(8,128)(2,1)}, bf16[8,64,128]{2,1,0:T(8,128)(2,1)S(1)}, u32[]{:S(2)}, u32[]{:S(2)}) %collective-permute-start.15) | collective-permute-done | bytes 131104 | tf_op jit(solution)/shard_map/ppermute | solution.py:407
  144.0 3.3 %collective-permute-done.16.r_got = bf16[8,64,128]{2,1,0:T(8,128)(2,1)S(1)} collective-permute-done((bf16[8,64,128]{2,1,0:T(8,128)(2,1)}, bf16[8,64,128]{2,1,0:T(8,128)(2,1)S(1)}, u32[]{:S(2)}, u32[]{:S(2)}) %collective-permute-start.16) | collective-permute-done | bytes 131104 | tf_op jit(solution)/shard_map/ppermute | solution.py:411
  147.3 0.7 copy-done.19
  147.9 12.3 %layer.1 = bf16[256,2048]{1,0:T(8,128)(2,1)} custom-call(bf16[256,2048]{1,0:T(8,128)(2,1)} %get-tuple-element.30.u_f, bf16[256,2048]{1,0:T(8,128)(2,1)} %collective-permute-done.other_u, bf16[2,256,128]{2,1,0:T(8,128)(2,1)} %proj.7, f32[264,128]{1,0:T(8,128)} %copy-done.3, f32[264,128]{1,0:T(8,128)} %copy-done.8, ...), custom_call_target="tpu_custom_call" | custom-call | flops 10737418240 | bytes 6291456 | tf_op jit(solution)/shard_map/layer/pallas_call | solution.py:648
  160.3 8.9 %back.2 = f32[256,1024]{1,0:T(8,128)} custom-call(s32[1]{0:T(128)} %bitcast.4.half, bf16[256,2048]{1,0:T(8,128)(2,1)} %get-tuple-element.56.du_f, bf16[256,2048]{1,0:T(8,128)(2,1)} %get-tuple-element.57.du_r, bf16[2048,2048]{1,0:T(8,128)(2,1)} %mirrored.3, bf16[2048,2048]{1,0:T(8,128)(2,1)} %mirrored.3), custom_call_target="tpu_custom_call" | custom-call | flops 2147483648 | bytes 11534336 | tf_op jit(solution)/shard_map/back/pallas_call | solution.py:687
  169.2 2.2 %add_convert_fusion = bf16[256,1024]{1,0:T(8,128)(2,1)} fusion(f32[256,1024]{1,0:T(8,128)} %back.2, bf16[256,1024]{1,0:T(8,128)(2,1)S(1)} %collective-permute-done.20), kind=kLoop, calls=%fused_computation | loop fusion | flops 786432 | bytes 2097152 | tf_op jit(solution)/shard_map/convert_element_type | solution.py:718
  (59 shorter events, 5.6 us)
Async XLA Ops:
  3.5 2.1 %copy-start.3 = (f32[264,128]{1,0:T(8,128)}, f32[264,128]{1,0:T(8,128)S(1)}, u32[]{:S(2)}) copy-start(f32[264,128]{1,0:T(8,128)S(1)} %pad_maximum_fusion.pack) | copy-start | bytes 405508
  3.5 24.4 %copy-start.2 = (bf16[256,2048]{1,0:T(8,128)(2,1)S(1)}, bf16[256,2048]{1,0:T(8,128)(2,1)}, u32[]{:S(2)}) copy-start(bf16[256,2048]{1,0:T(8,128)(2,1)} %cot.5) | copy-start | bytes 3145732
  3.5 17.0 %collective-permute-start.1 = (f32[264,128]{1,0:T(8,128)S(1)}, f32[264,128]{1,0:T(8,128)S(1)}, u32[]{:S(2)}, u32[]{:S(2)}) collective-permute-start(f32[264,128]{1,0:T(8,128)S(1)} %pad_maximum_fusion.pack), channel_id=1, source_target_pairs={{0,1},{1,0},{2,3},{3,2},{4,5},{5,4},{6,7},{7,6},{8,9},{9,8},{10,11... | collective-permute-start | bytes 405512 | tf_op jit(solution)/shard_map/ppermute | solution.py:407
  20.5 0.7 copy-start.8
  27.0 2.8 %collective-permute-start.2 = (bf16[8,272,128]{2,1,0:T(8,128)(2,1)}, bf16[8,272,128]{2,1,0:T(8,128)(2,1)S(1)}, u32[]{:S(2)}, u32[]{:S(2)}) collective-permute-start(bf16[8,272,128]{2,1,0:T(8,128)(2,1)} %get-tuple-element.34), channel_id=1, source_target_pairs={{0,2},{2,0},{4,6},{6,4},{8,10},{10,8},{12,14},{14,12},{16,18},{18,... | collective-permute-start | bytes 1671176 | tf_op jit(solution)/shard_map/ppermute | solution.py:387
  28.0 84.5 %collective-permute-start.17 = (bf16[256,2048]{1,0:T(8,128)(2,1)S(1)}, bf16[256,2048]{1,0:T(8,128)(2,1)S(1)}, u32[]{:S(2)}, u32[]{:S(2)}) collective-permute-start(bf16[256,2048]{1,0:T(8,128)(2,1)S(1)} %copy-done.2), channel_id=1, source_target_pairs={{0,1},{1,0},{2,3},{3,2},{4,5},{5,4},{6,7},{7,6},{8,9},{9,8},{10,11... | collective-permute-start | bytes 3145736 | tf_op jit(solution)/shard_map/ppermute | solution.py:407
  29.8 0.8 copy-start
  32.9 27.3 %collective-permute-start.3 = (bf16[4,272,128]{2,1,0:T(8,128)(2,1)}, bf16[4,272,128]{2,1,0:T(8,128)(2,1)S(1)}, u32[]{:S(2)}, u32[]{:S(2)}) collective-permute-start(bf16[4,272,128]{2,1,0:T(8,128)(2,1)} %get-tuple-element.36), channel_id=1, source_target_pairs={{0,4},{2,6},{4,0},{6,2},{8,12},{10,14},{12,8},{14,10},{16,20},{18,... | collective-permute-start | bytes 835592 | tf_op jit(solution)/shard_map/ppermute | solution.py:387
  60.2 0.7 copy-start.1
  62.7 5.0 %collective-permute-start.4 = (bf16[1,272,128]{2,1,0:T(8,128)(2,1)}, bf16[1,272,128]{2,1,0:T(8,128)(2,1)S(1)}, u32[]{:S(2)}, u32[]{:S(2)}) collective-permute-start(bf16[1,272,128]{2,1,0:T(8,128)(2,1)} %get-tuple-element.38), channel_id=1, source_target_pairs={{0,8},{2,10},{4,12},{6,14},{8,16},{10,18},{12,20},{14,22},{16,24},... | collective-permute-start | bytes 208904 | tf_op jit(solution)/shard_map/ppermute | solution.py:387
  64.0 5.4 %collective-permute-start.5 = (bf16[1,272,128]{2,1,0:T(8,128)(2,1)}, bf16[1,272,128]{2,1,0:T(8,128)(2,1)S(1)}, u32[]{:S(2)}, u32[]{:S(2)}) collective-permute-start(bf16[1,272,128]{2,1,0:T(8,128)(2,1)} %get-tuple-element.39), channel_id=1, source_target_pairs={{0,16},{2,18},{4,20},{6,22},{8,24},{10,26},{12,28},{14,30},{16,0},... | collective-permute-start | bytes 208904 | tf_op jit(solution)/shard_map/ppermute | solution.py:387
  66.6 3.9 %collective-permute-start.6 = (bf16[1,272,128]{2,1,0:T(8,128)(2,1)}, bf16[1,272,128]{2,1,0:T(8,128)(2,1)S(1)}, u32[]{:S(2)}, u32[]{:S(2)}) collective-permute-start(bf16[1,272,128]{2,1,0:T(8,128)(2,1)} %get-tuple-element.40), channel_id=1, source_target_pairs={{0,24},{2,26},{4,28},{6,30},{8,0},{10,2},{12,4},{14,6},{16,8},{18,... | collective-permute-start | bytes 208904 | tf_op jit(solution)/shard_map/ppermute | solution.py:387
  67.7 2.8 %copy-start.4 = (bf16[1,272,128]{2,1,0:T(8,128)(2,1)}, bf16[1,272,128]{2,1,0:T(8,128)(2,1)S(1)}, u32[]{:S(2)}) copy-start(bf16[1,272,128]{2,1,0:T(8,128)(2,1)S(1)} %collective-permute-done.4.a1) | copy-start | bytes 208900
  69.4 1.1 copy-start.5
  70.5 0.6 copy-start.6
  72.9 5.7 %collective-permute-start.7 = (bf16[144,128]{1,0:T(8,128)(2,1)}, bf16[144,128]{1,0:T(8,128)(2,1)S(1)}, u32[]{:S(2)}, u32[]{:S(2)}) collective-permute-start(bf16[144,128]{1,0:T(8,128)(2,1)} %get-tuple-element.41), channel_id=1, source_target_pairs={{0,32},{2,34},{4,36},{6,38},{8,40},{10,42},{12,44},{14,46},{16,48}... | collective-permute-start | bytes 110600 | tf_op jit(solution)/shard_map/ppermute | solution.py:387
  74.5 5.2 %collective-permute-start.8 = (bf16[144,128]{1,0:T(8,128)(2,1)}, bf16[144,128]{1,0:T(8,128)(2,1)S(1)}, u32[]{:S(2)}, u32[]{:S(2)}) collective-permute-start(bf16[144,128]{1,0:T(8,128)(2,1)} %get-tuple-element.42), channel_id=1, source_target_pairs={{0,64},{2,66},{4,68},{6,70},{8,72},{10,74},{12,76},{14,78},{16,80}... | collective-permute-start | bytes 110600 | tf_op jit(solution)/shard_map/ppermute | solution.py:387
  77.8 3.0 %collective-permute-start.9 = (bf16[144,128]{1,0:T(8,128)(2,1)}, bf16[144,128]{1,0:T(8,128)(2,1)S(1)}, u32[]{:S(2)}, u32[]{:S(2)}) collective-permute-start(bf16[144,128]{1,0:T(8,128)(2,1)} %get-tuple-element.43), channel_id=1, source_target_pairs={{0,96},{2,98},{4,100},{6,102},{8,104},{10,106},{12,108},{14,110},{... | collective-permute-start | bytes 110600 | tf_op jit(solution)/shard_map/ppermute | solution.py:387
  78.5 2.3 %copy-start.12 = (bf16[144,128]{1,0:T(8,128)(2,1)}, bf16[144,128]{1,0:T(8,128)(2,1)S(1)}, u32[]{:S(2)}) copy-start(bf16[144,128]{1,0:T(8,128)(2,1)S(1)} %collective-permute-done.7.q1) | copy-start | bytes 110596
  79.8 1.1 copy-start.13
  80.8 0.6 copy-start.14
  83.3 4.4 %collective-permute-start.10 = (bf16[256,128]{1,0:T(8,128)(2,1)}, bf16[256,128]{1,0:T(8,128)(2,1)S(1)}, u32[]{:S(2)}, u32[]{:S(2)}) collective-permute-start(bf16[256,128]{1,0:T(8,128)(2,1)} %get-tuple-element.45), channel_id=1, source_target_pairs={{0,24},{2,26},{4,28},{6,30},{8,0},{10,2},{12,4},{14,6},{16,8},{18,... | collective-permute-start | bytes 196616 | tf_op jit(solution)/shard_map/ppermute | solution.py:387
  85.5 4.9 %collective-permute-start.11 = (bf16[256,128]{1,0:T(8,128)(2,1)}, bf16[256,128]{1,0:T(8,128)(2,1)S(1)}, u32[]{:S(2)}, u32[]{:S(2)}) collective-permute-start(bf16[256,128]{1,0:T(8,128)(2,1)} %get-tuple-element.46), channel_id=1, source_target_pairs={{0,16},{2,18},{4,20},{6,22},{8,24},{10,26},{12,28},{14,30},{16,0},... | collective-permute-start | bytes 196616 | tf_op jit(solution)/shard_map/ppermute | solution.py:387
  85.5 5.2 %collective-permute-start.12 = (bf16[256,128]{1,0:T(8,128)(2,1)}, bf16[256,128]{1,0:T(8,128)(2,1)S(1)}, u32[]{:S(2)}, u32[]{:S(2)}) collective-permute-start(bf16[256,128]{1,0:T(8,128)(2,1)} %get-tuple-element.47), channel_id=1, source_target_pairs={{0,8},{2,10},{4,12},{6,14},{8,16},{10,18},{12,20},{14,22},{16,24},... | collective-permute-start | bytes 196616 | tf_op jit(solution)/shard_map/ppermute | solution.py:387
  87.7 3.0 %copy-start.9 = (bf16[256,128]{1,0:T(8,128)(2,1)}, bf16[256,128]{1,0:T(8,128)(2,1)S(1)}, u32[]{:S(2)}) copy-start(bf16[256,128]{1,0:T(8,128)(2,1)S(1)} %collective-permute-done.10.c1) | copy-start | bytes 196612
  90.4 0.6 copy-start.10
  90.7 0.6 copy-start.11
  93.6 6.9 %collective-permute-start.13 = (bf16[4,256,128]{2,1,0:T(8,128)(2,1)}, bf16[4,256,128]{2,1,0:T(8,128)(2,1)S(1)}, u32[]{:S(2)}, u32[]{:S(2)}) collective-permute-start(bf16[4,256,128]{2,1,0:T(8,128)(2,1)} %get-tuple-element.49), channel_id=1, source_target_pairs={{0,4},{2,6},{4,0},{6,2},{8,12},{10,14},{12,8},{14,10},{16,20},{18,... | collective-permute-start | bytes 786440 | tf_op jit(solution)/shard_map/ppermute | solution.py:387
  100.5 0.7 copy-start.7
  104.1 15.1 %collective-permute-start.14 = (bf16[8,128,128]{2,1,0:T(8,128)(2,1)}, bf16[8,128,128]{2,1,0:T(8,128)(2,1)S(1)}, u32[]{:S(2)}, u32[]{:S(2)}) collective-permute-start(bf16[8,128,128]{2,1,0:T(8,128)(2,1)} %get-tuple-element.51), channel_id=1, source_target_pairs={{0,2},{2,0},{4,6},{6,4},{8,10},{10,8},{12,14},{14,12},{16,18},{18,... | collective-permute-start | bytes 786440 | tf_op jit(solution)/shard_map/ppermute | solution.py:387
  110.5 5.3 %collective-permute-start.18 = (bf16[8,64,128]{2,1,0:T(8,128)(2,1)}, bf16[8,64,128]{2,1,0:T(8,128)(2,1)S(1)}, u32[]{:S(2)}, u32[]{:S(2)}) collective-permute-start(bf16[8,64,128]{2,1,0:T(8,128)(2,1)} %get-tuple-element.54), channel_id=1, source_target_pairs={{0,1},{1,0},{2,3},{3,2},{4,5},{5,4},{6,7},{7,6},{8,9},{9,8},{10,11... | collective-permute-start | bytes 393224 | tf_op jit(solution)/shard_map/ppermute | solution.py:407
  110.8 8.3 %collective-permute-start.19 = (bf16[8,64,128]{2,1,0:T(8,128)(2,1)}, bf16[8,64,128]{2,1,0:T(8,128)(2,1)S(1)}, u32[]{:S(2)}, u32[]{:S(2)}) collective-permute-start(bf16[8,64,128]{2,1,0:T(8,128)(2,1)} %get-tuple-element.55), channel_id=1, source_target_pairs={{0,3},{1,2},{2,1},{3,0},{4,7},{5,6},{6,5},{7,4},{8,11},{9,10},{10,... | collective-permute-start | bytes 393224 | tf_op jit(solution)/shard_map/ppermute | solution.py:411
  112.2 29.1 %collective-permute-start = (bf16[256,2048]{1,0:T(8,128)(2,1)}, bf16[256,2048]{1,0:T(8,128)(2,1)}, u32[]{:S(2)}, u32[]{:S(2)}) collective-permute-start(bf16[256,2048]{1,0:T(8,128)(2,1)} %get-tuple-element.31), channel_id=1, source_target_pairs={{0,1},{1,0},{2,3},{3,2},{4,5},{5,4},{6,7},{7,6},{8,9},{9,8},{10,11... | collective-permute-start | bytes 3145736 | tf_op jit(solution)/shard_map/ppermute | solution.py:407
  112.5 6.7 %copy-start.15 = (bf16[256,2048]{1,0:T(8,128)(2,1)}, bf16[256,2048]{1,0:T(8,128)(2,1)S(1)}, u32[]{:S(2)}) copy-start(bf16[256,2048]{1,0:T(8,128)(2,1)S(1)} %collective-permute-done.17.other_cot) | copy-start | bytes 3145732
  112.5 31.5 %collective-permute-start.15 = (bf16[8,64,128]{2,1,0:T(8,128)(2,1)}, bf16[8,64,128]{2,1,0:T(8,128)(2,1)S(1)}, u32[]{:S(2)}, u32[]{:S(2)}) collective-permute-start(bf16[8,64,128]{2,1,0:T(8,128)(2,1)} %get-tuple-element.52), channel_id=1, source_target_pairs={{0,1},{1,0},{2,3},{3,2},{4,5},{5,4},{6,7},{7,6},{8,9},{9,8},{10,11... | collective-permute-start | bytes 393224 | tf_op jit(solution)/shard_map/ppermute | solution.py:407
  115.9 3.3 %copy-start.18 = (bf16[8,64,128]{2,1,0:T(8,128)(2,1)}, bf16[8,64,128]{2,1,0:T(8,128)(2,1)S(1)}, u32[]{:S(2)}) copy-start(bf16[8,64,128]{2,1,0:T(8,128)(2,1)S(1)} %collective-permute-done.18.b_keep) | copy-start | bytes 393220
  115.9 31.4 %collective-permute-start.16 = (bf16[8,64,128]{2,1,0:T(8,128)(2,1)}, bf16[8,64,128]{2,1,0:T(8,128)(2,1)S(1)}, u32[]{:S(2)}, u32[]{:S(2)}) collective-permute-start(bf16[8,64,128]{2,1,0:T(8,128)(2,1)} %get-tuple-element.53), channel_id=1, source_target_pairs={{0,3},{1,2},{2,1},{3,0},{4,7},{5,6},{6,5},{7,4},{8,11},{9,10},{10,... | collective-permute-start | bytes 393224 | tf_op jit(solution)/shard_map/ppermute | solution.py:411
  119.2 0.7 copy-start.20
  119.2 0.7 copy-start.16
  140.9 28.3 %collective-permute-start.20 = (bf16[256,1024]{1,0:T(8,128)(2,1)}, bf16[256,1024]{1,0:T(8,128)(2,1)S(1)}, u32[]{:S(2)}, u32[]{:S(2)}) collective-permute-start(bf16[256,1024]{1,0:T(8,128)(2,1)} %back.3), channel_id=1, source_target_pairs={{0,1},{1,0},{2,3},{3,2},{4,5},{5,4},{6,7},{7,6},{8,9},{9,8},{10,11... | collective-permute-start | bytes 1572872 | tf_op jit(solution)/shard_map/ppermute | solution.py:407
  143.9 3.3 %copy-start.17 = (bf16[8,64,128]{2,1,0:T(8,128)(2,1)}, bf16[8,64,128]{2,1,0:T(8,128)(2,1)S(1)}, u32[]{:S(2)}) copy-start(bf16[8,64,128]{2,1,0:T(8,128)(2,1)S(1)} %collective-permute-done.15.r_keep) | copy-start | bytes 393220
  147.3 0.7 copy-start.19

commit v2 on v1

--- a/solution.py
+++ b/solution.py
@@ -203,20 +203,30 @@
                 write(send)
 
 
-def whole(kernel, outs, args, scratch=(), name=None, flops=0):
+def whole(kernel, outs, args, scratch=(), name=None, flops=0, after=(), through=()):
     bytes_accessed = sum(a.size * a.dtype.itemsize for a in args)
     bytes_accessed += sum(2 * o.size for o in outs)
+    first = len(args)
+    start = first + len(after) + len(through)
+    end = start + len(outs)
+
+    def body(*refs):
+        kernel(*refs[:first], *refs[start:end], *refs[end + len(through) :])
+
+    there = [pl.BlockSpec(memory_space=pl.ANY)]
     return pl.pallas_call(
-        kernel,
-        out_shape=outs,
-        in_specs=[pl.BlockSpec(memory_space=pltpu.VMEM)] * len(args),
-        out_specs=[pl.BlockSpec(memory_space=pltpu.VMEM)] * len(outs),
+        body,
+        out_shape=list(outs) + [jax.ShapeDtypeStruct(t.shape, t.dtype) for t in through],
+        in_specs=[pl.BlockSpec(memory_space=pltpu.VMEM)] * len(args)
+        + there * (len(after) + len(through)),
+        out_specs=[pl.BlockSpec(memory_space=pltpu.VMEM)] * len(outs) + there * len(through),
+        input_output_aliases={first + len(after) + i: len(outs) + i for i in range(len(through))},
         scratch_shapes=list(scratch),
         cost_estimate=pl.CostEstimate(
             flops=flops, bytes_accessed=bytes_accessed, transcendentals=0
         ),
         name=name,
-    )(*args)
+    )(*args, *after, *through)
 
 
 def shape(*dims):
@@ -411,14 +421,21 @@
     return lax.ppermute(x, ("ctx", "chan"), [(i, i ^ 3) for i in range(128)])
 
 
-def carries(keep1, send1):
+def carries(keep1, send1, other_cot, u_r):
     slices = SLICES // 2
     got1 = core_swap(send1)
     keep2, send2 = whole(
-        core_up_kernel, [shape(4, FULL, TILE)] * 2, (keep1, got1), name="core_up"
+        core_up_kernel,
+        [shape(4, FULL, TILE)] * 2,
+        (keep1, got1),
+        name="core_up",
+        after=(other_cot,),
     )
     got2 = x_swap(send2)
-    tops = whole(x_up_kernel, [shape(1, FULL, TILE)] * 4, (keep2, got2), name="x_up")
+    *tops, u_r = whole(
+        x_up_kernel, [shape(1, FULL, TILE)] * 4, (keep2, got2), name="x_up", through=(u_r,)
+    )
+    other_u = chan_swap(u_r)
     row = [tops[0]] + [y_shift(tops[k], k) for k in (1, 2, 3)]
     stack = pltpu.VMEM((4, FULL, TILE), BF16)
     planes = whole(
@@ -438,7 +455,11 @@
     )
     down = [down[0]] + [y_shift(down[k], -k) for k in (1, 2, 3)]
     keep3, send3 = whole(
-        x_down_kernel, [shape(4, BODY, TILE)] * 2, [*down, keep2, got2], name="x_down"
+        x_down_kernel,
+        [shape(4, BODY, TILE)] * 2,
+        [*down, keep2, got2],
+        name="x_down",
+        after=(other_u,),
     )
     got3 = x_swap(send3)
     f_keep, f_send, b_same, b_cross, r_same, r_cross = whole(
@@ -448,6 +469,7 @@
         name="core_down",
     )
     return (
+        other_u,
         (f_keep, core_swap(f_send)),
         (chan_swap(b_same), cross_swap(b_cross)),
         (chan_swap(r_same), cross_swap(r_cross)),
@@ -708,8 +730,7 @@
         (cotangent, state_proj, pack, other_pack, states),
         name="mirror",
     )
-    other_u = chan_swap(u_r)
-    f_carry, b_carry, r_carry = carries(keep, send)
+    other_u, f_carry, b_carry, r_carry = carries(keep, send, other_cot, u_r)
     du_f, du_r = grads(cotangent, other_cot, state_proj, pack, f_carry, b_carry)
     here = lax.axis_index("chan").astype(jnp.int32)[None]
     given = chan_swap(back(1 - here, du_f, du_r, in_weight, BF16))

time: 172 us -> 160 us (0.930)
  waiting for transfers between devices: 53 us -> 35.6 us
  starting transfers between devices: 30.7 us -> 34.4 us
    ppermute x13, waiting for transfers between devices: 42.8 us -> 23.3 us  [ctx_permute(): return lax.ppermute(x, 'ctx', [(i, target(i)) for i in range(64)])]
    ppermute x6, waiting for transfers between devices: 4.92 us -> 8.93 us  [chan_swap(): return lax.ppermute(x, 'chan', [(0, 1), (1, 0)])]
    ppermute x13, starting transfers between devices: 23.5 us -> 27 us  [ctx_permute(): return lax.ppermute(x, 'ctx', [(i, target(i)) for i in range(64)])]
    ppermute x2, waiting for transfers between devices: 5.25 us -> 3.32 us  [cross_swap(): return lax.ppermute(x, ('ctx', 'chan'), [(i, i ^ 3) for i in range(128)])]
  transfers between devices with their start and end apart: 21 -> 21, of which waited for: 14 -> 13; matrix products, arithmetic and copies ran while one was open for 0% -> 2% of each run, Pallas kernels for 41% -> 42%
where the time goes in v2:
time: 160 us; the launch traced here: 159 us
  Pallas kernels  75.8 us (47%)
  waiting for transfers between devices  35.6 us (22%)
  starting transfers between devices  34.4 us (22%)
  local copies, waits for them, and re-layouts  10.1 us (6%)
  other arithmetic  2.33 us (1%)
    ppermute x13, starting transfers between devices, ctx_permute(): return lax.ppermute(x, 'ctx', [(i, target(i)) for i in range(64)])  27 us
    ppermute x13, waiting for transfers between devices, ctx_permute(): return lax.ppermute(x, 'ctx', [(i, target(i)) for i in range(64)])  23.3 us
    pallas_call x7, Pallas kernels, whole(): pl.pallas_call(body, out_shape=list(outs) + [jax.ShapeDtypeStruct(t.shape...  18.7 us
    pallas_call x2, Pallas kernels, back(): pl.pallas_call(back_kernel, grid_spec=spec, out_shape=jax.ShapeDtypeStruc...  17.7 us
    pallas_call x1, Pallas kernels, project(): pl.pallas_call(project_kernel, grid=(STEPS,), in_specs=[pl.BlockSpec((ROW...  14.8 us
    pallas_call x1, Pallas kernels, layer(): pl.pallas_call(layer_kernel, grid=(STEPS,), in_specs=[COLUMNS, MIRRORED,...  12.3 us
    pallas_call x1, Pallas kernels, grads(): pl.pallas_call(grads_kernel, grid=(STEPS,), in_specs=[COLUMNS, MIRRORED,...  12.2 us
    ppermute x6, waiting for transfers between devices, chan_swap(): return lax.ppermute(x, 'chan', [(0, 1), (1, 0)])  8.93 us
  transfers between devices with their start and end apart: 21, of which 13 were waited for; matrix products, arithmetic and copies ran while one was open for 2% of the time, Pallas kernels for 42%

profile of v2, /device:TPU:1, one launch (start us, length us, event | category | flops | bytes accessed | tf_op | source)
XLA Modules:
  0.0 158.9 jit_solution(6317925569967331445)
XLA Ops:
  0.6 2.1 %collective-permute-start.2 = (bf16[256,2048]{1,0:T(8,128)(2,1)}, bf16[256,2048]{1,0:T(8,128)(2,1)S(1)}, u32[]{:S(2)}, u32[]{:S(2)}) collective-permute-start(bf16[256,2048]{1,0:T(8,128)(2,1)} %cot.3), channel_id=1, source_target_pairs={{0,1},{1,0},{2,3},{3,2},{4,5},{5,4},{6,7},{7,6},{8,9},{9,8},{10,11... | collective-permute-start | bytes 3145736 | tf_op jit(solution)/shard_map/ppermute | solution.py:417
  2.7 0.7 tile.2
  3.5 0.8 fusion
  4.3 0.8 fusion.1
  6.3 14.8 %project.1 = (bf16[256,2048]{1,0:T(8,128)(2,1)}, bf16[256,2048]{1,0:T(8,128)(2,1)}, bf16[16,192,128]{2,1,0:T(8,128)(2,1)}) custom-call(bf16[256,2048]{1,0:T(8,128)(2,1)} %hidden.1, bf16[2048,2048]{1,0:T(8,128)(2,1)} %mirrored.3, bf16[2,256,128]{2,1,0:T(8,128)(2,1)} %proj.5, f32[264,128]{1,0:T(8,128)} %copy-done.4, bf16[256,2048]{1,0:T(8,128)(2,1)} %cot.3), custom_call_target="tpu_custom_call" | custom-call | flops 4294967296 | bytes 14680064 | tf_op jit(solution)/shard_map/project/pallas_call | solution.py:122
  21.1 7.1 %collective-permute-done.refs_3_.other_pack = f32[264,128]{1,0:T(8,128)S(1)} collective-permute-done((f32[264,128]{1,0:T(8,128)S(1)}, f32[264,128]{1,0:T(8,128)S(1)}, u32[]{:S(2)}, u32[]{:S(2)}) %collective-permute-start) | collective-permute-done | bytes 135200 | tf_op jit(solution)/shard_map/ppermute | solution.py:417
  28.2 0.7 copy-done.9
  28.9 5.9 %mirror.1 = (bf16[8,272,128]{2,1,0:T(8,128)(2,1)}, bf16[8,272,128]{2,1,0:T(8,128)(2,1)}) custom-call(bf16[256,2048]{1,0:T(8,128)(2,1)} %cot.3, bf16[2,256,128]{2,1,0:T(8,128)(2,1)} %proj.5, f32[264,128]{1,0:T(8,128)} %copy-done.4, f32[264,128]{1,0:T(8,128)} %copy-done.9, bf16[16,192,128]{2,1,0:T(8,128)(2,1)} %get-tuple-element.32.refs_4_), custom_call_target="tpu_custom_call" | custom-call | bytes 3350528 | tf_op jit(solution)/shard_map/mirror/pallas_call | solution.py:217
  34.8 1.7 %collective-permute-start.1 = (bf16[8,272,128]{2,1,0:T(8,128)(2,1)}, bf16[8,272,128]{2,1,0:T(8,128)(2,1)S(1)}, u32[]{:S(2)}, u32[]{:S(2)}) collective-permute-start(bf16[8,272,128]{2,1,0:T(8,128)(2,1)} %get-tuple-element.34), channel_id=1, source_target_pairs={{0,2},{2,0},{4,6},{6,4},{8,10},{10,8},{12,14},{14,12},{16,18},{18,... | collective-permute-start | bytes 1671176 | tf_op jit(solution)/shard_map/ppermute | solution.py:397
  36.5 1.8 %collective-permute-done.1.refs_1_.refs_3_ = bf16[8,272,128]{2,1,0:T(8,128)(2,1)S(1)} collective-permute-done((bf16[8,272,128]{2,1,0:T(8,128)(2,1)}, bf16[8,272,128]{2,1,0:T(8,128)(2,1)S(1)}, u32[]{:S(2)}, u32[]{:S(2)}) %collective-permute-start.1) | collective-permute-done | bytes 557088 | tf_op jit(solution)/shard_map/ppermute | solution.py:397
  38.3 0.8 copy-done
  39.4 2.3 %core_up.1 = (bf16[4,272,128]{2,1,0:T(8,128)(2,1)}, bf16[4,272,128]{2,1,0:T(8,128)(2,1)}) custom-call(bf16[8,272,128]{2,1,0:T(8,128)(2,1)} %get-tuple-element.33.refs_0_.refs_2_, bf16[8,272,128]{2,1,0:T(8,128)(2,1)} %copy-done, bf16[256,2048]{1,0:T(8,128)(2,1)} %copy-done.3), custom_call_target="tpu_custom_call" | custom-call | bytes 1671168 | tf_op jit(solution)/shard_map/core_up/pallas_call | solution.py:217
  41.8 3.0 %collective-permute-start.3 = (bf16[4,272,128]{2,1,0:T(8,128)(2,1)}, bf16[4,272,128]{2,1,0:T(8,128)(2,1)S(1)}, u32[]{:S(2)}, u32[]{:S(2)}) collective-permute-start(bf16[4,272,128]{2,1,0:T(8,128)(2,1)} %get-tuple-element.36), channel_id=1, source_target_pairs={{0,4},{2,6},{4,0},{6,2},{8,12},{10,14},{12,8},{14,10},{16,20},{18,... | collective-permute-start | bytes 835592 | tf_op jit(solution)/shard_map/ppermute | solution.py:397
  44.8 6.6 %collective-permute-done.3.refs_1_.refs_5_ = bf16[4,272,128]{2,1,0:T(8,128)(2,1)S(1)} collective-permute-done((bf16[4,272,128]{2,1,0:T(8,128)(2,1)}, bf16[4,272,128]{2,1,0:T(8,128)(2,1)S(1)}, u32[]{:S(2)}, u32[]{:S(2)}) %collective-permute-start.3) | collective-permute-done | bytes 278560 | tf_op jit(solution)/shard_map/ppermute | solution.py:397
  51.4 0.7 copy-done.1
  52.1 1.8 %x_up.1 = (bf16[1,272,128]{2,1,0:T(8,128)(2,1)}, bf16[1,272,128]{2,1,0:T(8,128)(2,1)}, bf16[1,272,128]{2,1,0:T(8,128)(2,1)}, bf16[1,272,128]{2,1,0:T(8,128)(2,1)}, bf16[256,2048]{1,0:T(8,128)(2,1)}) custom-call(bf16[4,272,128]{2,1,0:T(8,128)(2,1)} %get-tuple-element.35.refs_0_.refs_4_, ...), custom_call_target="tpu_custom_call", output_to_operand_aliasing={{4}: (2, {})} | custom-call | bytes 835584 | tf_op jit(solution)/shard_map/x_up/pallas_call | solution.py:217
  53.9 1.4 collective-permute-start.4
  55.3 1.3 collective-permute-start.5
  56.6 2.6 %collective-permute-start.6 = (bf16[1,272,128]{2,1,0:T(8,128)(2,1)}, bf16[1,272,128]{2,1,0:T(8,128)(2,1)S(1)}, u32[]{:S(2)}, u32[]{:S(2)}) collective-permute-start(bf16[1,272,128]{2,1,0:T(8,128)(2,1)} %get-tuple-element.41), channel_id=1, source_target_pairs={{0,16},{2,18},{4,20},{6,22},{8,24},{10,26},{12,28},{14,30},{16,0},... | collective-permute-start | bytes 208904 | tf_op jit(solution)/shard_map/ppermute | solution.py:397
  59.3 1.1 collective-permute-start.7
  60.3 1.7 %collective-permute-done.6.refs_2_ = bf16[1,272,128]{2,1,0:T(8,128)(2,1)S(1)} collective-permute-done((bf16[1,272,128]{2,1,0:T(8,128)(2,1)}, bf16[1,272,128]{2,1,0:T(8,128)(2,1)S(1)}, u32[]{:S(2)}, u32[]{:S(2)}) %collective-permute-start.6) | collective-permute-done | bytes 69664 | tf_op jit(solution)/shard_map/ppermute | solution.py:397
  62.0 1.6 collective-permute-done.7.refs_3_
  64.2 1.7 %y_total.1 = (bf16[144,128]{1,0:T(8,128)(2,1)}, bf16[144,128]{1,0:T(8,128)(2,1)}, bf16[144,128]{1,0:T(8,128)(2,1)}) custom-call(bf16[1,272,128]{2,1,0:T(8,128)(2,1)} %get-tuple-element.39.refs_0_, bf16[1,272,128]{2,1,0:T(8,128)(2,1)} %copy-done.5, bf16[1,272,128]{2,1,0:T(8,128)(2,1)} %copy-done.6, bf16[1,272,128]{2,1,0:T(8,128)(2,1)} %copy-done.7), custom_call_target="tpu_custom_call" | custom-call | bytes 389120 | tf_op jit(solution)/shard_map/y_total/pallas_call | solution.py:217
  65.9 1.6 %collective-permute-start.8 = (bf16[144,128]{1,0:T(8,128)(2,1)}, bf16[144,128]{1,0:T(8,128)(2,1)S(1)}, u32[]{:S(2)}, u32[]{:S(2)}) collective-permute-start(bf16[144,128]{1,0:T(8,128)(2,1)} %get-tuple-element.43), channel_id=1, source_target_pairs={{0,32},{2,34},{4,36},{6,38},{8,40},{10,42},{12,44},{14,46},{16,48}... | collective-permute-start | bytes 110600 | tf_op jit(solution)/shard_map/ppermute | solution.py:397
  67.6 3.3 %collective-permute-start.9 = (bf16[144,128]{1,0:T(8,128)(2,1)}, bf16[144,128]{1,0:T(8,128)(2,1)S(1)}, u32[]{:S(2)}, u32[]{:S(2)}) collective-permute-start(bf16[144,128]{1,0:T(8,128)(2,1)} %get-tuple-element.44), channel_id=1, source_target_pairs={{0,64},{2,66},{4,68},{6,70},{8,72},{10,74},{12,76},{14,78},{16,80}... | collective-permute-start | bytes 110600 | tf_op jit(solution)/shard_map/ppermute | solution.py:397
  70.9 0.7 collective-permute-start.10
  71.6 1.2 collective-permute-done.9.refs_5_
  72.8 1.4 collective-permute-done.10.refs_6_
  74.8 1.8 %z_carry.1 = (bf16[256,128]{1,0:T(8,128)(2,1)}, bf16[256,128]{1,0:T(8,128)(2,1)}, bf16[256,128]{1,0:T(8,128)(2,1)}, bf16[256,128]{1,0:T(8,128)(2,1)}) custom-call(bf16[1,272,128]{2,1,0:T(8,128)(2,1)} %get-tuple-element.39.refs_0_, bf16[1,272,128]{2,1,0:T(8,128)(2,1)} %copy-done.5, bf16[1,272,128]{2,1,0:T(8,128)(2,1)} %copy-done.6, ...), custom_call_target="tpu_custom_call" | custom-call | bytes 651264 | tf_op jit(solution)/shard_map/z_carry/pallas_call | solution.py:217
  76.6 2.2 %collective-permute-start.11 = (bf16[256,128]{1,0:T(8,128)(2,1)}, bf16[256,128]{1,0:T(8,128)(2,1)S(1)}, u32[]{:S(2)}, u32[]{:S(2)}) collective-permute-start(bf16[256,128]{1,0:T(8,128)(2,1)} %get-tuple-element.47), channel_id=1, source_target_pairs={{0,24},{2,26},{4,28},{6,30},{8,0},{10,2},{12,4},{14,6},{16,8},{18,... | collective-permute-start | bytes 196616 | tf_op jit(solution)/shard_map/ppermute | solution.py:397
  79.4 1.6 %collective-permute-done.11.refs_1_ = bf16[256,128]{1,0:T(8,128)(2,1)S(1)} collective-permute-done((bf16[256,128]{1,0:T(8,128)(2,1)}, bf16[256,128]{1,0:T(8,128)(2,1)S(1)}, u32[]{:S(2)}, u32[]{:S(2)}) %collective-permute-start.11) | collective-permute-done | bytes 65568 | tf_op jit(solution)/shard_map/ppermute | solution.py:397
  81.1 2.7 %collective-permute-done.12.refs_2_ = bf16[256,128]{1,0:T(8,128)(2,1)S(1)} collective-permute-done((bf16[256,128]{1,0:T(8,128)(2,1)}, bf16[256,128]{1,0:T(8,128)(2,1)S(1)}, u32[]{:S(2)}, u32[]{:S(2)}) %collective-permute-start.12) | collective-permute-done | bytes 65568 | tf_op jit(solution)/shard_map/ppermute | solution.py:397
  85.0 2.2 %x_down.1 = (bf16[4,256,128]{2,1,0:T(8,128)(2,1)}, bf16[4,256,128]{2,1,0:T(8,128)(2,1)}) custom-call(bf16[256,128]{1,0:T(8,128)(2,1)} %get-tuple-element.46.refs_0_, bf16[256,128]{1,0:T(8,128)(2,1)} %copy-done.10, bf16[256,128]{1,0:T(8,128)(2,1)} %copy-done.11, bf16[256,128]{1,0:T(8,128)(2,1)} %copy-done.12, ...), custom_call_target="tpu_custom_call" | custom-call | bytes 1343488 | tf_op jit(solution)/shard_map/x_down/pallas_call | solution.py:217
  87.3 2.5 %collective-permute-start.14 = (bf16[4,256,128]{2,1,0:T(8,128)(2,1)}, bf16[4,256,128]{2,1,0:T(8,128)(2,1)S(1)}, u32[]{:S(2)}, u32[]{:S(2)}) collective-permute-start(bf16[4,256,128]{2,1,0:T(8,128)(2,1)} %get-tuple-element.51), channel_id=1, source_target_pairs={{0,4},{2,6},{4,0},{6,2},{8,12},{10,14},{12,8},{14,10},{16,20},{18,... | collective-permute-start | bytes 786440 | tf_op jit(solution)/shard_map/ppermute | solution.py:397
  89.7 4.5 %collective-permute-done.14.refs_1_ = bf16[4,256,128]{2,1,0:T(8,128)(2,1)S(1)} collective-permute-done((bf16[4,256,128]{2,1,0:T(8,128)(2,1)}, bf16[4,256,128]{2,1,0:T(8,128)(2,1)S(1)}, u32[]{:S(2)}, u32[]{:S(2)}) %collective-permute-start.14) | collective-permute-done | bytes 262176 | tf_op jit(solution)/shard_map/ppermute | solution.py:397
  94.2 0.7 copy-done.8
  94.9 2.9 %core_down.1 = (bf16[8,128,128]{2,1,0:T(8,128)(2,1)}, bf16[8,128,128]{2,1,0:T(8,128)(2,1)}, bf16[8,64,128]{2,1,0:T(8,128)(2,1)}, bf16[8,64,128]{2,1,0:T(8,128)(2...) custom-call(bf16[4,256,128]{2,1,0:T(8,128)(2,1)} %get-tuple-element.50.refs_0_, ...), custom_call_target="tpu_custom_call" | custom-call | bytes 2686976 | tf_op jit(solution)/shard_map/core_down/pallas_call | solution.py:217
  97.8 6.4 %collective-permute-start.15 = (bf16[8,128,128]{2,1,0:T(8,128)(2,1)}, bf16[8,128,128]{2,1,0:T(8,128)(2,1)S(1)}, u32[]{:S(2)}, u32[]{:S(2)}) collective-permute-start(bf16[8,128,128]{2,1,0:T(8,128)(2,1)} %get-tuple-element.53), channel_id=1, source_target_pairs={{0,2},{2,0},{4,6},{6,4},{8,10},{10,8},{12,14},{14,12},{16,18},{18,... | collective-permute-start | bytes 786440 | tf_op jit(solution)/shard_map/ppermute | solution.py:397
  104.4 1.4 collective-permute-start.19
  106.0 1.6 %collective-permute-start.17 = (bf16[8,64,128]{2,1,0:T(8,128)(2,1)}, bf16[8,64,128]{2,1,0:T(8,128)(2,1)S(1)}, u32[]{:S(2)}, u32[]{:S(2)}) collective-permute-start(bf16[8,64,128]{2,1,0:T(8,128)(2,1)} %get-tuple-element.55), channel_id=1, source_target_pairs={{0,3},{1,2},{2,1},{3,0},{4,7},{5,6},{6,5},{7,4},{8,11},{9,10},{10,... | collective-permute-start | bytes 393224 | tf_op jit(solution)/shard_map/ppermute | solution.py:421
  107.6 1.8 %collective-permute-done.18.b_keep = bf16[8,64,128]{2,1,0:T(8,128)(2,1)S(1)} collective-permute-done((bf16[8,64,128]{2,1,0:T(8,128)(2,1)}, bf16[8,64,128]{2,1,0:T(8,128)(2,1)S(1)}, u32[]{:S(2)}, u32[]{:S(2)}) %collective-permute-start.18) | collective-permute-done | bytes 131104 | tf_op jit(solution)/shard_map/ppermute | solution.py:417
  109.5 3.3 %collective-permute-done.19.b_got = bf16[8,64,128]{2,1,0:T(8,128)(2,1)S(1)} collective-permute-done((bf16[8,64,128]{2,1,0:T(8,128)(2,1)}, bf16[8,64,128]{2,1,0:T(8,128)(2,1)S(1)}, u32[]{:S(2)}, u32[]{:S(2)}) %collective-permute-start.19) | collective-permute-done | bytes 131104 | tf_op jit(solution)/shard_map/ppermute | solution.py:421
  113.5 12.2 %grads.1 = (bf16[256,2048]{1,0:T(8,128)(2,1)}, bf16[256,2048]{1,0:T(8,128)(2,1)}) custom-call(bf16[256,2048]{1,0:T(8,128)(2,1)} %cot.3, bf16[256,2048]{1,0:T(8,128)(2,1)} %copy-done.3, bf16[2,256,128]{2,1,0:T(8,128)(2,1)} %proj.5, f32[264,128]{1,0:T(8,128)} %copy-done.4, bf16[8,128,128]{2,1,0:T(8,128)(2,1)} %get-tuple-element.52.f_keep, ...), custom_call_target="tpu_custom_call" | custom-call | flops 10737418240 | bytes 6291456 | tf_op jit(solution)/shard_map/grads/pallas_call | solution.py:655
  125.7 8.8 %back.3 = bf16[256,1024]{1,0:T(8,128)(2,1)} custom-call(s32[1]{0:T(128)S(6)} %sub.3.half, bf16[256,2048]{1,0:T(8,128)(2,1)} %get-tuple-element.58.du_f, bf16[256,2048]{1,0:T(8,128)(2,1)} %get-tuple-element.59.du_r, bf16[2048,2048]{1,0:T(8,128)(2,1)} %mirrored.3, bf16[2048,2048]{1,0:T(8,128)(2,1)} %mirrored.3), custom_call_target="tpu_custom_call" | custom-call | flops 2147483648 | bytes 11534336 | tf_op jit(solution)/shard_map/back/pallas_call | solution.py:709
  134.8 0.6 copy-done.17
  135.5 12.3 %layer.1 = bf16[256,2048]{1,0:T(8,128)(2,1)} custom-call(bf16[256,2048]{1,0:T(8,128)(2,1)} %get-tuple-element.31.u_f, bf16[256,2048]{1,0:T(8,128)(2,1)} %copy-done.2, bf16[2,256,128]{2,1,0:T(8,128)(2,1)} %proj.5, f32[264,128]{1,0:T(8,128)} %copy-done.4, f32[264,128]{1,0:T(8,128)} %copy-done.9, bf16[8,128,128]{2,1,0:T(8,128)(2,1)} %get-tuple-element.52.f_keep, ...), custom_call_target="tpu_custom_call" | custom-call | flops 10737418240 | bytes 6291456 | tf_op jit(solution)/shard_map/layer/pallas_call | solution.py:670
  147.8 8.9 %back.2 = f32[256,1024]{1,0:T(8,128)} custom-call(s32[1]{0:T(128)} %bitcast.4.half, bf16[256,2048]{1,0:T(8,128)(2,1)} %get-tuple-element.58.du_f, bf16[256,2048]{1,0:T(8,128)(2,1)} %get-tuple-element.59.du_r, bf16[2048,2048]{1,0:T(8,128)(2,1)} %mirrored.3, bf16[2048,2048]{1,0:T(8,128)(2,1)} %mirrored.3), custom_call_target="tpu_custom_call" | custom-call | flops 2147483648 | bytes 11534336 | tf_op jit(solution)/shard_map/back/pallas_call | solution.py:709
  156.7 2.2 %add_convert_fusion = bf16[256,1024]{1,0:T(8,128)(2,1)} fusion(f32[256,1024]{1,0:T(8,128)} %back.2, bf16[256,1024]{1,0:T(8,128)(2,1)S(1)} %collective-permute-done.20), kind=kLoop, calls=%fused_computation | loop fusion | flops 786432 | bytes 2097152 | tf_op jit(solution)/shard_map/convert_element_type | solution.py:739
  (59 shorter events, 6.4 us)
Async XLA Ops:
  0.6 37.7 %collective-permute-start.2 = (bf16[256,2048]{1,0:T(8,128)(2,1)}, bf16[256,2048]{1,0:T(8,128)(2,1)S(1)}, u32[]{:S(2)}, u32[]{:S(2)}) collective-permute-start(bf16[256,2048]{1,0:T(8,128)(2,1)} %cot.3), channel_id=1, source_target_pairs={{0,1},{1,0},{2,3},{3,2},{4,5},{5,4},{6,7},{7,6},{8,9},{9,8},{10,11... | collective-permute-start | bytes 3145736 | tf_op jit(solution)/shard_map/ppermute | solution.py:417
  5.6 0.7 copy-start.4
  5.6 22.6 %collective-permute-start = (f32[264,128]{1,0:T(8,128)S(1)}, f32[264,128]{1,0:T(8,128)S(1)}, u32[]{:S(2)}, u32[]{:S(2)}) collective-permute-start(f32[264,128]{1,0:T(8,128)S(1)} %pad_maximum_fusion.pack.refs_2_), channel_id=1, source_target_pairs={{0,1},{1,0},{2,3},{3,2},{4,5},{5,4},{6,7},{7,6},{8,9},{9,8},{10,11... | collective-permute-start | bytes 405512 | tf_op jit(solution)/shard_map/ppermute | solution.py:417
  28.2 0.7 copy-start.9
  34.8 3.5 %collective-permute-start.1 = (bf16[8,272,128]{2,1,0:T(8,128)(2,1)}, bf16[8,272,128]{2,1,0:T(8,128)(2,1)S(1)}, u32[]{:S(2)}, u32[]{:S(2)}) collective-permute-start(bf16[8,272,128]{2,1,0:T(8,128)(2,1)} %get-tuple-element.34), channel_id=1, source_target_pairs={{0,2},{2,0},{4,6},{6,4},{8,10},{10,8},{12,14},{14,12},{16,18},{18,... | collective-permute-start | bytes 1671176 | tf_op jit(solution)/shard_map/ppermute | solution.py:397
  38.3 0.8 copy-start
  38.3 1.1 copy-start.3
  41.8 9.6 %collective-permute-start.3 = (bf16[4,272,128]{2,1,0:T(8,128)(2,1)}, bf16[4,272,128]{2,1,0:T(8,128)(2,1)S(1)}, u32[]{:S(2)}, u32[]{:S(2)}) collective-permute-start(bf16[4,272,128]{2,1,0:T(8,128)(2,1)} %get-tuple-element.36), channel_id=1, source_target_pairs={{0,4},{2,6},{4,0},{6,2},{8,12},{10,14},{12,8},{14,10},{16,20},{18,... | collective-permute-start | bytes 835592 | tf_op jit(solution)/shard_map/ppermute | solution.py:397
  51.4 0.7 copy-start.1
  53.9 30.1 %collective-permute-start.4 = (bf16[256,2048]{1,0:T(8,128)(2,1)}, bf16[256,2048]{1,0:T(8,128)(2,1)S(1)}, u32[]{:S(2)}, u32[]{:S(2)}) collective-permute-start(bf16[256,2048]{1,0:T(8,128)(2,1)} %get-tuple-element.38), channel_id=1, source_target_pairs={{0,1},{1,0},{2,3},{3,2},{4,5},{5,4},{6,7},{7,6},{8,9},{9,8},{10,11... | collective-permute-start | bytes 3145736 | tf_op jit(solution)/shard_map/ppermute | solution.py:417
  55.3 5.0 %collective-permute-start.5 = (bf16[1,272,128]{2,1,0:T(8,128)(2,1)}, bf16[1,272,128]{2,1,0:T(8,128)(2,1)S(1)}, u32[]{:S(2)}, u32[]{:S(2)}) collective-permute-start(bf16[1,272,128]{2,1,0:T(8,128)(2,1)} %get-tuple-element.40), channel_id=1, source_target_pairs={{0,8},{2,10},{4,12},{6,14},{8,16},{10,18},{12,20},{14,22},{16,24},... | collective-permute-start | bytes 208904 | tf_op jit(solution)/shard_map/ppermute | solution.py:397
  56.6 5.4 %collective-permute-start.6 = (bf16[1,272,128]{2,1,0:T(8,128)(2,1)}, bf16[1,272,128]{2,1,0:T(8,128)(2,1)S(1)}, u32[]{:S(2)}, u32[]{:S(2)}) collective-permute-start(bf16[1,272,128]{2,1,0:T(8,128)(2,1)} %get-tuple-element.41), channel_id=1, source_target_pairs={{0,16},{2,18},{4,20},{6,22},{8,24},{10,26},{12,28},{14,30},{16,0},... | collective-permute-start | bytes 208904 | tf_op jit(solution)/shard_map/ppermute | solution.py:397
  59.3 4.3 %collective-permute-start.7 = (bf16[1,272,128]{2,1,0:T(8,128)(2,1)}, bf16[1,272,128]{2,1,0:T(8,128)(2,1)S(1)}, u32[]{:S(2)}, u32[]{:S(2)}) collective-permute-start(bf16[1,272,128]{2,1,0:T(8,128)(2,1)} %get-tuple-element.42), channel_id=1, source_target_pairs={{0,24},{2,26},{4,28},{6,30},{8,0},{10,2},{12,4},{14,6},{16,8},{18,... | collective-permute-start | bytes 208904 | tf_op jit(solution)/shard_map/ppermute | solution.py:397
  60.3 3.3 %copy-start.5 = (bf16[1,272,128]{2,1,0:T(8,128)(2,1)}, bf16[1,272,128]{2,1,0:T(8,128)(2,1)S(1)}, u32[]{:S(2)}) copy-start(bf16[1,272,128]{2,1,0:T(8,128)(2,1)S(1)} %collective-permute-done.5.refs_1_) | copy-start | bytes 208900
  62.0 1.6 copy-start.6
  63.6 0.6 copy-start.7
  65.9 5.7 %collective-permute-start.8 = (bf16[144,128]{1,0:T(8,128)(2,1)}, bf16[144,128]{1,0:T(8,128)(2,1)S(1)}, u32[]{:S(2)}, u32[]{:S(2)}) collective-permute-start(bf16[144,128]{1,0:T(8,128)(2,1)} %get-tuple-element.43), channel_id=1, source_target_pairs={{0,32},{2,34},{4,36},{6,38},{8,40},{10,42},{12,44},{14,46},{16,48}... | collective-permute-start | bytes 110600 | tf_op jit(solution)/shard_map/ppermute | solution.py:397
  67.6 5.2 %collective-permute-start.9 = (bf16[144,128]{1,0:T(8,128)(2,1)}, bf16[144,128]{1,0:T(8,128)(2,1)S(1)}, u32[]{:S(2)}, u32[]{:S(2)}) collective-permute-start(bf16[144,128]{1,0:T(8,128)(2,1)} %get-tuple-element.44), channel_id=1, source_target_pairs={{0,64},{2,66},{4,68},{6,70},{8,72},{10,74},{12,76},{14,78},{16,80}... | collective-permute-start | bytes 110600 | tf_op jit(solution)/shard_map/ppermute | solution.py:397
  70.9 3.3 %collective-permute-start.10 = (bf16[144,128]{1,0:T(8,128)(2,1)}, bf16[144,128]{1,0:T(8,128)(2,1)S(1)}, u32[]{:S(2)}, u32[]{:S(2)}) collective-permute-start(bf16[144,128]{1,0:T(8,128)(2,1)} %get-tuple-element.45), channel_id=1, source_target_pairs={{0,96},{2,98},{4,100},{6,102},{8,104},{10,106},{12,108},{14,110},{... | collective-permute-start | bytes 110600 | tf_op jit(solution)/shard_map/ppermute | solution.py:397
  71.6 2.6 %copy-start.13 = (bf16[144,128]{1,0:T(8,128)(2,1)}, bf16[144,128]{1,0:T(8,128)(2,1)S(1)}, u32[]{:S(2)}) copy-start(bf16[144,128]{1,0:T(8,128)(2,1)S(1)} %collective-permute-done.8.refs_4_) | copy-start | bytes 110596
  72.8 1.4 copy-start.14
  74.2 0.6 copy-start.15
  76.6 4.4 %collective-permute-start.11 = (bf16[256,128]{1,0:T(8,128)(2,1)}, bf16[256,128]{1,0:T(8,128)(2,1)S(1)}, u32[]{:S(2)}, u32[]{:S(2)}) collective-permute-start(bf16[256,128]{1,0:T(8,128)(2,1)} %get-tuple-element.47), channel_id=1, source_target_pairs={{0,24},{2,26},{4,28},{6,30},{8,0},{10,2},{12,4},{14,6},{16,8},{18,... | collective-permute-start | bytes 196616 | tf_op jit(solution)/shard_map/ppermute | solution.py:397
  78.8 4.9 %collective-permute-start.12 = (bf16[256,128]{1,0:T(8,128)(2,1)}, bf16[256,128]{1,0:T(8,128)(2,1)S(1)}, u32[]{:S(2)}, u32[]{:S(2)}) collective-permute-start(bf16[256,128]{1,0:T(8,128)(2,1)} %get-tuple-element.48), channel_id=1, source_target_pairs={{0,16},{2,18},{4,20},{6,22},{8,24},{10,26},{12,28},{14,30},{16,0},... | collective-permute-start | bytes 196616 | tf_op jit(solution)/shard_map/ppermute | solution.py:397
  78.8 5.2 %collective-permute-start.13 = (bf16[256,128]{1,0:T(8,128)(2,1)}, bf16[256,128]{1,0:T(8,128)(2,1)S(1)}, u32[]{:S(2)}, u32[]{:S(2)}) collective-permute-start(bf16[256,128]{1,0:T(8,128)(2,1)} %get-tuple-element.49), channel_id=1, source_target_pairs={{0,8},{2,10},{4,12},{6,14},{8,16},{10,18},{12,20},{14,22},{16,24},... | collective-permute-start | bytes 196616 | tf_op jit(solution)/shard_map/ppermute | solution.py:397
  81.1 3.0 %copy-start.10 = (bf16[256,128]{1,0:T(8,128)(2,1)}, bf16[256,128]{1,0:T(8,128)(2,1)S(1)}, u32[]{:S(2)}) copy-start(bf16[256,128]{1,0:T(8,128)(2,1)S(1)} %collective-permute-done.11.refs_1_) | copy-start | bytes 196612
  83.7 0.6 copy-start.11
  84.0 0.6 copy-start.12
  84.1 1.0 copy-start.2
  87.3 6.9 %collective-permute-start.14 = (bf16[4,256,128]{2,1,0:T(8,128)(2,1)}, bf16[4,256,128]{2,1,0:T(8,128)(2,1)S(1)}, u32[]{:S(2)}, u32[]{:S(2)}) collective-permute-start(bf16[4,256,128]{2,1,0:T(8,128)(2,1)} %get-tuple-element.51), channel_id=1, source_target_pairs={{0,4},{2,6},{4,0},{6,2},{8,12},{10,14},{12,8},{14,10},{16,20},{18,... | collective-permute-start | bytes 786440 | tf_op jit(solution)/shard_map/ppermute | solution.py:397
  94.2 0.7 copy-start.8
  97.8 15.0 %collective-permute-start.15 = (bf16[8,128,128]{2,1,0:T(8,128)(2,1)}, bf16[8,128,128]{2,1,0:T(8,128)(2,1)S(1)}, u32[]{:S(2)}, u32[]{:S(2)}) collective-permute-start(bf16[8,128,128]{2,1,0:T(8,128)(2,1)} %get-tuple-element.53), channel_id=1, source_target_pairs={{0,2},{2,0},{4,6},{6,4},{8,10},{10,8},{12,14},{14,12},{16,18},{18,... | collective-permute-start | bytes 786440 | tf_op jit(solution)/shard_map/ppermute | solution.py:397
  104.1 5.3 %collective-permute-start.18 = (bf16[8,64,128]{2,1,0:T(8,128)(2,1)}, bf16[8,64,128]{2,1,0:T(8,128)(2,1)S(1)}, u32[]{:S(2)}, u32[]{:S(2)}) collective-permute-start(bf16[8,64,128]{2,1,0:T(8,128)(2,1)} %get-tuple-element.56), channel_id=1, source_target_pairs={{0,1},{1,0},{2,3},{3,2},{4,5},{5,4},{6,7},{7,6},{8,9},{9,8},{10,11... | collective-permute-start | bytes 393224 | tf_op jit(solution)/shard_map/ppermute | solution.py:417
  104.4 8.4 %collective-permute-start.19 = (bf16[8,64,128]{2,1,0:T(8,128)(2,1)}, bf16[8,64,128]{2,1,0:T(8,128)(2,1)S(1)}, u32[]{:S(2)}, u32[]{:S(2)}) collective-permute-start(bf16[8,64,128]{2,1,0:T(8,128)(2,1)} %get-tuple-element.57), channel_id=1, source_target_pairs={{0,3},{1,2},{2,1},{3,0},{4,7},{5,6},{6,5},{7,4},{8,11},{9,10},{10,... | collective-permute-start | bytes 393224 | tf_op jit(solution)/shard_map/ppermute | solution.py:421
  105.8 29.0 %collective-permute-start.16 = (bf16[8,64,128]{2,1,0:T(8,128)(2,1)}, bf16[8,64,128]{2,1,0:T(8,128)(2,1)S(1)}, u32[]{:S(2)}, u32[]{:S(2)}) collective-permute-start(bf16[8,64,128]{2,1,0:T(8,128)(2,1)} %get-tuple-element.54), channel_id=1, source_target_pairs={{0,1},{1,0},{2,3},{3,2},{4,5},{5,4},{6,7},{7,6},{8,9},{9,8},{10,11... | collective-permute-start | bytes 393224 | tf_op jit(solution)/shard_map/ppermute | solution.py:417
  106.0 28.7 %collective-permute-start.17 = (bf16[8,64,128]{2,1,0:T(8,128)(2,1)}, bf16[8,64,128]{2,1,0:T(8,128)(2,1)S(1)}, u32[]{:S(2)}, u32[]{:S(2)}) collective-permute-start(bf16[8,64,128]{2,1,0:T(8,128)(2,1)} %get-tuple-element.55), channel_id=1, source_target_pairs={{0,3},{1,2},{2,1},{3,0},{4,7},{5,6},{6,5},{7,4},{8,11},{9,10},{10,... | collective-permute-start | bytes 393224 | tf_op jit(solution)/shard_map/ppermute | solution.py:421
  109.5 3.3 %copy-start.19 = (bf16[8,64,128]{2,1,0:T(8,128)(2,1)}, bf16[8,64,128]{2,1,0:T(8,128)(2,1)S(1)}, u32[]{:S(2)}) copy-start(bf16[8,64,128]{2,1,0:T(8,128)(2,1)S(1)} %collective-permute-done.18.b_keep) | copy-start | bytes 393220
  112.8 0.7 copy-start.20
  112.8 0.7 copy-start.16
  134.5 22.2 %collective-permute-start.20 = (bf16[256,1024]{1,0:T(8,128)(2,1)}, bf16[256,1024]{1,0:T(8,128)(2,1)S(1)}, u32[]{:S(2)}, u32[]{:S(2)}) collective-permute-start(bf16[256,1024]{1,0:T(8,128)(2,1)} %back.3), channel_id=1, source_target_pairs={{0,1},{1,0},{2,3},{3,2},{4,5},{5,4},{6,7},{7,6},{8,9},{9,8},{10,11... | collective-permute-start | bytes 1572872 | tf_op jit(solution)/shard_map/ppermute | solution.py:417
  134.8 0.7 copy-start.17
  134.8 0.7 copy-start.18

commit v3 on v2

--- a/solution.py
+++ b/solution.py
@@ -693,8 +693,9 @@
     rest[-1][...] = total.astype(rest[-1].dtype)
 
 
-def back(half, du_f, du_r, weight, dtype):
+def back(half, du_f, du_r, weight, given=()):
     steps = STEPS // 2
+    columns = pl.BlockSpec((ROWS, LANES), lambda i, h: (0, i))
     spec = pltpu.PrefetchScalarGridSpec(
         num_scalar_prefetch=1,
         grid=(steps,),
@@ -703,24 +704,38 @@
             pl.BlockSpec((ROWS, WIDTH), lambda i, h: (0, 0)),
             pl.BlockSpec((LANES, WIDTH), lambda i, h: (h[0] * steps + i, 0)),
             pl.BlockSpec((LANES, WIDTH), lambda i, h: (STEPS - 1 - h[0] * steps - i, 0)),
-        ],
-        out_specs=pl.BlockSpec((ROWS, LANES), lambda i, h: (0, i)),
+        ]
+        + [columns] * len(given),
+        out_specs=columns,
     )
     return pl.pallas_call(
         back_kernel,
         grid_spec=spec,
-        out_shape=jax.ShapeDtypeStruct((ROWS, WIDTH // 2), dtype),
+        out_shape=shape(ROWS, WIDTH // 2),
         cost_estimate=pl.CostEstimate(
             flops=2 * ROWS * WIDTH * WIDTH, bytes_accessed=11 << 20, transcendentals=0
         ),
         name="back",
-    )(half, du_f, du_r, weight, weight)
+    )(half, du_f, du_r, weight, weight, *given)
+
+
+def pack_kernel(decay, step, gain, out):
+    parts = [decay[0], decay[1], step[0], step[1]]
+    out[0:ROWS, :] = jnp.concatenate(parts, axis=0).T
+    gains = jnp.concatenate([gain[...]] * 4, axis=1)
+    out[ROWS : ROWS + 8, :] = jnp.broadcast_to(gains, (8, TILE))
+
+
+def pack_table(decay, step, gain):
+    return pl.pallas_call(
+        pack_kernel,
+        out_shape=jax.ShapeDtypeStruct((ROWS + 8, TILE), F32),
+        name="pack",
+    )(jnp.swapaxes(decay, 1, 2), jnp.swapaxes(step, 1, 2), gain)
 
 
 def shards(hidden, in_weight, state_proj, log_decay, step_size, skip_gain, cotangent):
-    table = jnp.concatenate([log_decay[0], log_decay[1], step_size[0], step_size[1]], axis=1)
-    gains = jnp.broadcast_to(jnp.tile(skip_gain, 4)[None], (8, TILE))
-    pack = jnp.concatenate([table, gains], axis=0)
+    pack = pack_table(log_decay, step_size, skip_gain.reshape(1, 32))
     other_pack = chan_swap(pack)
     other_cot = chan_swap(cotangent)
     u_f, u_r, states = project(hidden, in_weight, state_proj, pack, cotangent)
@@ -729,14 +744,14 @@
         [shape(SLICES // 2, FULL, TILE)] * 2,
         (cotangent, state_proj, pack, other_pack, states),
         name="mirror",
+        flops=8 << 30,
     )
     other_u, f_carry, b_carry, r_carry = carries(keep, send, other_cot, u_r)
     du_f, du_r = grads(cotangent, other_cot, state_proj, pack, f_carry, b_carry)
     here = lax.axis_index("chan").astype(jnp.int32)[None]
-    given = chan_swap(back(1 - here, du_f, du_r, in_weight, BF16))
-    kept = back(here, du_f, du_r, in_weight, F32)
+    given = chan_swap(back(1 - here, du_f, du_r, in_weight))
     layer_out = layer(u_f, other_u, state_proj, pack, other_pack, f_carry, r_carry)
-    input_grad = (kept + given.astype(F32)).astype(BF16)
+    input_grad = back(here, du_f, du_r, in_weight, (given,))
     return (layer_out, input_grad)
 
 

time: 160 us -> 151 us (0.944)
  waiting for transfers between devices: 35.6 us -> 28.2 us
  local copies, waits for them, and re-layouts: 10.1 us -> 7.5 us
  other arithmetic: 2.33 us -> 0 us
  Pallas kernels: 75.8 us -> 77.7 us
    ppermute x6, waiting for transfers between devices: 8.93 us -> 3.4 us  [chan_swap(): return lax.ppermute(x, 'chan', [(0, 1), (1, 0)])]
    convert_element_type x1 -> x0, other arithmetic: 2.16 us -> none  [shards(): input_grad = (kept + given.astype(F32)).astype(BF16)]
    pallas_call x2 -> x3, Pallas kernels: 17.7 us -> 19.6 us  [the longest x2 17.9 us: back(): pl.pallas_call(back_kernel, grid_spec=spec, out_shape=shape(ROWS, WIDTH /...]
    ppermute x13, waiting for transfers between devices: 23.3 us -> 21.5 us  [ctx_permute(): return lax.ppermute(x, 'ctx', [(i, target(i)) for i in range(64)])]
    ppermute x13, starting transfers between devices: 27 us -> 28.7 us  [ctx_permute(): return lax.ppermute(x, 'ctx', [(i, target(i)) for i in range(64)])]
    unnamed x46 -> x42, local copies, waits for them, and re-layouts: 7.79 us -> 7.5 us
  transfers between devices with their start and end apart: 21 -> 21, of which waited for: 13 -> 14; matrix products, arithmetic and copies ran while one was open for 2% -> 0% of each run, Pallas kernels for 42% -> 38%
where the time goes in v3:
time: 151 us; the launch traced here: 150 us
  Pallas kernels  77.7 us (51%)
  starting transfers between devices  35.9 us (24%)
  waiting for transfers between devices  28.2 us (19%)
  local copies, waits for them, and re-layouts  7.5 us (5%)
    ppermute x13, starting transfers between devices, ctx_permute(): return lax.ppermute(x, 'ctx', [(i, target(i)) for i in range(64)])  28.7 us
    ppermute x13, waiting for transfers between devices, ctx_permute(): return lax.ppermute(x, 'ctx', [(i, target(i)) for i in range(64)])  21.5 us
    pallas_call x7, Pallas kernels, whole(): pl.pallas_call(body, out_shape=list(outs) + [jax.ShapeDtypeStruct(t.shape...  18.7 us
    pallas_call x2, Pallas kernels, back(): pl.pallas_call(back_kernel, grid_spec=spec, out_shape=shape(ROWS, WIDTH /...  17.9 us
    pallas_call x1, Pallas kernels, project(): pl.pallas_call(project_kernel, grid=(STEPS,), in_specs=[pl.BlockSpec((ROW...  14.8 us
    pallas_call x1, Pallas kernels, layer(): pl.pallas_call(layer_kernel, grid=(STEPS,), in_specs=[COLUMNS, MIRRORED,...  12.3 us
    pallas_call x1, Pallas kernels, grads(): pl.pallas_call(grads_kernel, grid=(STEPS,), in_specs=[COLUMNS, MIRRORED,...  12.2 us
    unnamed x42, local copies, waits for them, and re-layouts  7.5 us
  transfers between devices with their start and end apart: 21, of which 14 were waited for; matrix products, arithmetic and copies ran while one was open for 0% of the time, Pallas kernels for 38%

profile of v3, /device:TPU:1, one launch (start us, length us, event | category | flops | bytes accessed | tf_op | source)
XLA Modules:
  0.0 150.0 jit_solution(17270091519316102012)
XLA Ops:
  0.6 1.7 %pack.1.refs_2_ = f32[264,128]{1,0:T(8,128)} custom-call(f32[2,32,256]{2,1,0:T(8,128)} %bitcast.4, f32[2,32,256]{2,1,0:T(8,128)} %bitcast.5, f32[1,32]{1,0:T(1,128)} %bitcast.6), custom_call_target="tpu_custom_call" | custom-call | tf_op jit(solution)/shard_map/pack/pallas_call | solution.py:730
  2.3 2.0 %collective-permute-start = (f32[264,128]{1,0:T(8,128)}, f32[264,128]{1,0:T(8,128)S(1)}, u32[]{:S(2)}, u32[]{:S(2)}) collective-permute-start(f32[264,128]{1,0:T(8,128)} %pack.1.refs_2_), channel_id=1, source_target_pairs={{0,1},{1,0},{2,3},{3,2},{4,5},{5,4},{6,7},{7,6},{8,9},{9,8},{10,11... | collective-permute-start | bytes 405512 | tf_op jit(solution)/shard_map/ppermute | solution.py:417
  4.4 14.8 %project.1 = (bf16[256,2048]{1,0:T(8,128)(2,1)}, bf16[256,2048]{1,0:T(8,128)(2,1)}, bf16[16,192,128]{2,1,0:T(8,128)(2,1)}) custom-call(bf16[256,2048]{1,0:T(8,128)(2,1)} %hidden.1, bf16[2048,2048]{1,0:T(8,128)(2,1)} %mirrored.3, bf16[2,256,128]{2,1,0:T(8,128)(2,1)} %proj.5, f32[264,128]{1,0:T(8,128)} %pack.1.refs_2_, bf16[256,2048]{1,0:T(8,128)(2,1)} %cot.3), custom_call_target="tpu_custom_call" | custom-call | flops 4294967296 | bytes 14680064 | tf_op jit(solution)/shard_map/project/pallas_call | solution.py:122
  19.2 0.6 copy-done.16
  19.8 5.8 %mirror.1 = (bf16[8,272,128]{2,1,0:T(8,128)(2,1)}, bf16[8,272,128]{2,1,0:T(8,128)(2,1)}) custom-call(bf16[256,2048]{1,0:T(8,128)(2,1)} %cot.3, bf16[2,256,128]{2,1,0:T(8,128)(2,1)} %proj.5, f32[264,128]{1,0:T(8,128)} %pack.1.refs_2_, f32[264,128]{1,0:T(8,128)} %copy-done.16, bf16[16,192,128]{2,1,0:T(8,128)(2,1)} %get-tuple-element.32.refs_4_), custom_call_target="tpu_custom_call" | custom-call | flops 8589934592 | bytes 3350528 | tf_op jit(solution)/shard_map/mirror/pallas_call | solution.py:217
  25.7 1.4 collective-permute-start.1
  27.1 1.8 %collective-permute-done.1.refs_1_.refs_3_ = bf16[8,272,128]{2,1,0:T(8,128)(2,1)S(1)} collective-permute-done((bf16[8,272,128]{2,1,0:T(8,128)(2,1)}, bf16[8,272,128]{2,1,0:T(8,128)(2,1)S(1)}, u32[]{:S(2)}, u32[]{:S(2)}) %collective-permute-start.1) | collective-permute-done | bytes 557088 | tf_op jit(solution)/shard_map/ppermute | solution.py:397
  28.9 1.0 collective-permute-done.2.refs_2_.other_cot
  29.8 1.0 copy-done.3
  30.8 2.4 %core_up.1 = (bf16[4,272,128]{2,1,0:T(8,128)(2,1)}, bf16[4,272,128]{2,1,0:T(8,128)(2,1)}) custom-call(bf16[8,272,128]{2,1,0:T(8,128)(2,1)} %get-tuple-element.33.refs_0_.refs_2_, bf16[8,272,128]{2,1,0:T(8,128)(2,1)} %copy-done, bf16[256,2048]{1,0:T(8,128)(2,1)} %copy-done.3), custom_call_target="tpu_custom_call" | custom-call | bytes 1671168 | tf_op jit(solution)/shard_map/core_up/pallas_call | solution.py:217
  33.2 3.2 %collective-permute-start.3 = (bf16[4,272,128]{2,1,0:T(8,128)(2,1)}, bf16[4,272,128]{2,1,0:T(8,128)(2,1)S(1)}, u32[]{:S(2)}, u32[]{:S(2)}) collective-permute-start(bf16[4,272,128]{2,1,0:T(8,128)(2,1)} %get-tuple-element.36), channel_id=1, source_target_pairs={{0,4},{2,6},{4,0},{6,2},{8,12},{10,14},{12,8},{14,10},{16,20},{18,... | collective-permute-start | bytes 835592 | tf_op jit(solution)/shard_map/ppermute | solution.py:397
  36.3 5.4 %collective-permute-done.3.refs_1_.refs_5_ = bf16[4,272,128]{2,1,0:T(8,128)(2,1)S(1)} collective-permute-done((bf16[4,272,128]{2,1,0:T(8,128)(2,1)}, bf16[4,272,128]{2,1,0:T(8,128)(2,1)S(1)}, u32[]{:S(2)}, u32[]{:S(2)}) %collective-permute-start.3) | collective-permute-done | bytes 278560 | tf_op jit(solution)/shard_map/ppermute | solution.py:397
  41.7 0.7 copy-done.1
  42.4 1.8 %x_up.1 = (bf16[1,272,128]{2,1,0:T(8,128)(2,1)}, bf16[1,272,128]{2,1,0:T(8,128)(2,1)}, bf16[1,272,128]{2,1,0:T(8,128)(2,1)}, bf16[1,272,128]{2,1,0:T(8,128)(2,1)}, bf16[256,2048]{1,0:T(8,128)(2,1)}) custom-call(bf16[4,272,128]{2,1,0:T(8,128)(2,1)} %get-tuple-element.35.refs_0_.refs_4_, ...), custom_call_target="tpu_custom_call", output_to_operand_aliasing={{4}: (2, {})} | custom-call | bytes 835584 | tf_op jit(solution)/shard_map/x_up/pallas_call | solution.py:217
  44.3 1.4 collective-permute-start.4
  45.7 1.3 collective-permute-start.5
  47.0 2.6 %collective-permute-start.6 = (bf16[1,272,128]{2,1,0:T(8,128)(2,1)}, bf16[1,272,128]{2,1,0:T(8,128)(2,1)S(1)}, u32[]{:S(2)}, u32[]{:S(2)}) collective-permute-start(bf16[1,272,128]{2,1,0:T(8,128)(2,1)} %get-tuple-element.41), channel_id=1, source_target_pairs={{0,16},{2,18},{4,20},{6,22},{8,24},{10,26},{12,28},{14,30},{16,0},... | collective-permute-start | bytes 208904 | tf_op jit(solution)/shard_map/ppermute | solution.py:397
  49.6 1.1 collective-permute-start.7
  50.7 1.6 %collective-permute-done.6.refs_2_ = bf16[1,272,128]{2,1,0:T(8,128)(2,1)S(1)} collective-permute-done((bf16[1,272,128]{2,1,0:T(8,128)(2,1)}, bf16[1,272,128]{2,1,0:T(8,128)(2,1)S(1)}, u32[]{:S(2)}, u32[]{:S(2)}) %collective-permute-start.6) | collective-permute-done | bytes 69664 | tf_op jit(solution)/shard_map/ppermute | solution.py:397
  52.2 1.0 collective-permute-done.7.refs_3_
  53.9 1.7 %y_total.1 = (bf16[144,128]{1,0:T(8,128)(2,1)}, bf16[144,128]{1,0:T(8,128)(2,1)}, bf16[144,128]{1,0:T(8,128)(2,1)}) custom-call(bf16[1,272,128]{2,1,0:T(8,128)(2,1)} %get-tuple-element.39.refs_0_, bf16[1,272,128]{2,1,0:T(8,128)(2,1)} %copy-done.5, bf16[1,272,128]{2,1,0:T(8,128)(2,1)} %copy-done.6, bf16[1,272,128]{2,1,0:T(8,128)(2,1)} %copy-done.7), custom_call_target="tpu_custom_call" | custom-call | bytes 389120 | tf_op jit(solution)/shard_map/y_total/pallas_call | solution.py:217
  55.6 1.6 %collective-permute-start.8 = (bf16[144,128]{1,0:T(8,128)(2,1)}, bf16[144,128]{1,0:T(8,128)(2,1)S(1)}, u32[]{:S(2)}, u32[]{:S(2)}) collective-permute-start(bf16[144,128]{1,0:T(8,128)(2,1)} %get-tuple-element.43), channel_id=1, source_target_pairs={{0,32},{2,34},{4,36},{6,38},{8,40},{10,42},{12,44},{14,46},{16,48}... | collective-permute-start | bytes 110600 | tf_op jit(solution)/shard_map/ppermute | solution.py:397
  57.3 3.3 %collective-permute-start.9 = (bf16[144,128]{1,0:T(8,128)(2,1)}, bf16[144,128]{1,0:T(8,128)(2,1)S(1)}, u32[]{:S(2)}, u32[]{:S(2)}) collective-permute-start(bf16[144,128]{1,0:T(8,128)(2,1)} %get-tuple-element.44), channel_id=1, source_target_pairs={{0,64},{2,66},{4,68},{6,70},{8,72},{10,74},{12,76},{14,78},{16,80}... | collective-permute-start | bytes 110600 | tf_op jit(solution)/shard_map/ppermute | solution.py:397
  60.6 0.7 collective-permute-start.10
  61.3 1.2 collective-permute-done.9.refs_5_
  62.5 1.4 collective-permute-done.10.refs_6_
  64.5 1.9 %z_carry.1 = (bf16[256,128]{1,0:T(8,128)(2,1)}, bf16[256,128]{1,0:T(8,128)(2,1)}, bf16[256,128]{1,0:T(8,128)(2,1)}, bf16[256,128]{1,0:T(8,128)(2,1)}) custom-call(bf16[1,272,128]{2,1,0:T(8,128)(2,1)} %get-tuple-element.39.refs_0_, bf16[1,272,128]{2,1,0:T(8,128)(2,1)} %copy-done.5, bf16[1,272,128]{2,1,0:T(8,128)(2,1)} %copy-done.6, ...), custom_call_target="tpu_custom_call" | custom-call | bytes 651264 | tf_op jit(solution)/shard_map/z_carry/pallas_call | solution.py:217
  66.4 2.0 %collective-permute-start.11 = (bf16[256,128]{1,0:T(8,128)(2,1)}, bf16[256,128]{1,0:T(8,128)(2,1)S(1)}, u32[]{:S(2)}, u32[]{:S(2)}) collective-permute-start(bf16[256,128]{1,0:T(8,128)(2,1)} %get-tuple-element.47), channel_id=1, source_target_pairs={{0,24},{2,26},{4,28},{6,30},{8,0},{10,2},{12,4},{14,6},{16,8},{18,... | collective-permute-start | bytes 196616 | tf_op jit(solution)/shard_map/ppermute | solution.py:397
  68.3 0.6 collective-permute-start.13
  69.0 1.6 %collective-permute-done.11.refs_1_ = bf16[256,128]{1,0:T(8,128)(2,1)S(1)} collective-permute-done((bf16[256,128]{1,0:T(8,128)(2,1)}, bf16[256,128]{1,0:T(8,128)(2,1)S(1)}, u32[]{:S(2)}, u32[]{:S(2)}) %collective-permute-start.11) | collective-permute-done | bytes 65568 | tf_op jit(solution)/shard_map/ppermute | solution.py:397
  70.6 2.7 %collective-permute-done.12.refs_2_ = bf16[256,128]{1,0:T(8,128)(2,1)S(1)} collective-permute-done((bf16[256,128]{1,0:T(8,128)(2,1)}, bf16[256,128]{1,0:T(8,128)(2,1)S(1)}, u32[]{:S(2)}, u32[]{:S(2)}) %collective-permute-start.12) | collective-permute-done | bytes 65568 | tf_op jit(solution)/shard_map/ppermute | solution.py:397
  74.6 2.2 %x_down.1 = (bf16[4,256,128]{2,1,0:T(8,128)(2,1)}, bf16[4,256,128]{2,1,0:T(8,128)(2,1)}) custom-call(bf16[256,128]{1,0:T(8,128)(2,1)} %get-tuple-element.46.refs_0_, bf16[256,128]{1,0:T(8,128)(2,1)} %copy-done.9, bf16[256,128]{1,0:T(8,128)(2,1)} %copy-done.10, bf16[256,128]{1,0:T(8,128)(2,1)} %copy-done.11, ...), custom_call_target="tpu_custom_call" | custom-call | bytes 1343488 | tf_op jit(solution)/shard_map/x_down/pallas_call | solution.py:217
  76.8 2.4 %collective-permute-start.14 = (bf16[4,256,128]{2,1,0:T(8,128)(2,1)}, bf16[4,256,128]{2,1,0:T(8,128)(2,1)S(1)}, u32[]{:S(2)}, u32[]{:S(2)}) collective-permute-start(bf16[4,256,128]{2,1,0:T(8,128)(2,1)} %get-tuple-element.51), channel_id=1, source_target_pairs={{0,4},{2,6},{4,0},{6,2},{8,12},{10,14},{12,8},{14,10},{16,20},{18,... | collective-permute-start | bytes 786440 | tf_op jit(solution)/shard_map/ppermute | solution.py:397
  79.2 4.5 %collective-permute-done.14.refs_1_ = bf16[4,256,128]{2,1,0:T(8,128)(2,1)S(1)} collective-permute-done((bf16[4,256,128]{2,1,0:T(8,128)(2,1)}, bf16[4,256,128]{2,1,0:T(8,128)(2,1)S(1)}, u32[]{:S(2)}, u32[]{:S(2)}) %collective-permute-start.14) | collective-permute-done | bytes 262176 | tf_op jit(solution)/shard_map/ppermute | solution.py:397
  83.7 0.7 copy-done.8
  84.4 2.9 %core_down.1 = (bf16[8,128,128]{2,1,0:T(8,128)(2,1)}, bf16[8,128,128]{2,1,0:T(8,128)(2,1)}, bf16[8,64,128]{2,1,0:T(8,128)(2,1)}, bf16[8,64,128]{2,1,0:T(8,128)(2...) custom-call(bf16[4,256,128]{2,1,0:T(8,128)(2,1)} %get-tuple-element.50.refs_0_, ...), custom_call_target="tpu_custom_call" | custom-call | bytes 2686976 | tf_op jit(solution)/shard_map/core_down/pallas_call | solution.py:217
  87.3 8.5 %collective-permute-start.15 = (bf16[8,128,128]{2,1,0:T(8,128)(2,1)}, bf16[8,128,128]{2,1,0:T(8,128)(2,1)S(1)}, u32[]{:S(2)}, u32[]{:S(2)}) collective-permute-start(bf16[8,128,128]{2,1,0:T(8,128)(2,1)} %get-tuple-element.53), channel_id=1, source_target_pairs={{0,2},{2,0},{4,6},{6,4},{8,10},{10,8},{12,14},{14,12},{16,18},{18,... | collective-permute-start | bytes 786440 | tf_op jit(solution)/shard_map/ppermute | solution.py:397
  96.0 1.4 collective-permute-start.19
  97.7 1.6 %collective-permute-start.17 = (bf16[8,64,128]{2,1,0:T(8,128)(2,1)}, bf16[8,64,128]{2,1,0:T(8,128)(2,1)S(1)}, u32[]{:S(2)}, u32[]{:S(2)}) collective-permute-start(bf16[8,64,128]{2,1,0:T(8,128)(2,1)} %get-tuple-element.55), channel_id=1, source_target_pairs={{0,3},{1,2},{2,1},{3,0},{4,7},{5,6},{6,5},{7,4},{8,11},{9,10},{10,... | collective-permute-start | bytes 393224 | tf_op jit(solution)/shard_map/ppermute | solution.py:421
  99.3 1.8 %collective-permute-done.18.b_keep = bf16[8,64,128]{2,1,0:T(8,128)(2,1)S(1)} collective-permute-done((bf16[8,64,128]{2,1,0:T(8,128)(2,1)}, bf16[8,64,128]{2,1,0:T(8,128)(2,1)S(1)}, u32[]{:S(2)}, u32[]{:S(2)}) %collective-permute-start.18) | collective-permute-done | bytes 131104 | tf_op jit(solution)/shard_map/ppermute | solution.py:417
  101.1 3.3 %collective-permute-done.19.b_got = bf16[8,64,128]{2,1,0:T(8,128)(2,1)S(1)} collective-permute-done((bf16[8,64,128]{2,1,0:T(8,128)(2,1)}, bf16[8,64,128]{2,1,0:T(8,128)(2,1)S(1)}, u32[]{:S(2)}, u32[]{:S(2)}) %collective-permute-start.19) | collective-permute-done | bytes 131104 | tf_op jit(solution)/shard_map/ppermute | solution.py:421
  104.4 0.6 copy-done.20
  105.1 12.2 %grads.1 = (bf16[256,2048]{1,0:T(8,128)(2,1)}, bf16[256,2048]{1,0:T(8,128)(2,1)}) custom-call(bf16[256,2048]{1,0:T(8,128)(2,1)} %cot.3, bf16[256,2048]{1,0:T(8,128)(2,1)} %copy-done.3, bf16[2,256,128]{2,1,0:T(8,128)(2,1)} %proj.5, f32[264,128]{1,0:T(8,128)} %pack.1.refs_2_, bf16[8,128,128]{2,1,0:T(8,128)(2,1)} %get-tuple-element.52.f_keep, ...), custom_call_target="tpu_custom_call" | custom-call | flops 10737418240 | bytes 6291456 | tf_op jit(solution)/shard_map/grads/pallas_call | solution.py:655
  117.4 8.8 %back.2 = bf16[256,1024]{1,0:T(8,128)(2,1)} custom-call(s32[1]{0:T(128)S(6)} %sub.3.half, bf16[256,2048]{1,0:T(8,128)(2,1)} %get-tuple-element.58.du_f, bf16[256,2048]{1,0:T(8,128)(2,1)} %get-tuple-element.59.du_r, bf16[2048,2048]{1,0:T(8,128)(2,1)} %mirrored.3, bf16[2048,2048]{1,0:T(8,128)(2,1)} %mirrored.3), custom_call_target="tpu_custom_call" | custom-call | flops 2147483648 | bytes 11534336 | tf_op jit(solution)/shard_map/back/pallas_call | solution.py:711
  126.4 0.6 copy-done.17
  127.1 12.3 %layer.1 = bf16[256,2048]{1,0:T(8,128)(2,1)} custom-call(bf16[256,2048]{1,0:T(8,128)(2,1)} %get-tuple-element.31.u_f, bf16[256,2048]{1,0:T(8,128)(2,1)} %copy-done.2, bf16[2,256,128]{2,1,0:T(8,128)(2,1)} %proj.5, f32[264,128]{1,0:T(8,128)} %pack.1.refs_2_, f32[264,128]{1,0:T(8,128)} %copy-done.16, bf16[8,128,128]{2,1,0:T(8,128)(2,1)} %get-tuple-element.52.f_keep, ...), custom_call_target="tpu_custom_call" | custom-call | flops 10737418240 | bytes 6291456 | tf_op jit(solution)/shard_map/layer/pallas_call | solution.py:670
  140.0 0.8 copy-done.4
  140.8 9.1 %back.3 = bf16[256,1024]{1,0:T(8,128)(2,1)} custom-call(s32[1]{0:T(128)} %bitcast.3.half, bf16[256,2048]{1,0:T(8,128)(2,1)} %get-tuple-element.58.du_f, bf16[256,2048]{1,0:T(8,128)(2,1)} %get-tuple-element.59.du_r, bf16[2048,2048]{1,0:T(8,128)(2,1)} %mirrored.3, bf16[2048,2048]{1,0:T(8,128)(2,1)} %mirrored.3, bf16[256,1024]{1,0:T(8,128)(2,1)} %copy-done.4), custom_call_target="tpu_custom_call" | custom-call | flops 2147483648 | bytes 11534336 | tf_op jit(solution)/shard_map/back/pallas_call | solution.py:711
  (49 shorter events, 4.1 us)
Async XLA Ops:
  2.3 16.9 %collective-permute-start = (f32[264,128]{1,0:T(8,128)}, f32[264,128]{1,0:T(8,128)S(1)}, u32[]{:S(2)}, u32[]{:S(2)}) collective-permute-start(f32[264,128]{1,0:T(8,128)} %pack.1.refs_2_), channel_id=1, source_target_pairs={{0,1},{1,0},{2,3},{3,2},{4,5},{5,4},{6,7},{7,6},{8,9},{9,8},{10,11... | collective-permute-start | bytes 405512 | tf_op jit(solution)/shard_map/ppermute | solution.py:417
  4.3 25.5 %collective-permute-start.2 = (bf16[256,2048]{1,0:T(8,128)(2,1)}, bf16[256,2048]{1,0:T(8,128)(2,1)S(1)}, u32[]{:S(2)}, u32[]{:S(2)}) collective-permute-start(bf16[256,2048]{1,0:T(8,128)(2,1)} %cot.3), channel_id=1, source_target_pairs={{0,1},{1,0},{2,3},{3,2},{4,5},{5,4},{6,7},{7,6},{8,9},{9,8},{10,11... | collective-permute-start | bytes 3145736 | tf_op jit(solution)/shard_map/ppermute | solution.py:417
  19.2 0.7 copy-start.16
  25.7 3.2 %collective-permute-start.1 = (bf16[8,272,128]{2,1,0:T(8,128)(2,1)}, bf16[8,272,128]{2,1,0:T(8,128)(2,1)S(1)}, u32[]{:S(2)}, u32[]{:S(2)}) collective-permute-start(bf16[8,272,128]{2,1,0:T(8,128)(2,1)} %get-tuple-element.34), channel_id=1, source_target_pairs={{0,2},{2,0},{4,6},{6,4},{8,10},{10,8},{12,14},{14,12},{16,18},{18,... | collective-permute-start | bytes 1671176 | tf_op jit(solution)/shard_map/ppermute | solution.py:397
  28.9 1.0 copy-start
  29.8 1.0 copy-start.3
  33.2 8.6 %collective-permute-start.3 = (bf16[4,272,128]{2,1,0:T(8,128)(2,1)}, bf16[4,272,128]{2,1,0:T(8,128)(2,1)S(1)}, u32[]{:S(2)}, u32[]{:S(2)}) collective-permute-start(bf16[4,272,128]{2,1,0:T(8,128)(2,1)} %get-tuple-element.36), channel_id=1, source_target_pairs={{0,4},{2,6},{4,0},{6,2},{8,12},{10,14},{12,8},{14,10},{16,20},{18,... | collective-permute-start | bytes 835592 | tf_op jit(solution)/shard_map/ppermute | solution.py:397
  41.7 0.7 copy-start.1
  44.3 29.3 %collective-permute-start.4 = (bf16[256,2048]{1,0:T(8,128)(2,1)}, bf16[256,2048]{1,0:T(8,128)(2,1)S(1)}, u32[]{:S(2)}, u32[]{:S(2)}) collective-permute-start(bf16[256,2048]{1,0:T(8,128)(2,1)} %get-tuple-element.38), channel_id=1, source_target_pairs={{0,1},{1,0},{2,3},{3,2},{4,5},{5,4},{6,7},{7,6},{8,9},{9,8},{10,11... | collective-permute-start | bytes 3145736 | tf_op jit(solution)/shard_map/ppermute | solution.py:417
  45.7 5.0 %collective-permute-start.5 = (bf16[1,272,128]{2,1,0:T(8,128)(2,1)}, bf16[1,272,128]{2,1,0:T(8,128)(2,1)S(1)}, u32[]{:S(2)}, u32[]{:S(2)}) collective-permute-start(bf16[1,272,128]{2,1,0:T(8,128)(2,1)} %get-tuple-element.40), channel_id=1, source_target_pairs={{0,8},{2,10},{4,12},{6,14},{8,16},{10,18},{12,20},{14,22},{16,24},... | collective-permute-start | bytes 208904 | tf_op jit(solution)/shard_map/ppermute | solution.py:397
  47.0 5.3 %collective-permute-start.6 = (bf16[1,272,128]{2,1,0:T(8,128)(2,1)}, bf16[1,272,128]{2,1,0:T(8,128)(2,1)S(1)}, u32[]{:S(2)}, u32[]{:S(2)}) collective-permute-start(bf16[1,272,128]{2,1,0:T(8,128)(2,1)} %get-tuple-element.41), channel_id=1, source_target_pairs={{0,16},{2,18},{4,20},{6,22},{8,24},{10,26},{12,28},{14,30},{16,0},... | collective-permute-start | bytes 208904 | tf_op jit(solution)/shard_map/ppermute | solution.py:397
  49.6 3.7 %collective-permute-start.7 = (bf16[1,272,128]{2,1,0:T(8,128)(2,1)}, bf16[1,272,128]{2,1,0:T(8,128)(2,1)S(1)}, u32[]{:S(2)}, u32[]{:S(2)}) collective-permute-start(bf16[1,272,128]{2,1,0:T(8,128)(2,1)} %get-tuple-element.42), channel_id=1, source_target_pairs={{0,24},{2,26},{4,28},{6,30},{8,0},{10,2},{12,4},{14,6},{16,8},{18,... | collective-permute-start | bytes 208904 | tf_op jit(solution)/shard_map/ppermute | solution.py:397
  50.7 2.6 %copy-start.5 = (bf16[1,272,128]{2,1,0:T(8,128)(2,1)}, bf16[1,272,128]{2,1,0:T(8,128)(2,1)S(1)}, u32[]{:S(2)}) copy-start(bf16[1,272,128]{2,1,0:T(8,128)(2,1)S(1)} %collective-permute-done.5.refs_1_) | copy-start | bytes 208900
  52.2 1.0 copy-start.6
  53.3 0.6 copy-start.7
  55.6 5.7 %collective-permute-start.8 = (bf16[144,128]{1,0:T(8,128)(2,1)}, bf16[144,128]{1,0:T(8,128)(2,1)S(1)}, u32[]{:S(2)}, u32[]{:S(2)}) collective-permute-start(bf16[144,128]{1,0:T(8,128)(2,1)} %get-tuple-element.43), channel_id=1, source_target_pairs={{0,32},{2,34},{4,36},{6,38},{8,40},{10,42},{12,44},{14,46},{16,48}... | collective-permute-start | bytes 110600 | tf_op jit(solution)/shard_map/ppermute | solution.py:397
  57.3 5.2 %collective-permute-start.9 = (bf16[144,128]{1,0:T(8,128)(2,1)}, bf16[144,128]{1,0:T(8,128)(2,1)S(1)}, u32[]{:S(2)}, u32[]{:S(2)}) collective-permute-start(bf16[144,128]{1,0:T(8,128)(2,1)} %get-tuple-element.44), channel_id=1, source_target_pairs={{0,64},{2,66},{4,68},{6,70},{8,72},{10,74},{12,76},{14,78},{16,80}... | collective-permute-start | bytes 110600 | tf_op jit(solution)/shard_map/ppermute | solution.py:397
  60.6 3.3 %collective-permute-start.10 = (bf16[144,128]{1,0:T(8,128)(2,1)}, bf16[144,128]{1,0:T(8,128)(2,1)S(1)}, u32[]{:S(2)}, u32[]{:S(2)}) collective-permute-start(bf16[144,128]{1,0:T(8,128)(2,1)} %get-tuple-element.45), channel_id=1, source_target_pairs={{0,96},{2,98},{4,100},{6,102},{8,104},{10,106},{12,108},{14,110},{... | collective-permute-start | bytes 110600 | tf_op jit(solution)/shard_map/ppermute | solution.py:397
  61.3 2.6 %copy-start.12 = (bf16[144,128]{1,0:T(8,128)(2,1)}, bf16[144,128]{1,0:T(8,128)(2,1)S(1)}, u32[]{:S(2)}) copy-start(bf16[144,128]{1,0:T(8,128)(2,1)S(1)} %collective-permute-done.8.refs_4_) | copy-start | bytes 110596
  62.5 1.4 copy-start.13
  63.9 0.6 copy-start.14
  66.4 4.2 %collective-permute-start.11 = (bf16[256,128]{1,0:T(8,128)(2,1)}, bf16[256,128]{1,0:T(8,128)(2,1)S(1)}, u32[]{:S(2)}, u32[]{:S(2)}) collective-permute-start(bf16[256,128]{1,0:T(8,128)(2,1)} %get-tuple-element.47), channel_id=1, source_target_pairs={{0,24},{2,26},{4,28},{6,30},{8,0},{10,2},{12,4},{14,6},{16,8},{18,... | collective-permute-start | bytes 196616 | tf_op jit(solution)/shard_map/ppermute | solution.py:397
  68.3 4.9 %collective-permute-start.12 = (bf16[256,128]{1,0:T(8,128)(2,1)}, bf16[256,128]{1,0:T(8,128)(2,1)S(1)}, u32[]{:S(2)}, u32[]{:S(2)}) collective-permute-start(bf16[256,128]{1,0:T(8,128)(2,1)} %get-tuple-element.48), channel_id=1, source_target_pairs={{0,16},{2,18},{4,20},{6,22},{8,24},{10,26},{12,28},{14,30},{16,0},... | collective-permute-start | bytes 196616 | tf_op jit(solution)/shard_map/ppermute | solution.py:397
  68.3 5.2 %collective-permute-start.13 = (bf16[256,128]{1,0:T(8,128)(2,1)}, bf16[256,128]{1,0:T(8,128)(2,1)S(1)}, u32[]{:S(2)}, u32[]{:S(2)}) collective-permute-start(bf16[256,128]{1,0:T(8,128)(2,1)} %get-tuple-element.49), channel_id=1, source_target_pairs={{0,8},{2,10},{4,12},{6,14},{8,16},{10,18},{12,20},{14,22},{16,24},... | collective-permute-start | bytes 196616 | tf_op jit(solution)/shard_map/ppermute | solution.py:397
  70.6 3.0 %copy-start.9 = (bf16[256,128]{1,0:T(8,128)(2,1)}, bf16[256,128]{1,0:T(8,128)(2,1)S(1)}, u32[]{:S(2)}) copy-start(bf16[256,128]{1,0:T(8,128)(2,1)S(1)} %collective-permute-done.11.refs_1_) | copy-start | bytes 196612
  73.3 0.6 copy-start.10
  73.6 0.6 copy-start.11
  73.6 1.0 copy-start.2
  76.8 6.9 %collective-permute-start.14 = (bf16[4,256,128]{2,1,0:T(8,128)(2,1)}, bf16[4,256,128]{2,1,0:T(8,128)(2,1)S(1)}, u32[]{:S(2)}, u32[]{:S(2)}) collective-permute-start(bf16[4,256,128]{2,1,0:T(8,128)(2,1)} %get-tuple-element.51), channel_id=1, source_target_pairs={{0,4},{2,6},{4,0},{6,2},{8,12},{10,14},{12,8},{14,10},{16,20},{18,... | collective-permute-start | bytes 786440 | tf_op jit(solution)/shard_map/ppermute | solution.py:397
  83.7 0.7 copy-start.8
  87.3 17.1 %collective-permute-start.15 = (bf16[8,128,128]{2,1,0:T(8,128)(2,1)}, bf16[8,128,128]{2,1,0:T(8,128)(2,1)S(1)}, u32[]{:S(2)}, u32[]{:S(2)}) collective-permute-start(bf16[8,128,128]{2,1,0:T(8,128)(2,1)} %get-tuple-element.53), channel_id=1, source_target_pairs={{0,2},{2,0},{4,6},{6,4},{8,10},{10,8},{12,14},{14,12},{16,18},{18,... | collective-permute-start | bytes 786440 | tf_op jit(solution)/shard_map/ppermute | solution.py:397
  95.8 5.3 %collective-permute-start.18 = (bf16[8,64,128]{2,1,0:T(8,128)(2,1)}, bf16[8,64,128]{2,1,0:T(8,128)(2,1)S(1)}, u32[]{:S(2)}, u32[]{:S(2)}) collective-permute-start(bf16[8,64,128]{2,1,0:T(8,128)(2,1)} %get-tuple-element.56), channel_id=1, source_target_pairs={{0,1},{1,0},{2,3},{3,2},{4,5},{5,4},{6,7},{7,6},{8,9},{9,8},{10,11... | collective-permute-start | bytes 393224 | tf_op jit(solution)/shard_map/ppermute | solution.py:417
  96.0 8.4 %collective-permute-start.19 = (bf16[8,64,128]{2,1,0:T(8,128)(2,1)}, bf16[8,64,128]{2,1,0:T(8,128)(2,1)S(1)}, u32[]{:S(2)}, u32[]{:S(2)}) collective-permute-start(bf16[8,64,128]{2,1,0:T(8,128)(2,1)} %get-tuple-element.57), channel_id=1, source_target_pairs={{0,3},{1,2},{2,1},{3,0},{4,7},{5,6},{6,5},{7,4},{8,11},{9,10},{10,... | collective-permute-start | bytes 393224 | tf_op jit(solution)/shard_map/ppermute | solution.py:421
  97.4 29.0 %collective-permute-start.16 = (bf16[8,64,128]{2,1,0:T(8,128)(2,1)}, bf16[8,64,128]{2,1,0:T(8,128)(2,1)S(1)}, u32[]{:S(2)}, u32[]{:S(2)}) collective-permute-start(bf16[8,64,128]{2,1,0:T(8,128)(2,1)} %get-tuple-element.54), channel_id=1, source_target_pairs={{0,1},{1,0},{2,3},{3,2},{4,5},{5,4},{6,7},{7,6},{8,9},{9,8},{10,11... | collective-permute-start | bytes 393224 | tf_op jit(solution)/shard_map/ppermute | solution.py:417
  97.7 28.7 %collective-permute-start.17 = (bf16[8,64,128]{2,1,0:T(8,128)(2,1)}, bf16[8,64,128]{2,1,0:T(8,128)(2,1)S(1)}, u32[]{:S(2)}, u32[]{:S(2)}) collective-permute-start(bf16[8,64,128]{2,1,0:T(8,128)(2,1)} %get-tuple-element.55), channel_id=1, source_target_pairs={{0,3},{1,2},{2,1},{3,0},{4,7},{5,6},{6,5},{7,4},{8,11},{9,10},{10,... | collective-permute-start | bytes 393224 | tf_op jit(solution)/shard_map/ppermute | solution.py:421
  101.1 3.3 %copy-start.19 = (bf16[8,64,128]{2,1,0:T(8,128)(2,1)}, bf16[8,64,128]{2,1,0:T(8,128)(2,1)S(1)}, u32[]{:S(2)}) copy-start(bf16[8,64,128]{2,1,0:T(8,128)(2,1)S(1)} %collective-permute-done.18.b_keep) | copy-start | bytes 393220
  104.4 0.7 copy-start.20
  104.4 0.7 copy-start.15
  126.1 13.9 %collective-permute-start.20 = (bf16[256,1024]{1,0:T(8,128)(2,1)}, bf16[256,1024]{1,0:T(8,128)(2,1)S(1)}, u32[]{:S(2)}, u32[]{:S(2)}) collective-permute-start(bf16[256,1024]{1,0:T(8,128)(2,1)} %back.2), channel_id=1, source_target_pairs={{0,1},{1,0},{2,3},{3,2},{4,5},{5,4},{6,7},{7,6},{8,9},{9,8},{10,11... | collective-permute-start | bytes 1572872 | tf_op jit(solution)/shard_map/ppermute | solution.py:417
  126.4 0.7 copy-start.17
  126.4 0.7 copy-start.18
  140.0 0.8 copy-start.4

commit v4 on v3

--- a/solution.py
+++ b/solution.py
@@ -421,7 +421,7 @@
     return lax.ppermute(x, ("ctx", "chan"), [(i, i ^ 3) for i in range(128)])
 
 
-def carries(keep1, send1, other_cot, u_r):
+def carries(keep1, send1, other_cot, u_r, grads_tables, layer_tables):
     slices = SLICES // 2
     got1 = core_swap(send1)
     keep2, send2 = whole(
@@ -433,7 +433,12 @@
     )
     got2 = x_swap(send2)
     *tops, u_r = whole(
-        x_up_kernel, [shape(1, FULL, TILE)] * 4, (keep2, got2), name="x_up", through=(u_r,)
+        x_up_kernel,
+        [shape(1, FULL, TILE)] * 4,
+        (keep2, got2),
+        name="x_up",
+        after=(grads_tables[2],),
+        through=(u_r,),
     )
     other_u = chan_swap(u_r)
     row = [tops[0]] + [y_shift(tops[k], k) for k in (1, 2, 3)]
@@ -467,6 +472,7 @@
         [shape(slices, 2 * STATE, TILE)] * 2 + [shape(slices, STATE, TILE)] * 4,
         (keep3, got3, keep1, got1),
         name="core_down",
+        after=(layer_tables[2],),
     )
     return (
         other_u,
@@ -549,23 +555,26 @@
     return jnp.concatenate(parts, axis=1)
 
 
+def grads_tables_kernel(proj, pack, *out):
+    prepare((pack, pack), proj, (False, True), (True, True), False, *out[0:3])
+    prepare_matrices(proj[0], 0, False, *out[3:6])
+    prepare_matrices(proj[1], 0, True, *out[6:9])
+
+
+def layer_tables_kernel(proj, pack, other_pack, *out):
+    prepare((pack, other_pack), proj, (True, False), (False, False), True, *out[0:3])
+    prepare_matrices(proj[0], STATE, True, *out[3:6])
+    prepare_matrices(proj[1], STATE, False, *out[6:9])
+
+
 def grads_kernel(
-    cot, other_cot, proj, pack, f_keep, f_got, b_keep, b_got, du_f, du_r, *scratch
+    cot, other_cot, f_keep, f_got, b_keep, b_got, *refs
 ):
     step = pl.program_id(0)
     core, _, _, _ = place()
-    in_scale, out_scale, rows_scale = scratch[0:3]
-    straight, turned = scratch[3:6], scratch[6:9]
-
-    @pl.when(step == 0)
-    def _():
-        tables = (pack, pack)
-        prepare(
-            tables, proj, (False, True), (True, True), False, in_scale, out_scale, rows_scale
-        )
-        prepare_matrices(proj[0], 0, False, *straight)
-        prepare_matrices(proj[1], 0, True, *turned)
-
+    in_scale, out_scale, rows_scale = refs[0:3]
+    straight, turned = refs[3:6], refs[6:9]
+    du_f, du_r = refs[9:]
     back = STEPS - 1 - step
     du_f[...] = scan_block(
         cot[...].astype(F32),
@@ -591,22 +600,13 @@
 
 
 def layer_kernel(
-    u_f, other_u, proj, pack, other_pack, f_keep, f_got, r_keep, r_got, out, *scratch
+    u_f, other_u, f_keep, f_got, r_keep, r_got, *refs
 ):
     step = pl.program_id(0)
     core, _, _, _ = place()
-    in_scale, out_scale, rows_scale = scratch[0:3]
-    straight, turned = scratch[3:6], scratch[6:9]
-
-    @pl.when(step == 0)
-    def _():
-        tables = (pack, other_pack)
-        prepare(
-            tables, proj, (True, False), (False, False), True, in_scale, out_scale, rows_scale
-        )
-        prepare_matrices(proj[0], STATE, True, *straight)
-        prepare_matrices(proj[1], STATE, False, *turned)
-
+    in_scale, out_scale, rows_scale = refs[0:3]
+    straight, turned = refs[3:6], refs[6:9]
+    out = refs[9]
     back = STEPS - 1 - step
     y_f = scan_block(
         u_f[...].astype(F32),
@@ -631,10 +631,8 @@
     out[...] = (y_f + mm(y_r, exchange_matrix(LANES))).astype(BF16)
 
 
-def scan_scratch():
-    square = pltpu.VMEM((ROWS, ROWS), BF16)
-    wide = pltpu.VMEM((ROWS, 2 * TILE), BF16)
-    return [wide, wide, pltpu.VMEM((16, 2 * TILE), BF16)] + [square] * 6
+TABLES = [shape(ROWS, 2 * TILE)] * 2 + [shape(16, 2 * TILE)] + [shape(ROWS, ROWS)] * 6
+TABLE_SPECS = [pl.BlockSpec(t.shape, lambda i: (0, 0)) for t in TABLES]
 
 
 def carry_specs(rows, mirrored):
@@ -646,39 +644,37 @@
 
 COLUMNS = pl.BlockSpec((ROWS, LANES), lambda i: (0, i))
 MIRRORED = pl.BlockSpec((ROWS, LANES), lambda i: (0, STEPS - 1 - i))
-PROJ = pl.BlockSpec((2, ROWS, TILE), lambda i: (0, 0, 0))
-PACK = pl.BlockSpec((ROWS + 8, TILE), lambda i: (0, 0))
 SCAN_COST = pl.CostEstimate(flops=10 << 30, bytes_accessed=6 << 20, transcendentals=0)
 
 
-def grads(cot, other_cot, proj, pack, f_carry, b_carry):
+def grads(cot, other_cot, tables, f_carry, b_carry):
     return pl.pallas_call(
         grads_kernel,
         grid=(STEPS,),
-        in_specs=[COLUMNS, MIRRORED, PROJ, PACK]
+        in_specs=[COLUMNS, MIRRORED]
         + carry_specs(2 * STATE, False)
-        + carry_specs(STATE, True),
+        + carry_specs(STATE, True)
+        + TABLE_SPECS,
         out_specs=[COLUMNS, COLUMNS],
         out_shape=[shape(ROWS, WIDTH), shape(ROWS, WIDTH)],
-        scratch_shapes=scan_scratch(),
         cost_estimate=SCAN_COST,
         name="grads",
-    )(cot, other_cot, proj, pack, *f_carry, *b_carry)
-
-
-def layer(u_f, other_u, proj, pack, other_pack, f_carry, r_carry):
+    )(cot, other_cot, *f_carry, *b_carry, *tables)
+
+
+def layer(u_f, other_u, tables, f_carry, r_carry):
     return pl.pallas_call(
         layer_kernel,
         grid=(STEPS,),
-        in_specs=[COLUMNS, MIRRORED, PROJ, PACK, PACK]
+        in_specs=[COLUMNS, MIRRORED]
         + carry_specs(2 * STATE, False)
-        + carry_specs(STATE, True),
+        + carry_specs(STATE, True)
+        + TABLE_SPECS,
         out_specs=COLUMNS,
         out_shape=shape(ROWS, WIDTH),
-        scratch_shapes=scan_scratch(),
         cost_estimate=SCAN_COST,
         name="layer",
-    )(u_f, other_u, proj, pack, other_pack, *f_carry, *r_carry)
+    )(u_f, other_u, *f_carry, *r_carry, *tables)
 
 
 def back_kernel(half, du_f, du_r, direct, mirrored, *rest):
@@ -746,11 +742,23 @@
         name="mirror",
         flops=8 << 30,
     )
-    other_u, f_carry, b_carry, r_carry = carries(keep, send, other_cot, u_r)
-    du_f, du_r = grads(cotangent, other_cot, state_proj, pack, f_carry, b_carry)
+    grads_tables = whole(
+        grads_tables_kernel, TABLES, (state_proj, pack), name="grads_tables", flops=1 << 30
+    )
+    layer_tables = whole(
+        layer_tables_kernel,
+        TABLES,
+        (state_proj, pack, other_pack),
+        name="layer_tables",
+        flops=1 << 30,
+    )
+    other_u, f_carry, b_carry, r_carry = carries(
+        keep, send, other_cot, u_r, grads_tables, layer_tables
+    )
+    du_f, du_r = grads(cotangent, other_cot, grads_tables, f_carry, b_carry)
     here = lax.axis_index("chan").astype(jnp.int32)[None]
     given = chan_swap(back(1 - here, du_f, du_r, in_weight))
-    layer_out = layer(u_f, other_u, state_proj, pack, other_pack, f_carry, r_carry)
+    layer_out = layer(u_f, other_u, layer_tables, f_carry, r_carry)
     input_grad = back(here, du_f, du_r, in_weight, (given,))
     return (layer_out, input_grad)
 

time: 151 us -> 150 us (level)
  waiting for transfers between devices: 28.2 us -> 23.5 us
  Pallas kernels: 77.7 us -> 82.1 us
    pallas_call x7 -> x9, Pallas kernels: 18.7 us -> 23.6 us  [whole(): pl.pallas_call(body, out_shape=list(outs) + [jax.ShapeDtypeStruct(t.shape...]
    ppermute x13, waiting for transfers between devices: 21.5 us -> 16.6 us  [ctx_permute(): return lax.ppermute(x, 'ctx', [(i, target(i)) for i in range(64)])]
  transfers between devices with their start and end apart: 21 -> 21, of which waited for: 14 -> 14; matrix products, arithmetic and copies ran while one was open for 0% -> 0% of each run, Pallas kernels for 38% -> 41%
where the time goes in v4:
time: 150 us
  Pallas kernels  82.1 us (55%)
  starting transfers between devices  35.9 us (24%)
  waiting for transfers between devices  23.5 us (16%)
  local copies, waits for them, and re-layouts  7.53 us (5%)
    ppermute x13, starting transfers between devices, ctx_permute(): return lax.ppermute(x, 'ctx', [(i, target(i)) for i in range(64)])  28.7 us
    pallas_call x9, Pallas kernels, whole(): pl.pallas_call(body, out_shape=list(outs) + [jax.ShapeDtypeStruct(t.shape...  23.6 us
    pallas_call x2, Pallas kernels, back(): pl.pallas_call(back_kernel, grid_spec=spec, out_shape=shape(ROWS, WIDTH /...  17.9 us
    ppermute x13, waiting for transfers between devices, ctx_permute(): return lax.ppermute(x, 'ctx', [(i, target(i)) for i in range(64)])  16.6 us
    pallas_call x1, Pallas kernels, project(): pl.pallas_call(project_kernel, grid=(STEPS,), in_specs=[pl.BlockSpec((ROW...  14.9 us
    pallas_call x1, Pallas kernels, layer(): pl.pallas_call(layer_kernel, grid=(STEPS,), in_specs=[COLUMNS, MIRRORED]...  12.1 us
    pallas_call x1, Pallas kernels, grads(): pl.pallas_call(grads_kernel, grid=(STEPS,), in_specs=[COLUMNS, MIRRORED]...  11.9 us
    unnamed x42, local copies, waits for them, and re-layouts  7.53 us
  transfers between devices with their start and end apart: 21, of which 14 were waited for; matrix products, arithmetic and copies ran while one was open for 0% of the time, Pallas kernels for 41%

profile of v4, /device:TPU:1, one launch (start us, length us, event | category | flops | bytes accessed | tf_op | source)
XLA Modules:
  0.0 149.7 jit_solution(2642111168413622589)
XLA Ops:
  0.6 1.7 %pack.1.refs_2_.refs_1_ = f32[264,128]{1,0:T(8,128)} custom-call(f32[2,32,256]{2,1,0:T(8,128)} %bitcast.4, f32[2,32,256]{2,1,0:T(8,128)} %bitcast.5, f32[1,32]{1,0:T(1,128)} %bitcast.6), custom_call_target="tpu_custom_call" | custom-call | tf_op jit(solution)/shard_map/pack/pallas_call | solution.py:726
  2.3 2.0 %collective-permute-start = (f32[264,128]{1,0:T(8,128)}, f32[264,128]{1,0:T(8,128)S(1)}, u32[]{:S(2)}, u32[]{:S(2)}) collective-permute-start(f32[264,128]{1,0:T(8,128)} %pack.1.refs_2_.refs_1_), channel_id=1, source_target_pairs={{0,1},{1,0},{2,3},{3,2},{4,5},{5,4},{6,7},{7,6},{8,9},{9,8},{10,11... | collective-permute-start | bytes 405512 | tf_op jit(solution)/shard_map/ppermute | solution.py:417
  4.4 14.9 %project.1 = (bf16[256,2048]{1,0:T(8,128)(2,1)}, bf16[256,2048]{1,0:T(8,128)(2,1)}, bf16[16,192,128]{2,1,0:T(8,128)(2,1)}) custom-call(bf16[256,2048]{1,0:T(8,128)(2,1)} %hidden.1, bf16[2048,2048]{1,0:T(8,128)(2,1)} %mirrored.3, bf16[2,256,128]{2,1,0:T(8,128)(2,1)} %refs_0_.5, f32[264,128]{1,0:T(8,128)} %pack.1.refs_2_.refs_1_, bf16[256,2048]{1,0:T(8,128)(2,1)} %cot.3), custom_call_target="tpu_custom_call" | custom-call | flops 4294967296 | bytes 14680064 | tf_op jit(solution)/shard_map/project/pallas_call | solution.py:122
  19.2 0.7 copy-done.16
  19.9 5.9 %mirror.1 = (bf16[8,272,128]{2,1,0:T(8,128)(2,1)}, bf16[8,272,128]{2,1,0:T(8,128)(2,1)}) custom-call(bf16[256,2048]{1,0:T(8,128)(2,1)} %cot.3, bf16[2,256,128]{2,1,0:T(8,128)(2,1)} %refs_0_.5, f32[264,128]{1,0:T(8,128)} %pack.1.refs_2_.refs_1_, f32[264,128]{1,0:T(8,128)} %copy-done.16, bf16[16,192,128]{2,1,0:T(8,128)(2,1)} %get-tuple-element.50.refs_4_), custom_call_target="tpu_custom_call" | custom-call | flops 8589934592 | bytes 3350528 | tf_op jit(solution)/shard_map/mirror/pallas_call | solution.py:217
  25.8 1.4 collective-permute-start.1
  27.1 1.8 %collective-permute-done.1.refs_1_.refs_3_ = bf16[8,272,128]{2,1,0:T(8,128)(2,1)S(1)} collective-permute-done((bf16[8,272,128]{2,1,0:T(8,128)(2,1)}, bf16[8,272,128]{2,1,0:T(8,128)(2,1)S(1)}, u32[]{:S(2)}, u32[]{:S(2)}) %collective-permute-start.1) | collective-permute-done | bytes 557088 | tf_op jit(solution)/shard_map/ppermute | solution.py:397
  28.9 0.9 collective-permute-done.2.refs_2_.other_cot
  29.8 1.0 copy-done.3
  30.8 2.3 %core_up.1 = (bf16[4,272,128]{2,1,0:T(8,128)(2,1)}, bf16[4,272,128]{2,1,0:T(8,128)(2,1)}) custom-call(bf16[8,272,128]{2,1,0:T(8,128)(2,1)} %get-tuple-element.51.refs_0_.refs_2_, bf16[8,272,128]{2,1,0:T(8,128)(2,1)} %copy-done, bf16[256,2048]{1,0:T(8,128)(2,1)} %copy-done.3), custom_call_target="tpu_custom_call" | custom-call | bytes 1671168 | tf_op jit(solution)/shard_map/core_up/pallas_call | solution.py:217
  33.1 3.2 %collective-permute-start.3 = (bf16[4,272,128]{2,1,0:T(8,128)(2,1)}, bf16[4,272,128]{2,1,0:T(8,128)(2,1)S(1)}, u32[]{:S(2)}, u32[]{:S(2)}) collective-permute-start(bf16[4,272,128]{2,1,0:T(8,128)(2,1)} %get-tuple-element.54), channel_id=1, source_target_pairs={{0,4},{2,6},{4,0},{6,2},{8,12},{10,14},{12,8},{14,10},{16,20},{18,... | collective-permute-start | bytes 835592 | tf_op jit(solution)/shard_map/ppermute | solution.py:397
  36.3 2.4 %grads_tables.1 = (bf16[256,256]{1,0:T(8,128)(2,1)}, bf16[256,256]{1,0:T(8,128)(2,1)}, bf16[16,256]{1,0:T(8,128)(2,1)}, bf16[256,256]{1,0:T(8,128)(2,1)}, bf16[2...) custom-call(bf16[2,256,128]{2,1,0:T(8,128)(2,1)} %refs_0_.5, ...), custom_call_target="tpu_custom_call" | custom-call | flops 1073741824 | bytes 1323008 | tf_op jit(solution)/shard_map/grads_tables/pallas_call | solution.py:217
  38.7 3.0 %collective-permute-done.3.refs_1_.refs_5_ = bf16[4,272,128]{2,1,0:T(8,128)(2,1)S(1)} collective-permute-done((bf16[4,272,128]{2,1,0:T(8,128)(2,1)}, bf16[4,272,128]{2,1,0:T(8,128)(2,1)S(1)}, u32[]{:S(2)}, u32[]{:S(2)}) %collective-permute-start.3) | collective-permute-done | bytes 278560 | tf_op jit(solution)/shard_map/ppermute | solution.py:397
  41.7 0.7 copy-done.1
  42.4 1.8 %x_up.1 = (bf16[1,272,128]{2,1,0:T(8,128)(2,1)}, bf16[1,272,128]{2,1,0:T(8,128)(2,1)}, bf16[1,272,128]{2,1,0:T(8,128)(2,1)}, bf16[1,272,128]{2,1,0:T(8,128)(2,1)}, bf16[256,2048]{1,0:T(8,128)(2,1)}) custom-call(bf16[4,272,128]{2,1,0:T(8,128)(2,1)} %get-tuple-element.53.refs_0_.refs_4_, ...), custom_call_target="tpu_custom_call", output_to_operand_aliasing={{4}: (3, {})} | custom-call | bytes 835584 | tf_op jit(solution)/shard_map/x_up/pallas_call | solution.py:217
  44.2 1.4 collective-permute-start.4
  45.6 1.3 collective-permute-start.5
  46.9 2.6 %collective-permute-start.6 = (bf16[1,272,128]{2,1,0:T(8,128)(2,1)}, bf16[1,272,128]{2,1,0:T(8,128)(2,1)S(1)}, u32[]{:S(2)}, u32[]{:S(2)}) collective-permute-start(bf16[1,272,128]{2,1,0:T(8,128)(2,1)} %get-tuple-element.60), channel_id=1, source_target_pairs={{0,16},{2,18},{4,20},{6,22},{8,24},{10,26},{12,28},{14,30},{16,0},... | collective-permute-start | bytes 208904 | tf_op jit(solution)/shard_map/ppermute | solution.py:397
  49.6 1.1 collective-permute-start.7
  50.6 1.6 %collective-permute-done.6.refs_2_ = bf16[1,272,128]{2,1,0:T(8,128)(2,1)S(1)} collective-permute-done((bf16[1,272,128]{2,1,0:T(8,128)(2,1)}, bf16[1,272,128]{2,1,0:T(8,128)(2,1)S(1)}, u32[]{:S(2)}, u32[]{:S(2)}) %collective-permute-start.6) | collective-permute-done | bytes 69664 | tf_op jit(solution)/shard_map/ppermute | solution.py:397
  52.2 1.0 collective-permute-done.7.refs_3_
  53.9 1.8 %y_total.1 = (bf16[144,128]{1,0:T(8,128)(2,1)}, bf16[144,128]{1,0:T(8,128)(2,1)}, bf16[144,128]{1,0:T(8,128)(2,1)}) custom-call(bf16[1,272,128]{2,1,0:T(8,128)(2,1)} %get-tuple-element.58.refs_0_, bf16[1,272,128]{2,1,0:T(8,128)(2,1)} %copy-done.5, bf16[1,272,128]{2,1,0:T(8,128)(2,1)} %copy-done.6, bf16[1,272,128]{2,1,0:T(8,128)(2,1)} %copy-done.7), custom_call_target="tpu_custom_call" | custom-call | bytes 389120 | tf_op jit(solution)/shard_map/y_total/pallas_call | solution.py:217
  55.6 1.6 %collective-permute-start.8 = (bf16[144,128]{1,0:T(8,128)(2,1)}, bf16[144,128]{1,0:T(8,128)(2,1)S(1)}, u32[]{:S(2)}, u32[]{:S(2)}) collective-permute-start(bf16[144,128]{1,0:T(8,128)(2,1)} %get-tuple-element.62), channel_id=1, source_target_pairs={{0,32},{2,34},{4,36},{6,38},{8,40},{10,42},{12,44},{14,46},{16,48}... | collective-permute-start | bytes 110600 | tf_op jit(solution)/shard_map/ppermute | solution.py:397
  57.3 3.3 %collective-permute-start.9 = (bf16[144,128]{1,0:T(8,128)(2,1)}, bf16[144,128]{1,0:T(8,128)(2,1)S(1)}, u32[]{:S(2)}, u32[]{:S(2)}) collective-permute-start(bf16[144,128]{1,0:T(8,128)(2,1)} %get-tuple-element.63), channel_id=1, source_target_pairs={{0,64},{2,66},{4,68},{6,70},{8,72},{10,74},{12,76},{14,78},{16,80}... | collective-permute-start | bytes 110600 | tf_op jit(solution)/shard_map/ppermute | solution.py:397
  60.6 0.7 collective-permute-start.10
  61.3 1.2 collective-permute-done.9.refs_5_
  62.5 1.4 collective-permute-done.10.refs_6_
  64.5 1.9 %z_carry.1 = (bf16[256,128]{1,0:T(8,128)(2,1)}, bf16[256,128]{1,0:T(8,128)(2,1)}, bf16[256,128]{1,0:T(8,128)(2,1)}, bf16[256,128]{1,0:T(8,128)(2,1)}) custom-call(bf16[1,272,128]{2,1,0:T(8,128)(2,1)} %get-tuple-element.58.refs_0_, bf16[1,272,128]{2,1,0:T(8,128)(2,1)} %copy-done.5, bf16[1,272,128]{2,1,0:T(8,128)(2,1)} %copy-done.6, ...), custom_call_target="tpu_custom_call" | custom-call | bytes 651264 | tf_op jit(solution)/shard_map/z_carry/pallas_call | solution.py:217
  66.4 2.0 %collective-permute-start.11 = (bf16[256,128]{1,0:T(8,128)(2,1)}, bf16[256,128]{1,0:T(8,128)(2,1)S(1)}, u32[]{:S(2)}, u32[]{:S(2)}) collective-permute-start(bf16[256,128]{1,0:T(8,128)(2,1)} %get-tuple-element.66), channel_id=1, source_target_pairs={{0,24},{2,26},{4,28},{6,30},{8,0},{10,2},{12,4},{14,6},{16,8},{18,... | collective-permute-start | bytes 196616 | tf_op jit(solution)/shard_map/ppermute | solution.py:397
  69.0 1.6 %collective-permute-done.11.refs_1_ = bf16[256,128]{1,0:T(8,128)(2,1)S(1)} collective-permute-done((bf16[256,128]{1,0:T(8,128)(2,1)}, bf16[256,128]{1,0:T(8,128)(2,1)S(1)}, u32[]{:S(2)}, u32[]{:S(2)}) %collective-permute-start.11) | collective-permute-done | bytes 65568 | tf_op jit(solution)/shard_map/ppermute | solution.py:397
  70.6 2.7 %collective-permute-done.12.refs_2_ = bf16[256,128]{1,0:T(8,128)(2,1)S(1)} collective-permute-done((bf16[256,128]{1,0:T(8,128)(2,1)}, bf16[256,128]{1,0:T(8,128)(2,1)S(1)}, u32[]{:S(2)}, u32[]{:S(2)}) %collective-permute-start.12) | collective-permute-done | bytes 65568 | tf_op jit(solution)/shard_map/ppermute | solution.py:397
  74.6 2.2 %x_down.1 = (bf16[4,256,128]{2,1,0:T(8,128)(2,1)}, bf16[4,256,128]{2,1,0:T(8,128)(2,1)}) custom-call(bf16[256,128]{1,0:T(8,128)(2,1)} %get-tuple-element.65.refs_0_, bf16[256,128]{1,0:T(8,128)(2,1)} %copy-done.9, bf16[256,128]{1,0:T(8,128)(2,1)} %copy-done.10, bf16[256,128]{1,0:T(8,128)(2,1)} %copy-done.11, ...), custom_call_target="tpu_custom_call" | custom-call | bytes 1343488 | tf_op jit(solution)/shard_map/x_down/pallas_call | solution.py:217
  76.8 2.4 %collective-permute-start.14 = (bf16[4,256,128]{2,1,0:T(8,128)(2,1)}, bf16[4,256,128]{2,1,0:T(8,128)(2,1)S(1)}, u32[]{:S(2)}, u32[]{:S(2)}) collective-permute-start(bf16[4,256,128]{2,1,0:T(8,128)(2,1)} %get-tuple-element.70), channel_id=1, source_target_pairs={{0,4},{2,6},{4,0},{6,2},{8,12},{10,14},{12,8},{14,10},{16,20},{18,... | collective-permute-start | bytes 786440 | tf_op jit(solution)/shard_map/ppermute | solution.py:397
  79.2 2.5 %layer_tables.1 = (bf16[256,256]{1,0:T(8,128)(2,1)}, bf16[256,256]{1,0:T(8,128)(2,1)}, bf16[16,256]{1,0:T(8,128)(2,1)}, bf16[256,256]{1,0:T(8,128)(2,1)}, bf16[2...) custom-call(bf16[2,256,128]{2,1,0:T(8,128)(2,1)} %refs_0_.5, ...), custom_call_target="tpu_custom_call" | custom-call | flops 1073741824 | bytes 1458176 | tf_op jit(solution)/shard_map/layer_tables/pallas_call | solution.py:217
  81.7 2.0 %collective-permute-done.14.refs_1_ = bf16[4,256,128]{2,1,0:T(8,128)(2,1)S(1)} collective-permute-done((bf16[4,256,128]{2,1,0:T(8,128)(2,1)}, bf16[4,256,128]{2,1,0:T(8,128)(2,1)S(1)}, u32[]{:S(2)}, u32[]{:S(2)}) %collective-permute-start.14) | collective-permute-done | bytes 262176 | tf_op jit(solution)/shard_map/ppermute | solution.py:397
  83.8 0.7 copy-done.8
  84.5 2.8 %core_down.1 = (bf16[8,128,128]{2,1,0:T(8,128)(2,1)}, bf16[8,128,128]{2,1,0:T(8,128)(2,1)}, bf16[8,64,128]{2,1,0:T(8,128)(2,1)}, bf16[8,64,128]{2,1,0:T(8,128)(2...) custom-call(bf16[4,256,128]{2,1,0:T(8,128)(2,1)} %get-tuple-element.69.refs_0_, ...), custom_call_target="tpu_custom_call" | custom-call | bytes 2686976 | tf_op jit(solution)/shard_map/core_down/pallas_call | solution.py:217
  87.3 8.5 %collective-permute-start.15 = (bf16[8,128,128]{2,1,0:T(8,128)(2,1)}, bf16[8,128,128]{2,1,0:T(8,128)(2,1)S(1)}, u32[]{:S(2)}, u32[]{:S(2)}) collective-permute-start(bf16[8,128,128]{2,1,0:T(8,128)(2,1)} %get-tuple-element.73), channel_id=1, source_target_pairs={{0,2},{2,0},{4,6},{6,4},{8,10},{10,8},{12,14},{14,12},{16,18},{18,... | collective-permute-start | bytes 786440 | tf_op jit(solution)/shard_map/ppermute | solution.py:397
  96.0 1.4 collective-permute-start.19
  97.7 1.6 %collective-permute-start.17 = (bf16[8,64,128]{2,1,0:T(8,128)(2,1)}, bf16[8,64,128]{2,1,0:T(8,128)(2,1)S(1)}, u32[]{:S(2)}, u32[]{:S(2)}) collective-permute-start(bf16[8,64,128]{2,1,0:T(8,128)(2,1)} %get-tuple-element.75), channel_id=1, source_target_pairs={{0,3},{1,2},{2,1},{3,0},{4,7},{5,6},{6,5},{7,4},{8,11},{9,10},{10,... | collective-permute-start | bytes 393224 | tf_op jit(solution)/shard_map/ppermute | solution.py:421
  99.3 1.8 %collective-permute-done.18.b_keep = bf16[8,64,128]{2,1,0:T(8,128)(2,1)S(1)} collective-permute-done((bf16[8,64,128]{2,1,0:T(8,128)(2,1)}, bf16[8,64,128]{2,1,0:T(8,128)(2,1)S(1)}, u32[]{:S(2)}, u32[]{:S(2)}) %collective-permute-start.18) | collective-permute-done | bytes 131104 | tf_op jit(solution)/shard_map/ppermute | solution.py:417
  101.1 3.3 %collective-permute-done.19.b_got = bf16[8,64,128]{2,1,0:T(8,128)(2,1)S(1)} collective-permute-done((bf16[8,64,128]{2,1,0:T(8,128)(2,1)}, bf16[8,64,128]{2,1,0:T(8,128)(2,1)S(1)}, u32[]{:S(2)}, u32[]{:S(2)}) %collective-permute-start.19) | collective-permute-done | bytes 131104 | tf_op jit(solution)/shard_map/ppermute | solution.py:421
  105.2 11.9 %grads.1 = (bf16[256,2048]{1,0:T(8,128)(2,1)}, bf16[256,2048]{1,0:T(8,128)(2,1)}) custom-call(bf16[256,2048]{1,0:T(8,128)(2,1)} %cot.3, bf16[256,2048]{1,0:T(8,128)(2,1)} %copy-done.3, bf16[8,128,128]{2,1,0:T(8,128)(2,1)} %get-tuple-element.72.f_keep, bf16[8,128,128]{2,1,0:T(8,128)(2,1)} %copy-done.15, bf16[8,64,128]{2,1,0:T(8,128)(2,1)} %copy-done.19, ...), custom_call_target="tpu_custom_call" | custom-call | flops 10737418240 | bytes 6291456 | tf_op jit(solution)/shard_map/grads/pallas_call | solution.py:651
  117.1 8.8 %back.2 = bf16[256,1024]{1,0:T(8,128)(2,1)} custom-call(s32[1]{0:T(128)S(6)} %sub.3.half, bf16[256,2048]{1,0:T(8,128)(2,1)} %get-tuple-element.94.du_f, bf16[256,2048]{1,0:T(8,128)(2,1)} %get-tuple-element.95.du_r, bf16[2048,2048]{1,0:T(8,128)(2,1)} %mirrored.3, bf16[2048,2048]{1,0:T(8,128)(2,1)} %mirrored.3), custom_call_target="tpu_custom_call" | custom-call | flops 2147483648 | bytes 11534336 | tf_op jit(solution)/shard_map/back/pallas_call | solution.py:707
  126.9 12.1 %layer.1 = bf16[256,2048]{1,0:T(8,128)(2,1)} custom-call(bf16[256,2048]{1,0:T(8,128)(2,1)} %get-tuple-element.49.u_f, bf16[256,2048]{1,0:T(8,128)(2,1)} %copy-done.2, bf16[8,128,128]{2,1,0:T(8,128)(2,1)} %get-tuple-element.72.f_keep, bf16[8,128,128]{2,1,0:T(8,128)(2,1)} %copy-done.15, bf16[8,64,128]{2,1,0:T(8,128)(2,1)} %copy-done.17, ...), custom_call_target="tpu_custom_call" | custom-call | flops 10737418240 | bytes 6291456 | tf_op jit(solution)/shard_map/layer/pallas_call | solution.py:666
  138.9 0.9 collective-permute-done.20.rest_0_
  139.8 0.8 copy-done.4
  140.6 9.1 %back.3 = bf16[256,1024]{1,0:T(8,128)(2,1)} custom-call(s32[1]{0:T(128)} %bitcast.3.half, bf16[256,2048]{1,0:T(8,128)(2,1)} %get-tuple-element.94.du_f, bf16[256,2048]{1,0:T(8,128)(2,1)} %get-tuple-element.95.du_r, bf16[2048,2048]{1,0:T(8,128)(2,1)} %mirrored.3, bf16[2048,2048]{1,0:T(8,128)(2,1)} %mirrored.3, bf16[256,1024]{1,0:T(8,128)(2,1)} %copy-done.4), custom_call_target="tpu_custom_call" | custom-call | flops 2147483648 | bytes 11534336 | tf_op jit(solution)/shard_map/back/pallas_call | solution.py:707
  (51 shorter events, 5.4 us)
Async XLA Ops:
  2.3 16.9 %collective-permute-start = (f32[264,128]{1,0:T(8,128)}, f32[264,128]{1,0:T(8,128)S(1)}, u32[]{:S(2)}, u32[]{:S(2)}) collective-permute-start(f32[264,128]{1,0:T(8,128)} %pack.1.refs_2_.refs_1_), channel_id=1, source_target_pairs={{0,1},{1,0},{2,3},{3,2},{4,5},{5,4},{6,7},{7,6},{8,9},{9,8},{10,11... | collective-permute-start | bytes 405512 | tf_op jit(solution)/shard_map/ppermute | solution.py:417
  4.3 25.5 %collective-permute-start.2 = (bf16[256,2048]{1,0:T(8,128)(2,1)}, bf16[256,2048]{1,0:T(8,128)(2,1)S(1)}, u32[]{:S(2)}, u32[]{:S(2)}) collective-permute-start(bf16[256,2048]{1,0:T(8,128)(2,1)} %cot.3), channel_id=1, source_target_pairs={{0,1},{1,0},{2,3},{3,2},{4,5},{5,4},{6,7},{7,6},{8,9},{9,8},{10,11... | collective-permute-start | bytes 3145736 | tf_op jit(solution)/shard_map/ppermute | solution.py:417
  19.2 0.7 copy-start.16
  25.8 3.1 %collective-permute-start.1 = (bf16[8,272,128]{2,1,0:T(8,128)(2,1)}, bf16[8,272,128]{2,1,0:T(8,128)(2,1)S(1)}, u32[]{:S(2)}, u32[]{:S(2)}) collective-permute-start(bf16[8,272,128]{2,1,0:T(8,128)(2,1)} %get-tuple-element.52), channel_id=1, source_target_pairs={{0,2},{2,0},{4,6},{6,4},{8,10},{10,8},{12,14},{14,12},{16,18},{18,... | collective-permute-start | bytes 1671176 | tf_op jit(solution)/shard_map/ppermute | solution.py:397
  28.9 0.9 copy-start
  29.8 1.0 copy-start.3
  33.1 8.6 %collective-permute-start.3 = (bf16[4,272,128]{2,1,0:T(8,128)(2,1)}, bf16[4,272,128]{2,1,0:T(8,128)(2,1)S(1)}, u32[]{:S(2)}, u32[]{:S(2)}) collective-permute-start(bf16[4,272,128]{2,1,0:T(8,128)(2,1)} %get-tuple-element.54), channel_id=1, source_target_pairs={{0,4},{2,6},{4,0},{6,2},{8,12},{10,14},{12,8},{14,10},{16,20},{18,... | collective-permute-start | bytes 835592 | tf_op jit(solution)/shard_map/ppermute | solution.py:397
  41.7 0.7 copy-start.1
  44.2 29.4 %collective-permute-start.4 = (bf16[256,2048]{1,0:T(8,128)(2,1)}, bf16[256,2048]{1,0:T(8,128)(2,1)S(1)}, u32[]{:S(2)}, u32[]{:S(2)}) collective-permute-start(bf16[256,2048]{1,0:T(8,128)(2,1)} %get-tuple-element.57), channel_id=1, source_target_pairs={{0,1},{1,0},{2,3},{3,2},{4,5},{5,4},{6,7},{7,6},{8,9},{9,8},{10,11... | collective-permute-start | bytes 3145736 | tf_op jit(solution)/shard_map/ppermute | solution.py:417
  45.6 5.0 %collective-permute-start.5 = (bf16[1,272,128]{2,1,0:T(8,128)(2,1)}, bf16[1,272,128]{2,1,0:T(8,128)(2,1)S(1)}, u32[]{:S(2)}, u32[]{:S(2)}) collective-permute-start(bf16[1,272,128]{2,1,0:T(8,128)(2,1)} %get-tuple-element.59), channel_id=1, source_target_pairs={{0,8},{2,10},{4,12},{6,14},{8,16},{10,18},{12,20},{14,22},{16,24},... | collective-permute-start | bytes 208904 | tf_op jit(solution)/shard_map/ppermute | solution.py:397
  46.9 5.3 %collective-permute-start.6 = (bf16[1,272,128]{2,1,0:T(8,128)(2,1)}, bf16[1,272,128]{2,1,0:T(8,128)(2,1)S(1)}, u32[]{:S(2)}, u32[]{:S(2)}) collective-permute-start(bf16[1,272,128]{2,1,0:T(8,128)(2,1)} %get-tuple-element.60), channel_id=1, source_target_pairs={{0,16},{2,18},{4,20},{6,22},{8,24},{10,26},{12,28},{14,30},{16,0},... | collective-permute-start | bytes 208904 | tf_op jit(solution)/shard_map/ppermute | solution.py:397
  49.6 3.7 %collective-permute-start.7 = (bf16[1,272,128]{2,1,0:T(8,128)(2,1)}, bf16[1,272,128]{2,1,0:T(8,128)(2,1)S(1)}, u32[]{:S(2)}, u32[]{:S(2)}) collective-permute-start(bf16[1,272,128]{2,1,0:T(8,128)(2,1)} %get-tuple-element.61), channel_id=1, source_target_pairs={{0,24},{2,26},{4,28},{6,30},{8,0},{10,2},{12,4},{14,6},{16,8},{18,... | collective-permute-start | bytes 208904 | tf_op jit(solution)/shard_map/ppermute | solution.py:397
  50.6 2.6 %copy-start.5 = (bf16[1,272,128]{2,1,0:T(8,128)(2,1)}, bf16[1,272,128]{2,1,0:T(8,128)(2,1)S(1)}, u32[]{:S(2)}) copy-start(bf16[1,272,128]{2,1,0:T(8,128)(2,1)S(1)} %collective-permute-done.5.refs_1_) | copy-start | bytes 208900
  52.2 1.0 copy-start.6
  53.2 0.6 copy-start.7
  55.6 5.7 %collective-permute-start.8 = (bf16[144,128]{1,0:T(8,128)(2,1)}, bf16[144,128]{1,0:T(8,128)(2,1)S(1)}, u32[]{:S(2)}, u32[]{:S(2)}) collective-permute-start(bf16[144,128]{1,0:T(8,128)(2,1)} %get-tuple-element.62), channel_id=1, source_target_pairs={{0,32},{2,34},{4,36},{6,38},{8,40},{10,42},{12,44},{14,46},{16,48}... | collective-permute-start | bytes 110600 | tf_op jit(solution)/shard_map/ppermute | solution.py:397
  57.3 5.2 %collective-permute-start.9 = (bf16[144,128]{1,0:T(8,128)(2,1)}, bf16[144,128]{1,0:T(8,128)(2,1)S(1)}, u32[]{:S(2)}, u32[]{:S(2)}) collective-permute-start(bf16[144,128]{1,0:T(8,128)(2,1)} %get-tuple-element.63), channel_id=1, source_target_pairs={{0,64},{2,66},{4,68},{6,70},{8,72},{10,74},{12,76},{14,78},{16,80}... | collective-permute-start | bytes 110600 | tf_op jit(solution)/shard_map/ppermute | solution.py:397
  60.6 3.3 %collective-permute-start.10 = (bf16[144,128]{1,0:T(8,128)(2,1)}, bf16[144,128]{1,0:T(8,128)(2,1)S(1)}, u32[]{:S(2)}, u32[]{:S(2)}) collective-permute-start(bf16[144,128]{1,0:T(8,128)(2,1)} %get-tuple-element.64), channel_id=1, source_target_pairs={{0,96},{2,98},{4,100},{6,102},{8,104},{10,106},{12,108},{14,110},{... | collective-permute-start | bytes 110600 | tf_op jit(solution)/shard_map/ppermute | solution.py:397
  61.3 2.6 %copy-start.12 = (bf16[144,128]{1,0:T(8,128)(2,1)}, bf16[144,128]{1,0:T(8,128)(2,1)S(1)}, u32[]{:S(2)}) copy-start(bf16[144,128]{1,0:T(8,128)(2,1)S(1)} %collective-permute-done.8.refs_4_) | copy-start | bytes 110596
  62.5 1.4 copy-start.13
  63.9 0.6 copy-start.14
  66.4 4.2 %collective-permute-start.11 = (bf16[256,128]{1,0:T(8,128)(2,1)}, bf16[256,128]{1,0:T(8,128)(2,1)S(1)}, u32[]{:S(2)}, u32[]{:S(2)}) collective-permute-start(bf16[256,128]{1,0:T(8,128)(2,1)} %get-tuple-element.66), channel_id=1, source_target_pairs={{0,24},{2,26},{4,28},{6,30},{8,0},{10,2},{12,4},{14,6},{16,8},{18,... | collective-permute-start | bytes 196616 | tf_op jit(solution)/shard_map/ppermute | solution.py:397
  68.3 4.9 %collective-permute-start.12 = (bf16[256,128]{1,0:T(8,128)(2,1)}, bf16[256,128]{1,0:T(8,128)(2,1)S(1)}, u32[]{:S(2)}, u32[]{:S(2)}) collective-permute-start(bf16[256,128]{1,0:T(8,128)(2,1)} %get-tuple-element.67), channel_id=1, source_target_pairs={{0,16},{2,18},{4,20},{6,22},{8,24},{10,26},{12,28},{14,30},{16,0},... | collective-permute-start | bytes 196616 | tf_op jit(solution)/shard_map/ppermute | solution.py:397
  68.4 5.2 %collective-permute-start.13 = (bf16[256,128]{1,0:T(8,128)(2,1)}, bf16[256,128]{1,0:T(8,128)(2,1)S(1)}, u32[]{:S(2)}, u32[]{:S(2)}) collective-permute-start(bf16[256,128]{1,0:T(8,128)(2,1)} %get-tuple-element.68), channel_id=1, source_target_pairs={{0,8},{2,10},{4,12},{6,14},{8,16},{10,18},{12,20},{14,22},{16,24},... | collective-permute-start | bytes 196616 | tf_op jit(solution)/shard_map/ppermute | solution.py:397
  70.6 3.0 %copy-start.9 = (bf16[256,128]{1,0:T(8,128)(2,1)}, bf16[256,128]{1,0:T(8,128)(2,1)S(1)}, u32[]{:S(2)}) copy-start(bf16[256,128]{1,0:T(8,128)(2,1)S(1)} %collective-permute-done.11.refs_1_) | copy-start | bytes 196612
  73.3 0.6 copy-start.10
  73.6 0.6 copy-start.11
  73.6 1.0 copy-start.2
  76.8 6.9 %collective-permute-start.14 = (bf16[4,256,128]{2,1,0:T(8,128)(2,1)}, bf16[4,256,128]{2,1,0:T(8,128)(2,1)S(1)}, u32[]{:S(2)}, u32[]{:S(2)}) collective-permute-start(bf16[4,256,128]{2,1,0:T(8,128)(2,1)} %get-tuple-element.70), channel_id=1, source_target_pairs={{0,4},{2,6},{4,0},{6,2},{8,12},{10,14},{12,8},{14,10},{16,20},{18,... | collective-permute-start | bytes 786440 | tf_op jit(solution)/shard_map/ppermute | solution.py:397
  83.8 0.7 copy-start.8
  87.3 17.1 %collective-permute-start.15 = (bf16[8,128,128]{2,1,0:T(8,128)(2,1)}, bf16[8,128,128]{2,1,0:T(8,128)(2,1)S(1)}, u32[]{:S(2)}, u32[]{:S(2)}) collective-permute-start(bf16[8,128,128]{2,1,0:T(8,128)(2,1)} %get-tuple-element.73), channel_id=1, source_target_pairs={{0,2},{2,0},{4,6},{6,4},{8,10},{10,8},{12,14},{14,12},{16,18},{18,... | collective-permute-start | bytes 786440 | tf_op jit(solution)/shard_map/ppermute | solution.py:397
  95.8 5.3 %collective-permute-start.18 = (bf16[8,64,128]{2,1,0:T(8,128)(2,1)}, bf16[8,64,128]{2,1,0:T(8,128)(2,1)S(1)}, u32[]{:S(2)}, u32[]{:S(2)}) collective-permute-start(bf16[8,64,128]{2,1,0:T(8,128)(2,1)} %get-tuple-element.84), channel_id=1, source_target_pairs={{0,1},{1,0},{2,3},{3,2},{4,5},{5,4},{6,7},{7,6},{8,9},{9,8},{10,11... | collective-permute-start | bytes 393224 | tf_op jit(solution)/shard_map/ppermute | solution.py:417
  96.0 8.4 %collective-permute-start.19 = (bf16[8,64,128]{2,1,0:T(8,128)(2,1)}, bf16[8,64,128]{2,1,0:T(8,128)(2,1)S(1)}, u32[]{:S(2)}, u32[]{:S(2)}) collective-permute-start(bf16[8,64,128]{2,1,0:T(8,128)(2,1)} %get-tuple-element.85), channel_id=1, source_target_pairs={{0,3},{1,2},{2,1},{3,0},{4,7},{5,6},{6,5},{7,4},{8,11},{9,10},{10,... | collective-permute-start | bytes 393224 | tf_op jit(solution)/shard_map/ppermute | solution.py:421
  97.4 28.7 %collective-permute-start.16 = (bf16[8,64,128]{2,1,0:T(8,128)(2,1)}, bf16[8,64,128]{2,1,0:T(8,128)(2,1)S(1)}, u32[]{:S(2)}, u32[]{:S(2)}) collective-permute-start(bf16[8,64,128]{2,1,0:T(8,128)(2,1)} %get-tuple-element.74), channel_id=1, source_target_pairs={{0,1},{1,0},{2,3},{3,2},{4,5},{5,4},{6,7},{7,6},{8,9},{9,8},{10,11... | collective-permute-start | bytes 393224 | tf_op jit(solution)/shard_map/ppermute | solution.py:417
  97.7 28.5 %collective-permute-start.17 = (bf16[8,64,128]{2,1,0:T(8,128)(2,1)}, bf16[8,64,128]{2,1,0:T(8,128)(2,1)S(1)}, u32[]{:S(2)}, u32[]{:S(2)}) collective-permute-start(bf16[8,64,128]{2,1,0:T(8,128)(2,1)} %get-tuple-element.75), channel_id=1, source_target_pairs={{0,3},{1,2},{2,1},{3,0},{4,7},{5,6},{6,5},{7,4},{8,11},{9,10},{10,... | collective-permute-start | bytes 393224 | tf_op jit(solution)/shard_map/ppermute | solution.py:421
  101.1 3.3 %copy-start.19 = (bf16[8,64,128]{2,1,0:T(8,128)(2,1)}, bf16[8,64,128]{2,1,0:T(8,128)(2,1)S(1)}, u32[]{:S(2)}) copy-start(bf16[8,64,128]{2,1,0:T(8,128)(2,1)S(1)} %collective-permute-done.18.b_keep) | copy-start | bytes 393220
  104.4 0.7 copy-start.20
  104.4 0.7 copy-start.15
  125.9 13.9 %collective-permute-start.20 = (bf16[256,1024]{1,0:T(8,128)(2,1)}, bf16[256,1024]{1,0:T(8,128)(2,1)S(1)}, u32[]{:S(2)}, u32[]{:S(2)}) collective-permute-start(bf16[256,1024]{1,0:T(8,128)(2,1)} %back.2), channel_id=1, source_target_pairs={{0,1},{1,0},{2,3},{3,2},{4,5},{5,4},{6,7},{7,6},{8,9},{9,8},{10,11... | collective-permute-start | bytes 1572872 | tf_op jit(solution)/shard_map/ppermute | solution.py:417
  126.2 0.7 copy-start.17
  126.2 0.7 copy-start.18
  139.8 0.8 copy-start.4
